TPU v7x, 32 devices: a whole 2x2x4 slice. The times are simulated.
32 devices in a mesh: dp: 32 (over z, y, x, core).
Axes of the slice: x: 2, y: 2, z: 4, core: 2. Of those that a mesh axis runs over, the one named last changes fastest.
Arguments:
- hidden_in: bfloat16 [4096, 640], P('dp'), may hold values from -6 to 6
- cotangent: bfloat16 [4096, 640], P('dp'), may hold values from -6 to 6
- params: float32 [5573632], P('dp'), may hold values from -4 to 4
- moment_one: float32 [5573632], P('dp'), may hold values from -6 to 6
- moment_two: float32 [5573632], P('dp'), may hold values from 0.02 to 0.5
- seq_lengths: int32 [64], replicated, may hold values from 0 to 128, as said below
- seq_owner: int32 [64], replicated, may hold values from 0 to 31, as said below
Outputs:
- block_out: bfloat16 [4096, 640], P('dp')
- grad_in: float32 [4096, 640], P('dp')
- grad_flat: float32 [5573632], P('dp')
- params_new: float32 [5573632], P('dp')
- moment_one_new: float32 [5573632], P('dp')
- moment_two_new: float32 [5573632], P('dp')
Inputs may be any that keep to these rules, and one draw needn't show every extreme that they name: `seq_lengths`: sequences 2j and 2j + 1 go to the same device; on each device their lengths sum to 1 to 128, and sequence 2j has a token or more; one sequence has exactly 128 tokens and its partner has none; other sequences 2j + 1 may have none too. `seq_owner`: each device holds exactly the two sequences 2j and 2j + 1 for one j.
All inputs are finite; a program needn't handle non-finite values.
Results may differ from a plain program's by a relative error of at most 0.012.
The roundings to bfloat16 on the way count: a program that leaves them out, or rounds other values in their place, can miss the bound.
Values may be sent and summed in bfloat16 or wider, within the bound.
No kernel may reach another device: no remote copies, remote signals or barrier semaphores. Data moves between devices by JAX's collectives and lax.ppermute only.
A program may use at most 128 MiB of HBM per device.

v0:
```python
import jax
import jax.numpy as jnp
from jax import lax
from jax.sharding import PartitionSpec as P

D = 640
FF = 2048
HD = 256
HQ = 1024
CAP = 128
WINDOW = 64
STEP = 3
G1LEN = 1638400
G2LEN = 3932160


def rms_scale(values, gain_vec):
    return (
        values
        * lax.rsqrt(jnp.mean(values * values, axis=-1, keepdims=True) + 1e-06)
        * (1.0 + gain_vec)
    )


def rotate(values, cos_tab, sin_tab):
    half_dim = values.shape[-1] // 2
    lower_half = values[..., :half_dim]
    upper_half = values[..., half_dim:]
    return jnp.concatenate(
        [lower_half * cos_tab - upper_half * sin_tab, upper_half * cos_tab + lower_half * sin_tab],
        axis=-1,
    )


def query_key(query_raw, key_raw, gain_query, gain_key, cos_tab, sin_tab):
    per_head = query_raw.reshape(query_raw.shape[0], -1, HD).transpose(1, 0, 2)
    rot_query = rotate(rms_scale(per_head, gain_query), cos_tab, sin_tab) * HD ** (-0.5)
    rot_key = rotate(rms_scale(key_raw, gain_key), cos_tab, sin_tab)
    return (rot_query, rot_key)


def gated_gelu(gate_proj, up_proj):
    return jax.nn.gelu(gate_proj, approximate=True) * up_proj


def outer_sum(left_side, right_side):
    return lax.dot_general(
        left_side, right_side, (((0,), (0,)), ((), ())), preferred_element_type=jnp.float32
    )


def times_transposed(rows_in, matrix):
    return lax.dot_general(
        rows_in, matrix, (((1,), (1,)), ((), ())), preferred_element_type=jnp.float32
    )


def slot_setup(seq_lengths, seq_owner, device):
    mine_mask = seq_owner == device
    own_lengths = jnp.where(mine_mask, seq_lengths, 0)
    seq_ends = jnp.cumsum(own_lengths, dtype=jnp.int32)
    seq_begins = seq_ends - own_lengths
    slot_index = jnp.arange(CAP, dtype=jnp.int32)
    column = slot_index[:, None]
    inside_mask = (
        mine_mask[None, :] & (seq_begins[None, :] <= column) & (column < seq_ends[None, :])
    )
    live_mask = jnp.any(inside_mask, axis=1)
    seq_label = jnp.sum(
        (mine_mask[None, :] & (seq_ends[None, :] <= column)).astype(jnp.int32),
        axis=1,
        dtype=jnp.int32,
    )
    position = jnp.sum(
        jnp.where(inside_mask, column - seq_begins[None, :], 0), axis=1, dtype=jnp.int32
    )
    row_slot = slot_index[:, None]
    col_slot = slot_index[None, :]
    allowed = live_mask[:, None] & live_mask[None, :] & (
        seq_label[:, None] == seq_label[None, :]
    ) & (col_slot <= row_slot) & (row_slot - col_slot < WINDOW) | (row_slot == col_slot)
    half_dim = HD // 2
    frequency = 10000.0 ** (-2.0 * jnp.arange(half_dim, dtype=jnp.float32) / HD)
    angles = position.astype(jnp.float32)[:, None] * frequency[None, :]
    return (live_mask.astype(jnp.float32), allowed, jnp.cos(angles), jnp.sin(angles))


def attend(rot_query, rot_key, value_vec, allowed):
    num_heads = rot_query.shape[0]
    num_slots = rot_key.shape[0]
    flat_query = rot_query.reshape(num_heads * num_slots, HD)
    scores = lax.dot_general(
        flat_query, rot_key, (((1,), (1,)), ((), ())), preferred_element_type=jnp.float32
    )
    scores = jnp.where(allowed[None], scores.reshape(num_heads, num_slots, num_slots), -1e30)
    row_max = jnp.max(scores, axis=-1, keepdims=True)
    raised = jnp.exp(scores - row_max)
    summed = jnp.sum(raised, axis=-1, keepdims=True)
    log_total = row_max + jnp.log(summed)
    attn_prob = (raised / summed).astype(jnp.bfloat16)
    context = jnp.dot(
        attn_prob.reshape(num_heads * num_slots, num_slots),
        value_vec,
        preferred_element_type=jnp.float32,
    )
    context = (
        context.reshape(num_heads, num_slots, HD)
        .transpose(1, 0, 2)
        .reshape(num_slots, num_heads * HD)
    )
    return (context.astype(jnp.bfloat16), log_total)


def attend_back(rot_query, rot_key, value_vec, allowed, log_total, context, delta_context):
    num_heads = rot_query.shape[0]
    num_slots = rot_key.shape[0]
    head_delta = delta_context.reshape(num_slots, num_heads, HD).transpose(1, 0, 2).reshape(-1, HD)
    head_context = context.reshape(num_slots, num_heads, HD).transpose(1, 0, 2).reshape(-1, HD)
    row_dot = jnp.sum(
        head_delta.astype(jnp.float32) * head_context.astype(jnp.float32), axis=-1, keepdims=True
    )
    flat_query = rot_query.reshape(-1, HD)
    scores = lax.dot_general(
        flat_query, rot_key, (((1,), (1,)), ((), ())), preferred_element_type=jnp.float32
    )
    scores = jnp.where(allowed[None], scores.reshape(num_heads, num_slots, num_slots), -1e30)
    prob_exact = jnp.exp(scores - log_total).reshape(-1, num_slots)
    delta_value = lax.dot_general(
        prob_exact.astype(jnp.bfloat16),
        head_delta,
        (((0,), (0,)), ((), ())),
        preferred_element_type=jnp.float32,
    )
    delta_prob = lax.dot_general(
        head_delta, value_vec, (((1,), (1,)), ((), ())), preferred_element_type=jnp.float32
    )
    delta_score = (prob_exact * (delta_prob - row_dot)).astype(jnp.bfloat16)
    delta_query = jnp.dot(delta_score, rot_key, preferred_element_type=jnp.float32).reshape(
        num_heads, num_slots, HD
    )
    delta_key = lax.dot_general(
        delta_score, flat_query, (((0,), (0,)), ((), ())), preferred_element_type=jnp.float32
    )
    return (delta_query, delta_key, delta_value.astype(jnp.bfloat16))


def flat_table(arrays, devices):
    return jnp.concatenate([member.reshape(-1) for member in arrays]).reshape(devices, -1)


def unpack_weights(attn_flat, ffn_flat, gain_flat):
    cut_query = D * HQ
    cut_key = cut_query + D * HD
    cut_value = cut_key + D * HD
    query_weight = attn_flat[:cut_query].reshape(D, HQ)
    key_weight = attn_flat[cut_query:cut_key].reshape(D, HD)
    value_weight = attn_flat[cut_key:cut_value].reshape(D, HD)
    out_weight = attn_flat[cut_value:].reshape(HQ, D)
    cut_gate = D * FF
    gate_weight = ffn_flat[:cut_gate].reshape(D, FF)
    up_weight = ffn_flat[cut_gate : 2 * cut_gate].reshape(D, FF)
    down_weight = ffn_flat[2 * cut_gate :].reshape(FF, D)
    gains = gain_flat.astype(jnp.float32)
    gain_set = (
        gains[:D],
        gains[D : D + HD],
        gains[D + HD : D + 2 * HD],
        gains[D + 2 * HD : 2 * D + 2 * HD],
        gains[2 * D + 2 * HD : 3 * D + 2 * HD],
        gains[3 * D + 2 * HD :],
    )
    return (
        query_weight,
        key_weight,
        value_weight,
        out_weight,
        gate_weight,
        up_weight,
        down_weight,
        gain_set,
    )


def forward_pass(input_rows, weights, allowed, cos_tab, sin_tab):
    (
        query_weight,
        key_weight,
        value_weight,
        out_weight,
        gate_weight,
        up_weight,
        down_weight,
        gain_set,
    ) = weights
    gain_in, gain_query, gain_key, gain_post, gain_mid, gain_last = gain_set
    resid_in = input_rows.astype(jnp.float32)
    normed_in = rms_scale(resid_in, gain_in).astype(jnp.bfloat16)
    query_raw = jnp.dot(normed_in, query_weight, preferred_element_type=jnp.float32)
    key_raw = jnp.dot(normed_in, key_weight, preferred_element_type=jnp.float32)
    value_vec = jnp.dot(normed_in, value_weight, preferred_element_type=jnp.float32).astype(
        jnp.bfloat16
    )
    rot_query, rot_key = query_key(query_raw, key_raw, gain_query, gain_key, cos_tab, sin_tab)
    rot_query = rot_query.astype(jnp.bfloat16)
    rot_key = rot_key.astype(jnp.bfloat16)
    context, log_total = attend(rot_query, rot_key, value_vec, allowed)
    attn_out = jnp.dot(context, out_weight, preferred_element_type=jnp.float32)
    mid_stream = resid_in + rms_scale(attn_out, gain_post)
    normed_mid = rms_scale(mid_stream, gain_mid).astype(jnp.bfloat16)
    gate_proj = jnp.dot(normed_mid, gate_weight, preferred_element_type=jnp.float32)
    up_proj = jnp.dot(normed_mid, up_weight, preferred_element_type=jnp.float32)
    hidden = gated_gelu(gate_proj, up_proj).astype(jnp.bfloat16)
    ffn_out = jnp.dot(hidden, down_weight, preferred_element_type=jnp.float32)
    block_out = (mid_stream + rms_scale(ffn_out, gain_last)).astype(jnp.bfloat16)
    saved = (
        resid_in,
        normed_in,
        query_raw,
        key_raw,
        value_vec,
        rot_query,
        rot_key,
        context,
        log_total,
        attn_out,
        mid_stream,
        normed_mid,
        gate_proj,
        up_proj,
        hidden,
        ffn_out,
    )
    return (block_out, saved)


def ffn_backward(cot_rows, live_mask, weights, saved):
    gate_weight, up_weight, down_weight, gain_set = (weights[4], weights[5], weights[6], weights[7])
    gain_mid, gain_last = (gain_set[4], gain_set[5])
    mid_stream, normed_mid, gate_proj, up_proj, hidden, ffn_out = saved[10:]
    delta_out = cot_rows.astype(jnp.float32) * live_mask[:, None]
    unused, pullback = jax.vjp(rms_scale, ffn_out, gain_last)
    delta_ffn, gain_last_grad = pullback(delta_out)
    delta_ffn = delta_ffn.astype(jnp.bfloat16)
    down_grad = outer_sum(hidden, delta_ffn)
    delta_hidden = times_transposed(delta_ffn, down_weight)
    unused, pullback = jax.vjp(gated_gelu, gate_proj, up_proj)
    delta_gate, delta_up = pullback(delta_hidden)
    delta_gate = delta_gate.astype(jnp.bfloat16)
    delta_up = delta_up.astype(jnp.bfloat16)
    gate_grad = outer_sum(normed_mid, delta_gate)
    up_grad = outer_sum(normed_mid, delta_up)
    delta_normed = times_transposed(delta_gate, gate_weight) + times_transposed(delta_up, up_weight)
    unused, pullback = jax.vjp(rms_scale, mid_stream, gain_mid)
    delta_part, gain_mid_grad = pullback(delta_normed)
    delta_mid = delta_out + delta_part
    return (delta_mid, (gate_grad, up_grad, down_grad), (gain_mid_grad, gain_last_grad))


def attn_backward(delta_mid, weights, saved, allowed, cos_tab, sin_tab):
    query_weight, key_weight, value_weight, out_weight = weights[:4]
    gain_in, gain_query, gain_key, gain_post = weights[7][:4]
    (
        resid_in,
        normed_in,
        query_raw,
        key_raw,
        value_vec,
        rot_query,
        rot_key,
        context,
        log_total,
        attn_out,
    ) = saved[:10]
    unused, pullback = jax.vjp(rms_scale, attn_out, gain_post)
    delta_attn, gain_post_grad = pullback(delta_mid)
    delta_attn = delta_attn.astype(jnp.bfloat16)
    out_grad = outer_sum(context, delta_attn)
    delta_context = times_transposed(delta_attn, out_weight).astype(jnp.bfloat16)
    delta_query, delta_key, delta_value = attend_back(
        rot_query, rot_key, value_vec, allowed, log_total, context, delta_context
    )

    def rope_map(raw_query, raw_key, query_gain, key_gain):
        return query_key(raw_query, raw_key, query_gain, key_gain, cos_tab, sin_tab)

    unused, pullback = jax.vjp(rope_map, query_raw, key_raw, gain_query, gain_key)
    delta_qraw, delta_kraw, gain_query_grad, gain_key_grad = pullback((delta_query, delta_key))
    delta_qraw = delta_qraw.astype(jnp.bfloat16)
    delta_kraw = delta_kraw.astype(jnp.bfloat16)
    query_grad = outer_sum(normed_in, delta_qraw)
    key_grad = outer_sum(normed_in, delta_kraw)
    value_grad = outer_sum(normed_in, delta_value)
    delta_in = (
        times_transposed(delta_qraw, query_weight)
        + times_transposed(delta_kraw, key_weight)
        + times_transposed(delta_value, value_weight)
    )
    unused, pullback = jax.vjp(rms_scale, resid_in, gain_in)
    delta_part, gain_in_grad = pullback(delta_in)
    grad_in = delta_mid + delta_part
    return (
        grad_in,
        (query_grad, key_grad, value_grad, out_grad),
        (gain_in_grad, gain_query_grad, gain_key_grad, gain_post_grad),
    )


def adam_update(weight_shard, gradient, moment_one, moment_two):
    moment_one = 0.9 * moment_one + 0.1 * gradient
    moment_two = 0.999 * moment_two + 0.001 * gradient * gradient
    fix_one = 1.0 - 0.9**STEP
    fix_two = 1.0 - 0.999**STEP
    weight_shard = weight_shard - 0.02 * (
        moment_one / fix_one / (jnp.sqrt(moment_two / fix_two) + 1e-08) + 0.1 * weight_shard
    )
    return (weight_shard, moment_one, moment_two)


def per_device(hidden_in, cotangent, params, moment_one, moment_two, seq_lengths, seq_owner):
    devices = lax.axis_size("dp")
    attn_len = G1LEN // devices
    ffn_len = G2LEN // devices
    rounded = params.astype(jnp.bfloat16)
    attn_flat, ffn_flat, gain_flat = (
        lax.all_gather(rounded[:attn_len], "dp", axis=0, tiled=True),
        lax.all_gather(rounded[attn_len : attn_len + ffn_len], "dp", axis=0, tiled=True),
        lax.all_gather(rounded[attn_len + ffn_len :], "dp", axis=0, tiled=True),
    )
    weights = unpack_weights(attn_flat, ffn_flat, gain_flat)
    device = lax.axis_index("dp")
    live_mask, allowed, cos_tab, sin_tab = slot_setup(seq_lengths, seq_owner, device)
    block_out, saved = forward_pass(hidden_in, weights, allowed, cos_tab, sin_tab)
    delta_mid, ffn_grads, late_gains = ffn_backward(cotangent, live_mask, weights, saved)
    ffn_group = flat_table(ffn_grads, devices)
    grad_in, attn_grads, early_gains = attn_backward(
        delta_mid, weights, saved, allowed, cos_tab, sin_tab
    )
    attn_group = flat_table(attn_grads, devices)
    gain_group = flat_table(early_gains + late_gains, devices)
    attn_shard, ffn_shard, gain_shard = (
        lax.psum_scatter(attn_group, "dp", scatter_dimension=0, tiled=True),
        lax.psum_scatter(ffn_group, "dp", scatter_dimension=0, tiled=True),
        lax.psum_scatter(gain_group, "dp", scatter_dimension=0, tiled=True),
    )
    grad_shard = jnp.concatenate(
        [attn_shard.reshape(-1), ffn_shard.reshape(-1), gain_shard.reshape(-1)]
    )
    params_new, moment_one_new, moment_two_new = adam_update(
        params, grad_shard, moment_one, moment_two
    )
    return (block_out, grad_in, grad_shard, params_new, moment_one_new, moment_two_new)


def solution(mesh):
    in_specs = (P("dp", None), P("dp", None), P("dp"), P("dp"), P("dp"), P(), P())
    out_specs = (P("dp", None), P("dp", None), P("dp"), P("dp"), P("dp"), P("dp"))
    return jax.shard_map(
        per_device, mesh=mesh, in_specs=in_specs, out_specs=out_specs, check_vma=False
    )
```

profile of v0, /device:TPU:0, one launch (start us, length us, event | category | flops | bytes accessed | tf_op | source)
XLA Modules:
  0.0 640.7 jit_solution(17678911759446597382)
XLA Ops:
  12.6 42.1 %all-reduce.4 = bf16[3072]{0:T(1024)(128)(2,1)S(1)} all-reduce(bf16[3072]{0:T(1024)(128)(2,1)S(1)} %dynamic-update-slice), channel_id=1, replica_groups=mesh['dp'=32] {'dp'}, use_global_device_ids=true, to_apply=%add.4 | all-reduce | flops 3072 | bytes 12288
  57.6 15.9 %all-gather.3.cloned.1.call-done = bf16[1638400]{0:T(1024)(128)(2,1)} async-done(((bf16[51200]{0:T(1024)(128)(2,1)}), bf16[1638400]{0:T(1024)(128)(2,1)}) %all-gather.3.cloned.1.call-update) | async-done | bytes 3276816 | tf_op jit(solution)/shard_map/all_gather | solution.py:325
  73.5 3.0 fusion.90
  80.0 2.5 slice.134
  84.5 2.0 multiply_reduce_fusion.3
  91.5 59.1 %all-gather.5.cloned.1.call-done = bf16[3932160]{0:T(1024)(128)(2,1)} async-done(((bf16[122880]{0:T(1024)(128)(2,1)}), bf16[3932160]{0:T(1024)(128)(2,1)}) %all-gather.5.cloned.1.call-update) | async-done | bytes 7864336 | tf_op jit(solution)/shard_map/all_gather | solution.py:326
  150.5 5.0 fusion.89
  155.6 3.1 slice.155
  158.7 3.8 slice.153
  162.5 5.2 slice.151
  167.7 2.3 fusion.93
  181.1 3.3 fusion.76
  184.4 3.1 convolution_bitcast_fusion
  187.6 3.2 convolution_bitcast_fusion.1
  214.4 8.2 %pad_maximum_fusion.1 = f32[1638400]{0:T(1024)} fusion(f32[655360]{0:T(1024)S(1)} %copy-done.6, f32[163840]{0:T(1024)S(1)} %bitcast.107, f32[163840]{0:T(1024)S(1)} %bitcast.108, f32[655360]{0:T(1024)S(1)} %bitcast.104), kind=kLoop, calls=%fused_computation.1 | loop fusion | flops 4915200 | bytes 13107200 | tf_op jit(solution)/shard_map/concatenate | solution.py:148
  222.6 6.3 reshape.479
  228.9 6.6 %reshape.483 = f32[1310720]{0:T(1024)} reshape(f32[2048,640]{1,0:T(8,128)} %fusion.76) | data formatting | bytes 10485760 | tf_op jit(solution)/shard_map/reshape | solution.py:148
  235.6 3.9 copy.41
  241.0 17.2 %pad_maximum_fusion = f32[3932160]{0:T(1024)} fusion(f32[1310720]{0:T(1024)S(1)} %bitcast.100, f32[1310720]{0:T(1024)S(1)} %bitcast.101, f32[1310720]{0:T(1024)S(1)} %bitcast.102), kind=kLoop, calls=%fused_computation | loop fusion | flops 7864320 | bytes 31457280 | tf_op jit(solution)/shard_map/concatenate | solution.py:148
  258.2 11.7 %reshape.484 = f32[32,122880]{1,0:T(8,128)} reshape(f32[3932160]{0:T(1024)} %pad_maximum_fusion) | data formatting | bytes 31457280 | tf_op jit(solution)/shard_map/reshape | solution.py:148
  272.6 41.2 %all-reduce.7 = f32[32,96]{1,0:T(8,128)S(1)} all-reduce(f32[32,96]{1,0:T(8,128)S(1)} %reshape.486), channel_id=4, replica_groups=mesh['dp'=32] {'dp'}, use_global_device_ids=true, to_apply=%region_27.28.clone | all-reduce | flops 3072 | bytes 24576
  314.7 312.7 %all-reduce.11.cloned.1.call-done = (f32[32,122880]{1,0:T(8,128)}, f32[32,51200]{1,0:T(8,128)}) async-done(((f32[32,122880]{1,0:T(8,128)}, f32[32,51200]{1,0:T(8,128)}), (f32[32,122880]{1,0:T(8,128)}, f32[32,51200]{1,0:T(8,128)})) %all-reduce.11.cloned.1.call-update) | async-done | bytes 22282256
  627.3 2.5 constant_dynamic-slice_fusion.1
  631.4 2.8 multiply_subtract_fusion
  (255 shorter events, 59.2 us)
Async XLA Ops:
  7.2 66.3 %all-gather.3.cloned.1.call-start = ((), (), s32[]{:S(2)}) async-start(), calls=%async_computation | async-start | bytes 3379200 | tf_op jit(solution)/shard_map/all_gather | solution.py:325
  9.0 141.5 %all-gather.5.cloned.1.call-start = ((), (), s32[]{:S(2)}) async-start(), calls=%async_computation.1 | async-start | bytes 8110080 | tf_op jit(solution)/shard_map/all_gather | solution.py:326
  9.8 617.5 %all-reduce.11.cloned.1.call-start = ((), (), s32[]{:S(2)}) async-start(), calls=%async_computation.2 | async-start | bytes 44564480
  55.3 31.3 %copy-start.46 = (f32[256]{0:T(256)}, f32[256]{0:T(256)S(1)}, u32[]{:S(2)}) copy-start(f32[256]{0:T(256)S(1)} %get-tuple-element.53) | copy-start | bytes 3076
  56.3 31.6 %copy-start.44 = (f32[128]{0:T(128)}, f32[128]{0:T(128)S(1)}, u32[]{:S(2)}) copy-start(f32[128]{0:T(128)S(1)} %fusion.63) | copy-start | bytes 1540
  77.4 11.6 %copy-start.3 = (bf16[1024,640]{1,0:T(8,128)(2,1)}, bf16[1024,640]{1,0:T(8,128)(2,1)S(1)}, u32[]{:S(2)}) copy-start(bf16[1024,640]{1,0:T(8,128)(2,1)S(1)} %slice.146) | copy-start | bytes 3932164
  190.7 8.1 %copy-start.37 = (bf16[128,128]{1,0:T(8,128)(2,1)S(1)}, bf16[128,128]{1,0:T(8,128)(2,1)}, u32[]{:S(2)}) copy-start(bf16[128,128]{1,0:T(8,128)(2,1)} %copy-done.36) | copy-start | bytes 98308
  190.7 10.3 %copy-start.25 = (f32[128,256]{1,0:T(8,128)S(1)}, f32[128,256]{1,0:T(8,128)}, u32[]{:S(2)}) copy-start(f32[128,256]{1,0:T(8,128)} %copy-done.24) | copy-start | bytes 393220
  190.7 10.3 %copy-start.47 = (f32[256]{0:T(256)S(1)}, f32[256]{0:T(256)}, u32[]{:S(2)}) copy-start(f32[256]{0:T(256)} %copy-done.46) | copy-start | bytes 3076
  190.7 10.3 %copy-start.54 = (f32[128]{0:T(128)S(1)}, f32[128]{0:T(128)}, u32[]{:S(2)}) copy-start(f32[128]{0:T(128)} %copy-done.53) | copy-start | bytes 1540
  194.4 5.4 copy-start.27
  194.4 5.4 copy-start.29
  194.4 8.7 %copy-start.33 = (f32[128,128]{1,0:T(8,128)S(1)}, f32[128,128]{1,0:T(8,128)}, u32[]{:S(2)}) copy-start(f32[128,128]{1,0:T(8,128)} %copy-done.32) | copy-start | bytes 196612
  194.4 8.8 %copy-start.41 = (f32[4,128]{1,0:T(4,128)S(1)}, f32[4,128]{1,0:T(4,128)}, u32[]{:S(2)}) copy-start(f32[4,128]{1,0:T(4,128)} %copy-done.40) | copy-start | bytes 6148
  194.4 8.8 %copy-start.52 = (f32[256]{0:T(256)S(1)}, f32[256]{0:T(256)}, u32[]{:S(2)}) copy-start(f32[256]{0:T(256)} %get-tuple-element.54) | copy-start | bytes 3076
  197.5 5.9 copy-start.43
  200.1 6.1 copy-start.45
  203.2 4.5 copy-start.35
  228.9 10.5 %slice-start = ((s8[5242880]{0:T(1024)(128)(4,1)}), s8[1048576]{0:T(1024)(128)(4,1)S(1)}, s32[]{:S(2)}) async-start(s8[5242880]{0:T(1024)(128)(4,1)} %bitcast.97), calls=%async_computation.3 | async-start | bytes 2097152
  235.6 5.1 slice-start.2
  270.0 43.8 %copy-start.64 = (f32[128]{0:T(128)S(1)}, f32[128]{0:T(128)}, u32[]{:S(2)}) copy-start(f32[128]{0:T(128)} %copy-done.63) | copy-start | bytes 1540
  270.0 43.8 %copy-start.13 = (f32[128,640]{1,0:T(8,128)S(1)}, f32[128,640]{1,0:T(8,128)}, u32[]{:S(2)}) copy-start(f32[128,640]{1,0:T(8,128)} %copy-done.12) | copy-start | bytes 983044
  271.8 359.6 %copy-start.14 = (f32[174176]{0:T(1024)S(1)}, f32[174176]{0:T(1024)}, u32[]{:S(2)}) copy-start(f32[174176]{0:T(1024)} %param.9) | copy-start | bytes 2090116
  271.8 359.6 %copy-start.31 = (f32[174176]{0:T(1024)S(1)}, f32[174176]{0:T(1024)}, u32[]{:S(2)}) copy-start(f32[174176]{0:T(1024)} %param.10) | copy-start | bytes 2090116
  (53 other events, 107.4 us)
Sparse Core Ops, SparseCore 0:
  11.4 61.9 all-gather.2
  76.4 74.1 all-gather.4
  270.0 357.2 all-reduce.10
where the time goes:
time: 642 us; the launch traced here: 641 us
  waiting for transfers between devices  388 us (60%)
  blocking collectives  83.2 us (13%)
  local copies, waits for them, and re-layouts  77.9 us (12%)
  other arithmetic  45.4 us (7%)
  matrix products  31.4 us (5%)
  between operations  15 us (2%)
    unnamed x4, waiting for transfers between devices  313 us
    unnamed x2, blocking collectives  83.2 us
    all_gather x1, waiting for transfers between devices, per_device(): lax.all_gather(rounded[attn_len:attn_len + ffn_len], 'dp', axis=0, tiled=...  59.1 us
    concatenate x2, other arithmetic, flat_table(): jnp.concatenate([member.reshape(-1) for member in arrays])  25.4 us
    reshape x3, local copies, waits for them, and re-layouts, flat_table(): jnp.concatenate([member.reshape(-1) for member in arrays])  18.1 us
    unnamed x162, local copies, waits for them, and re-layouts  16.7 us
    all_gather x1, waiting for transfers between devices, per_device(): lax.all_gather(rounded[:attn_len], 'dp', axis=0, tiled=True)  15.9 us
    dot_general x7, matrix products, outer_sum(): lax.dot_general(left_side, right_side, (((0,), (0,)), ((), ())), preferre...  13.2 us
  transfers between devices with their start and end apart: 3, of which 3 were waited for; matrix products, arithmetic and copies ran while one was open for 4% of the time, Pallas kernels for 0%

commit v1 on v0

--- a/solution.py
+++ b/solution.py
@@ -1,6 +1,10 @@
+import functools
+
 import jax
 import jax.numpy as jnp
 from jax import lax
+from jax.experimental import pallas as pl
+from jax.experimental.pallas import tpu as pltpu
 from jax.sharding import PartitionSpec as P
 
 D = 640
@@ -12,6 +16,10 @@
 STEP = 3
 G1LEN = 1638400
 G2LEN = 3932160
+LANES = 128
+ROWS = 16
+ATTN_SIZES = ((D, HQ), (D, HD), (D, HD), (HQ, D))
+FFN_SIZES = ((D, FF), (D, FF), (FF, D))
 
 
 def rms_scale(values, gain_vec):
@@ -41,12 +49,6 @@
 
 def gated_gelu(gate_proj, up_proj):
     return jax.nn.gelu(gate_proj, approximate=True) * up_proj
-
-
-def outer_sum(left_side, right_side):
-    return lax.dot_general(
-        left_side, right_side, (((0,), (0,)), ((), ())), preferred_element_type=jnp.float32
-    )
 
 
 def times_transposed(rows_in, matrix):
@@ -144,40 +146,287 @@
     return (delta_query, delta_key, delta_value.astype(jnp.bfloat16))
 
 
-def flat_table(arrays, devices):
-    return jnp.concatenate([member.reshape(-1) for member in arrays]).reshape(devices, -1)
-
-
-def unpack_weights(attn_flat, ffn_flat, gain_flat):
-    cut_query = D * HQ
-    cut_key = cut_query + D * HD
-    cut_value = cut_key + D * HD
-    query_weight = attn_flat[:cut_query].reshape(D, HQ)
-    key_weight = attn_flat[cut_query:cut_key].reshape(D, HD)
-    value_weight = attn_flat[cut_key:cut_value].reshape(D, HD)
-    out_weight = attn_flat[cut_value:].reshape(HQ, D)
-    cut_gate = D * FF
-    gate_weight = ffn_flat[:cut_gate].reshape(D, FF)
-    up_weight = ffn_flat[cut_gate : 2 * cut_gate].reshape(D, FF)
-    down_weight = ffn_flat[2 * cut_gate :].reshape(FF, D)
+def bit_orders(devices, tuned):
+    bits = devices.bit_length() - 1
+    if bits == 5:
+        return [["cxyab".index(letter) for letter in order] for order in tuned]
+    return [[1 + (shift + step) % (bits - 1) for step in range(bits - 1)] for shift in range(3)]
+
+
+def across(block, bit, devices):
+    return lax.ppermute(block, "dp", [(i, i ^ (1 << bit)) for i in range(devices)])
+
+
+def offset_of(place, order):
+    return sum(((place >> k) & 1) << bit for k, bit in enumerate(order))
+
+
+def gather_chunk(piece, order, devices):
+    held = piece[None]
+    for bit in order[:-1]:
+        held = jnp.concatenate([held, across(held, bit, devices)])
+    last = across(held, order[-1], devices)
+    return (held, last, across(held, 0, devices), across(last, 0, devices))
+
+
+def scatter_chunk(home, away, order, devices):
+    for bit in [0] + list(order):
+        came = across(away, bit, devices)
+        half = home.shape[0] // 2
+
+        def added(low, high):
+            total = home[low:high].astype(jnp.float32) + came[low:high].astype(jnp.float32)
+            return total.astype(jnp.bfloat16) if half else total
+
+        if half:
+            home, away = (added(0, half), added(half, 2 * half))
+        else:
+            home = added(0, 1)
+    return home[0]
+
+
+def cut_rows(rows, parts):
+    each = -(-rows // (parts * ROWS)) * ROWS
+    return [(low, min(low + each, rows)) for low in range(0, rows, each)]
+
+
+def whole_specs(count):
+    return [pl.BlockSpec(memory_space=pltpu.VMEM)] * count
+
+
+def place_specs(count):
+    return [pl.BlockSpec(memory_space=pl.ANY)] * count
+
+
+def unpack_kernel(plan, sizes, tail_rows, sources, device_ref, *refs):
+    source_refs = refs[:sources]
+    matrices = refs[sources : sources + len(sizes)]
+    refs = refs[sources + len(sizes) :]
+    tails = None
+    if tail_rows:
+        tails, refs = refs[0], refs[1:]
+    flat, spread, sems = refs
+    device = device_ref[0]
+    copies = []
+    for source, index, offset, low, take, start, each in plan:
+        owner = device ^ offset
+        if start is None:
+            target = tails.at[owner]
+        else:
+            target = flat.at[pl.ds(pl.multiple_of(owner * each + start, ROWS), take), :]
+        copies.append(
+            pltpu.make_async_copy(
+                source_refs[source].at[index, pl.ds(low, take), :], target, sems.at[len(copies)]
+            )
+        )
+    for copy in copies:
+        copy.start()
+    for copy in copies:
+        copy.wait()
+    first = 0
+    for matrix, (rows, columns) in zip(matrices, sizes):
+        blocks = columns // LANES
+
+        @pl.loop(0, rows // LANES)
+        def _(step, matrix=matrix, blocks=blocks, first=first):
+            base = pl.multiple_of(first + step * (LANES * blocks), ROWS)
+            spread[: LANES * blocks] = flat[pl.ds(base, LANES * blocks), :].astype(jnp.float32)
+            at = pl.ds(pl.multiple_of(step * LANES, LANES), LANES)
+            for block in range(blocks):
+                matrix[at, block * LANES : (block + 1) * LANES] = spread[
+                    pl.ds(block, LANES, stride=blocks), :
+                ].astype(jnp.bfloat16)
+
+        first += rows * blocks
+
+
+def unpack_matrices(plan, sizes, tail_rows, device, arrays, devices):
+    flat_rows = sum(rows * columns for rows, columns in sizes) // LANES
+    widest = max(columns for _, columns in sizes)
+    shapes = [jax.ShapeDtypeStruct(size, jnp.bfloat16) for size in sizes]
+    if tail_rows:
+        shapes.append(jax.ShapeDtypeStruct((devices, tail_rows, LANES), jnp.bfloat16))
+    return pl.pallas_call(
+        functools.partial(unpack_kernel, plan, sizes, tail_rows, len(arrays)),
+        out_shape=shapes,
+        in_specs=[pl.BlockSpec(memory_space=pltpu.SMEM)] + place_specs(len(arrays)),
+        out_specs=whole_specs(len(shapes)),
+        scratch_shapes=[
+            pltpu.VMEM((flat_rows, LANES), jnp.bfloat16),
+            pltpu.VMEM((widest, LANES), jnp.float32),
+            pltpu.SemaphoreType.DMA((len(plan),)),
+        ],
+        compiler_params=pltpu.CompilerParams(vmem_limit_bytes=40 << 20),
+        cost_estimate=pl.CostEstimate(
+            flops=0, bytes_accessed=flat_rows * LANES * 4, transcendentals=0
+        ),
+    )(device, *arrays)
+
+
+def grads_kernel(plan, sizes, has_tails, device_ref, *refs):
+    pairs = refs[: 2 * len(sizes)]
+    refs = refs[2 * len(sizes) :]
+    tails = None
+    if has_tails:
+        tails, refs = refs[0], refs[1:]
+    targets = refs[:-3]
+    spread, flat, sems = refs[-3:]
+    device = device_ref[0]
+    first = 0
+    for number, (rows, columns) in enumerate(sizes):
+        left, right = pairs[2 * number : 2 * number + 2]
+        blocks = columns // LANES
+        wide = 2 - blocks % 2
+        turned = left[...].T
+        for block in range(0, blocks, wide):
+            product = jnp.dot(
+                turned,
+                right[:, block * LANES : (block + wide) * LANES],
+                preferred_element_type=jnp.float32,
+            )
+            for part in range(wide):
+                spread[pl.ds(block + part, rows, stride=blocks), :] = product[
+                    :, part * LANES : (part + 1) * LANES
+                ]
+
+        step_rows = 1280 if rows * blocks % 1280 == 0 else 1024
+
+        @pl.loop(0, rows * blocks // step_rows)
+        def _(step, first=first, step_rows=step_rows):
+            low = pl.multiple_of(step * step_rows, step_rows)
+            flat[pl.ds(pl.multiple_of(first + low, ROWS), step_rows), :] = spread[
+                pl.ds(low, step_rows), :
+            ].astype(jnp.bfloat16)
+
+        first += rows * blocks
+    copies = []
+    for target, index, offset, low, take, start, each in plan:
+        owner = device ^ offset
+        if start is None:
+            source = tails.at[owner]
+        else:
+            source = flat.at[pl.ds(pl.multiple_of(owner * each + start, ROWS), take), :]
+        copies.append(
+            pltpu.make_async_copy(
+                source, targets[target].at[index, pl.ds(low, take), :], sems.at[len(copies)]
+            )
+        )
+    for copy in copies:
+        copy.start()
+    for copy in copies:
+        copy.wait()
+
+
+def grad_blocks(plan, sizes, pairs, tails, device, shapes):
+    flat_rows = sum(rows * columns for rows, columns in sizes) // LANES
+    longest = max(rows * columns for rows, columns in sizes) // LANES
+    inputs = [member for pair in pairs for member in pair] + ([] if tails is None else [tails])
+    return pl.pallas_call(
+        functools.partial(grads_kernel, plan, sizes, tails is not None),
+        out_shape=[jax.ShapeDtypeStruct(shape, jnp.bfloat16) for shape in shapes],
+        in_specs=[pl.BlockSpec(memory_space=pltpu.SMEM)] + whole_specs(len(inputs)),
+        out_specs=place_specs(len(shapes)),
+        scratch_shapes=[
+            pltpu.VMEM((longest, LANES), jnp.float32),
+            pltpu.VMEM((flat_rows, LANES), jnp.bfloat16),
+            pltpu.SemaphoreType.DMA((len(plan),)),
+        ],
+        compiler_params=pltpu.CompilerParams(vmem_limit_bytes=40 << 20),
+        cost_estimate=pl.CostEstimate(
+            flops=2 * CAP * flat_rows * LANES,
+            bytes_accessed=flat_rows * LANES * 4,
+            transcendentals=0,
+        ),
+    )(device, *inputs)
+
+
+def gathered_matrices(pieces, orders, sizes, tail_rows, devices, device):
+    each = sum(rows * columns for rows, columns in sizes) // LANES // devices
+    arrays, plan, start = [], [], 0
+    for piece, order in zip(pieces, orders):
+        blocks = gather_chunk(piece, order, devices)
+        take = min(piece.shape[0], each - start)
+        if each % ROWS:
+            table = jnp.concatenate(blocks)
+            places = [offset_of(place, list(order) + [0]) for place in range(devices)]
+            back = sorted(range(devices), key=places.__getitem__)
+            mixed = offset_bits(device[0], list(order) + [0])
+            arrays.append(jnp.take(table, jnp.array(back, jnp.int32) ^ mixed, axis=0))
+            continue
+        for part, block in enumerate(blocks):
+            for index in range(block.shape[0]):
+                offset = offset_of(part * block.shape[0] + index, list(order) + [0])
+                plan.append((len(arrays), index, offset, 0, take, start, each))
+                if take < piece.shape[0]:
+                    plan.append((len(arrays), index, offset, take, tail_rows, None, each))
+            arrays.append(block)
+        start += take
+    if each % ROWS == 0:
+        return unpack_matrices(plan, sizes, tail_rows, device, arrays, devices)
+    table = jnp.concatenate(arrays, axis=1)
+    flat = table[:, :each].reshape(1, devices * each, LANES)
+    plan = [(0, 0, 0, 0, devices * each, 0, 0)]
+    found = list(unpack_matrices(plan, sizes, 0, device, [flat], devices))
+    return found + ([table[:, each : each + tail_rows]] if tail_rows else [])
+
+
+def offset_bits(device, order):
+    return sum(((device >> bit) & 1) << k for k, bit in enumerate(order))
+
+
+def scattered_rows(pairs, tails, orders, sizes, devices, device):
+    each = sum(rows * columns for rows, columns in sizes) // LANES // devices
+    tail_rows = 0 if tails is None else tails.shape[1]
+    parts = cut_rows(each + tail_rows, 3)
+    half = devices // 2
+    plan, shapes = [], []
+    for (low, high), order in zip(parts, orders):
+        order = list(order)[::-1]
+        for with_core in (0, 1):
+            for index in range(half):
+                offset = offset_of(index, order) ^ with_core
+                take = min(high, each) - low
+                plan.append((len(shapes), index, offset, 0, take, low, each))
+                if high > each:
+                    plan.append((len(shapes), index, offset, take, tail_rows, None, each))
+            shapes.append((half, high - low, LANES))
+    if each % ROWS == 0 and parts[-1][0] < each:
+        blocks = grad_blocks(plan, sizes, pairs, tails, device, shapes)
+    else:
+        flat = grad_blocks(
+            [(0, 0, 0, 0, devices * each, 0, 0)],
+            sizes,
+            pairs,
+            None,
+            device,
+            [(1, devices * each, LANES)],
+        )[0]
+        table = flat.reshape(devices, each, LANES)
+        table = table if tails is None else jnp.concatenate([table, tails], axis=1)
+        blocks = []
+        for (low, high), order in zip(parts, orders):
+            order = list(order)[::-1]
+            for with_core in (0, 1):
+                offsets = [offset_of(index, order) ^ with_core for index in range(half)]
+                owners = jnp.array(offsets, jnp.int32) ^ device[0]
+                blocks.append(jnp.take(table[:, low:high], owners, axis=0))
+    return jnp.concatenate(
+        [
+            scatter_chunk(blocks[2 * k], blocks[2 * k + 1], order, devices)
+            for k, order in enumerate(orders[: len(parts)])
+        ]
+    )
+
+
+def cut_gains(gain_flat):
     gains = gain_flat.astype(jnp.float32)
-    gain_set = (
+    return (
         gains[:D],
         gains[D : D + HD],
         gains[D + HD : D + 2 * HD],
         gains[D + 2 * HD : 2 * D + 2 * HD],
         gains[2 * D + 2 * HD : 3 * D + 2 * HD],
         gains[3 * D + 2 * HD :],
-    )
-    return (
-        query_weight,
-        key_weight,
-        value_weight,
-        out_weight,
-        gate_weight,
-        up_weight,
-        down_weight,
-        gain_set,
     )
 
 
@@ -241,19 +490,17 @@
     unused, pullback = jax.vjp(rms_scale, ffn_out, gain_last)
     delta_ffn, gain_last_grad = pullback(delta_out)
     delta_ffn = delta_ffn.astype(jnp.bfloat16)
-    down_grad = outer_sum(hidden, delta_ffn)
     delta_hidden = times_transposed(delta_ffn, down_weight)
     unused, pullback = jax.vjp(gated_gelu, gate_proj, up_proj)
     delta_gate, delta_up = pullback(delta_hidden)
     delta_gate = delta_gate.astype(jnp.bfloat16)
     delta_up = delta_up.astype(jnp.bfloat16)
-    gate_grad = outer_sum(normed_mid, delta_gate)
-    up_grad = outer_sum(normed_mid, delta_up)
     delta_normed = times_transposed(delta_gate, gate_weight) + times_transposed(delta_up, up_weight)
     unused, pullback = jax.vjp(rms_scale, mid_stream, gain_mid)
     delta_part, gain_mid_grad = pullback(delta_normed)
     delta_mid = delta_out + delta_part
-    return (delta_mid, (gate_grad, up_grad, down_grad), (gain_mid_grad, gain_last_grad))
+    pairs = ((normed_mid, delta_gate), (normed_mid, delta_up), (hidden, delta_ffn))
+    return (delta_mid, pairs, (gain_mid_grad, gain_last_grad))
 
 
 def attn_backward(delta_mid, weights, saved, allowed, cos_tab, sin_tab):
@@ -274,7 +521,6 @@
     unused, pullback = jax.vjp(rms_scale, attn_out, gain_post)
     delta_attn, gain_post_grad = pullback(delta_mid)
     delta_attn = delta_attn.astype(jnp.bfloat16)
-    out_grad = outer_sum(context, delta_attn)
     delta_context = times_transposed(delta_attn, out_weight).astype(jnp.bfloat16)
     delta_query, delta_key, delta_value = attend_back(
         rot_query, rot_key, value_vec, allowed, log_total, context, delta_context
@@ -287,9 +533,12 @@
     delta_qraw, delta_kraw, gain_query_grad, gain_key_grad = pullback((delta_query, delta_key))
     delta_qraw = delta_qraw.astype(jnp.bfloat16)
     delta_kraw = delta_kraw.astype(jnp.bfloat16)
-    query_grad = outer_sum(normed_in, delta_qraw)
-    key_grad = outer_sum(normed_in, delta_kraw)
-    value_grad = outer_sum(normed_in, delta_value)
+    pairs = (
+        (normed_in, delta_qraw),
+        (normed_in, delta_kraw),
+        (normed_in, delta_value),
+        (context, delta_attn),
+    )
     delta_in = (
         times_transposed(delta_qraw, query_weight)
         + times_transposed(delta_kraw, key_weight)
@@ -300,7 +549,7 @@
     grad_in = delta_mid + delta_part
     return (
         grad_in,
-        (query_grad, key_grad, value_grad, out_grad),
+        pairs,
         (gain_in_grad, gain_query_grad, gain_key_grad, gain_post_grad),
     )
 
@@ -318,32 +567,44 @@
 
 def per_device(hidden_in, cotangent, params, moment_one, moment_two, seq_lengths, seq_owner):
     devices = lax.axis_size("dp")
+    device = lax.axis_index("dp").astype(jnp.int32)
+    here = device.reshape(1)
     attn_len = G1LEN // devices
     ffn_len = G2LEN // devices
+    gain_len = params.shape[0] - attn_len - ffn_len
+    attn_rows = attn_len // LANES
+    tail_rows = -(-(attn_rows + 1) // ROWS) * ROWS - attn_rows
+    pad = tail_rows * LANES - gain_len
     rounded = params.astype(jnp.bfloat16)
-    attn_flat, ffn_flat, gain_flat = (
-        lax.all_gather(rounded[:attn_len], "dp", axis=0, tiled=True),
-        lax.all_gather(rounded[attn_len : attn_len + ffn_len], "dp", axis=0, tiled=True),
-        lax.all_gather(rounded[attn_len + ffn_len :], "dp", axis=0, tiled=True),
-    )
-    weights = unpack_weights(attn_flat, ffn_flat, gain_flat)
-    device = lax.axis_index("dp")
+    first_piece = jnp.concatenate(
+        [rounded[:attn_len], rounded[attn_len + ffn_len :], jnp.zeros((pad,), jnp.bfloat16)]
+    ).reshape(-1, LANES)
+    second_piece = rounded[attn_len : attn_len + ffn_len].reshape(-1, LANES)
+    second_pieces = [second_piece[low:high] for low, high in cut_rows(ffn_len // LANES, 2)]
+    orders = bit_orders(devices, ("abxy", "bxya", "byax"))
+    *attn_weights, tails = gathered_matrices(
+        [first_piece], orders[:1], ATTN_SIZES, tail_rows, devices, here
+    )
+    ffn_weights = gathered_matrices(second_pieces, orders[1:], FFN_SIZES, 0, devices, here)
+    gain_flat = tails.reshape(devices, -1)[:, :gain_len].reshape(-1)
+    weights = (*attn_weights, *ffn_weights, cut_gains(gain_flat))
     live_mask, allowed, cos_tab, sin_tab = slot_setup(seq_lengths, seq_owner, device)
     block_out, saved = forward_pass(hidden_in, weights, allowed, cos_tab, sin_tab)
-    delta_mid, ffn_grads, late_gains = ffn_backward(cotangent, live_mask, weights, saved)
-    ffn_group = flat_table(ffn_grads, devices)
-    grad_in, attn_grads, early_gains = attn_backward(
+    delta_mid, ffn_pairs, late_gains = ffn_backward(cotangent, live_mask, weights, saved)
+    orders = bit_orders(devices, ("yxba", "ayxb", "xayb"))
+    ffn_shard = scattered_rows(ffn_pairs, None, orders, FFN_SIZES, devices, here)
+    grad_in, attn_pairs, early_gains = attn_backward(
         delta_mid, weights, saved, allowed, cos_tab, sin_tab
     )
-    attn_group = flat_table(attn_grads, devices)
-    gain_group = flat_table(early_gains + late_gains, devices)
-    attn_shard, ffn_shard, gain_shard = (
-        lax.psum_scatter(attn_group, "dp", scatter_dimension=0, tiled=True),
-        lax.psum_scatter(ffn_group, "dp", scatter_dimension=0, tiled=True),
-        lax.psum_scatter(gain_group, "dp", scatter_dimension=0, tiled=True),
-    )
+    gain_table = jnp.concatenate(early_gains + late_gains).reshape(devices, gain_len)
+    gain_table = jnp.pad(gain_table.astype(jnp.bfloat16), ((0, 0), (0, pad)))
+    gain_table = gain_table.reshape(devices, tail_rows, LANES)
+    orders = bit_orders(devices, ("yabx", "axyb", "xyab"))
+    attn_shard = scattered_rows(
+        attn_pairs, gain_table, orders, ATTN_SIZES, devices, here
+    ).reshape(-1)
     grad_shard = jnp.concatenate(
-        [attn_shard.reshape(-1), ffn_shard.reshape(-1), gain_shard.reshape(-1)]
+        [attn_shard[:attn_len], ffn_shard.reshape(-1), attn_shard[attn_len : attn_len + gain_len]]
     )
     params_new, moment_one_new, moment_two_new = adam_update(
         params, grad_shard, moment_one, moment_two

time: 642 us -> 252 us (0.39)
  waiting for transfers between devices: 388 us -> 92.9 us
  blocking collectives: 83.2 us -> 0 us
  local copies, waits for them, and re-layouts: 77.9 us -> 17.4 us
  starting transfers between devices: 0.12 us -> 54.1 us
  Pallas kernels: 0 us -> 46.1 us
  other arithmetic: 45.4 us -> 23.8 us
  matrix products: 31.4 us -> 14.7 us
  between operations: 15 us -> 2.03 us
    unnamed x4 -> x0, waiting for transfers between devices: 313 us -> none
    ppermute x0 -> x48, waiting for transfers between devices: none -> 92.9 us  [across(): lax.ppermute(block, 'dp', [(i, i ^ 1 << bit) for i in range(devices)])]
    unnamed x2 -> x0, blocking collectives: 83.2 us -> none
    all_gather x2 -> x0, waiting for transfers between devices: 74.9 us -> none  [the longest x1 59.1 us: per_device(): lax.all_gather(rounded[attn_len:attn_len + ffn_len], 'dp', axis=0, tiled=...]
    ppermute x0 -> x48, starting transfers between devices: none -> 54.1 us  [across(): lax.ppermute(block, 'dp', [(i, i ^ 1 << bit) for i in range(devices)])]
    pallas_call x0 -> x4, Pallas kernels: none -> 46.1 us  [the longest x2 28.6 us: grad_blocks(): pl.pallas_call(functools.partial(grads_kernel, plan, sizes, tails is not...]
    slice x11 -> x2, local copies, waits for them, and re-layouts: 26.9 us -> 0.02 us  [the longest x1 0.01 us: per_device(): attn_shard[:attn_len]]
    reshape x6 -> x0, local copies, waits for them, and re-layouts: 26.3 us -> none  [the longest x3 18.1 us: flat_table(): jnp.concatenate([member.reshape(-1) for member in arrays])]
  transfers between devices with their start and end apart: 3 -> 48, of which waited for: 3 -> 24; matrix products, arithmetic and copies ran while one was open for 4% -> 8% of each run, Pallas kernels for 0% -> 11%
where the time goes in v1:
time: 252 us; the launch traced here: 251 us
  waiting for transfers between devices  92.9 us (37%)
  starting transfers between devices  54.1 us (21%)
  Pallas kernels  46.1 us (18%)
  other arithmetic  23.8 us (9%)
  local copies, waits for them, and re-layouts  17.4 us (7%)
  matrix products  14.7 us (6%)
    ppermute x48, waiting for transfers between devices, across(): lax.ppermute(block, 'dp', [(i, i ^ 1 << bit) for i in range(devices)])  92.9 us
    ppermute x48, starting transfers between devices, across(): lax.ppermute(block, 'dp', [(i, i ^ 1 << bit) for i in range(devices)])  54.1 us
    pallas_call x2, Pallas kernels, grad_blocks(): pl.pallas_call(functools.partial(grads_kernel, plan, sizes, tails is not...  28.6 us
    pallas_call x2, Pallas kernels, unpack_matrices(): pl.pallas_call(functools.partial(unpack_kernel, plan, sizes, tail_rows, l...  17.5 us
    unnamed x146, local copies, waits for them, and re-layouts  14.9 us
    dot_general x7, matrix products, times_transposed(): lax.dot_general(rows_in, matrix, (((1,), (1,)), ((), ())), preferred_elem...  6.96 us
    concatenate x9, other arithmetic, gather_chunk(): held = jnp.concatenate([held, across(held, bit, devices)])  5.27 us
  transfers between devices with their start and end apart: 48, of which 24 were waited for; matrix products, arithmetic and copies ran while one was open for 8% of the time, Pallas kernels for 11%

profile of v1, /device:TPU:0, one launch (start us, length us, event | category | flops | bytes accessed | tf_op | source)
XLA Modules:
  0.0 251.0 jit_solution(7426683205540239672)
XLA Ops:
  2.5 3.0 %collective-permute-start = (bf16[1,416,128]{2,1,0:T(8,128)(2,1)S(1)}, bf16[1,416,128]{2,1,0:T(8,128)(2,1)S(1)}, u32[]{:S(2)}, u32[]{:S(2)}) collective-permute-start(bf16[1,416,128]{2,1,0:T(8,128)(2,1)S(1)} %bitcast.154), channel_id=1, source_target_pairs={{0,8},{1,9},{2,10},{3,11},{4,12},{5,13},{6,14},{7,15},{8,0},{9,1},... | collective-permute-start | bytes 319496 | tf_op jit(solution)/shard_map/ppermute | solution.py:157
  5.5 2.7 %collective-permute-start.6 = (bf16[1,480,128]{2,1,0:T(8,128)(2,1)S(1)}, bf16[1,480,128]{2,1,0:T(8,128)(2,1)S(1)}, u32[]{:S(2)}, u32[]{:S(2)}) collective-permute-start(bf16[1,480,128]{2,1,0:T(8,128)(2,1)S(1)} %get-tuple-element.106), channel_id=1, source_target_pairs={{0,16},{1,17},{2,18},{3,19},{4,20},{5,21},{6,22},{7,23},{8,24},{9,... | collective-permute-start | bytes 368648 | tf_op jit(solution)/shard_map/ppermute | solution.py:157
  8.5 4.0 %collective-permute-start.1 = (bf16[2,416,128]{2,1,0:T(8,128)(2,1)S(1)}, bf16[2,416,128]{2,1,0:T(8,128)(2,1)S(1)}, u32[]{:S(2)}, u32[]{:S(2)}) collective-permute-start(bf16[2,416,128]{2,1,0:T(8,128)(2,1)S(1)} %pad_maximum_fusion.9), channel_id=1, source_target_pairs={{0,16},{1,17},{2,18},{3,19},{4,20},{5,21},{6,22},{7,23},{8,24},{9,... | collective-permute-start | bytes 638984 | tf_op jit(solution)/shard_map/ppermute | solution.py:157
  12.5 9.4 %collective-permute-done.6 = bf16[1,480,128]{2,1,0:T(8,128)(2,1)S(1)} collective-permute-done((bf16[1,480,128]{2,1,0:T(8,128)(2,1)S(1)}, bf16[1,480,128]{2,1,0:T(8,128)(2,1)S(1)}, u32[]{:S(2)}, u32[]{:S(2)}) %collective-permute-start.6) | collective-permute-done | bytes 122912 | tf_op jit(solution)/shard_map/ppermute | solution.py:157
  23.7 2.8 %collective-permute-done.1 = bf16[2,416,128]{2,1,0:T(8,128)(2,1)S(1)} collective-permute-done((bf16[2,416,128]{2,1,0:T(8,128)(2,1)S(1)}, bf16[2,416,128]{2,1,0:T(8,128)(2,1)S(1)}, u32[]{:S(2)}, u32[]{:S(2)}) %collective-permute-start.1) | collective-permute-done | bytes 213024 | tf_op jit(solution)/shard_map/ppermute | solution.py:157
  31.6 5.7 %collective-permute-done.13 = bf16[2,480,128]{2,1,0:T(8,128)(2,1)S(1)} collective-permute-done((bf16[2,480,128]{2,1,0:T(8,128)(2,1)S(1)}, bf16[2,480,128]{2,1,0:T(8,128)(2,1)S(1)}, u32[]{:S(2)}, u32[]{:S(2)}) %collective-permute-start.13) | collective-permute-done | bytes 245792 | tf_op jit(solution)/shard_map/ppermute | solution.py:157
  39.5 8.4 %collective-permute-done.8 = bf16[4,480,128]{2,1,0:T(8,128)(2,1)} collective-permute-done((bf16[4,480,128]{2,1,0:T(8,128)(2,1)}, bf16[4,480,128]{2,1,0:T(8,128)(2,1)}, u32[]{:S(2)}, u32[]{:S(2)}) %collective-permute-start.8) | collective-permute-done | bytes 491552 | tf_op jit(solution)/shard_map/ppermute | solution.py:157
  53.6 10.7 %collective-permute-done.3.refs_1_ = bf16[8,416,128]{2,1,0:T(8,128)(2,1)S(1)} collective-permute-done((bf16[8,416,128]{2,1,0:T(8,128)(2,1)S(1)}, bf16[8,416,128]{2,1,0:T(8,128)(2,1)S(1)}, u32[]{:S(2)}, u32[]{:S(2)}) %collective-permute-start.3) | collective-permute-done | bytes 852000 | tf_op jit(solution)/shard_map/ppermute | solution.py:157
  77.1 7.0 %shard_map.118 = (bf16[640,1024]{1,0:T(8,128)(2,1)S(1)}, bf16[640,256]{1,0:T(8,128)(2,1)S(1)}, bf16[640,256]{1,0:T(8,128)(2,1)S(1)}, bf16[1024,640]{1,0:T(8,128)(2,1)S(1)}, bf16[32,16,128]{2,1,0:T(8,128)(2,1)S(1)}) custom-call(s32[1]{0:T(128)} %bitcast.1.device_ref, bf16[8,416,128]{2,1,0:T(8,128)(2,1)S(1)} %pad_maximum_fusion.2.refs_0_, ...), custom_call_target="tpu_custom_call" | custom-call | bytes 6553600 | tf_op jit(solution)/shard_map/pallas_call | solution.py:249
  94.3 10.6 %shard_map.119 = (bf16[640,2048]{1,0:T(8,128)(2,1)S(1)}, bf16[640,2048]{1,0:T(8,128)(2,1)S(1)}, bf16[2048,640]{1,0:T(8,128)(2,1)}) custom-call(s32[1]{0:T(128)} %bitcast.1.device_ref, bf16[8,480,128]{2,1,0:T(8,128)(2,1)} %pad_maximum_fusion.refs_0_, bf16[8,480,128]{2,1,0:T(8,128)(2,1)} %collective-permute-done.9.refs_1_, ...), custom_call_target="tpu_custom_call" | custom-call | bytes 15728640 | tf_op jit(solution)/shard_map/pallas_call | solution.py:249
  127.6 9.2 %shard_map.120 = (bf16[16,144,128]{2,1,0:T(8,128)(2,1)S(1)}, bf16[16,144,128]{2,1,0:T(8,128)(2,1)S(1)}, bf16[16,144,128]{2,1,0:T(8,128)(2,1)S(1)}, bf16[16,144,1...) custom-call(s32[1]{0:T(128)} %bitcast.1.device_ref, ...), custom_call_target="tpu_custom_call" | custom-call | flops 419430400 | bytes 6553600 | tf_op jit(solution)/shard_map/pallas_call | solution.py:324
  138.4 19.4 %shard_map.121 = (bf16[16,320,128]{2,1,0:T(8,128)(2,1)S(1)}, bf16[16,320,128]{2,1,0:T(8,128)(2,1)S(1)}, bf16[16,320,128]{2,1,0:T(8,128)(2,1)S(1)}, bf16[16,320,1...) custom-call(s32[1]{0:T(128)} %bitcast.1.device_ref, ...), custom_call_target="tpu_custom_call" | custom-call | flops 1006632960 | bytes 15728640 | tf_op jit(solution)/shard_map/pallas_call | solution.py:324
  161.2 2.5 collective-permute-done.18
  164.0 3.5 %collective-permute-done.29 = bf16[8,128,128]{2,1,0:T(8,128)(2,1)S(1)} collective-permute-done((bf16[8,128,128]{2,1,0:T(8,128)(2,1)S(1)}, bf16[8,128,128]{2,1,0:T(8,128)(2,1)S(1)}, u32[]{:S(2)}, u32[]{:S(2)}) %collective-permute-start.29) | collective-permute-done | bytes 262176 | tf_op jit(solution)/shard_map/ppermute | solution.py:157
  169.8 8.6 %collective-permute-done.30 = bf16[4,128,128]{2,1,0:T(8,128)(2,1)S(1)} collective-permute-done((bf16[4,128,128]{2,1,0:T(8,128)(2,1)S(1)}, bf16[4,128,128]{2,1,0:T(8,128)(2,1)S(1)}, u32[]{:S(2)}, u32[]{:S(2)}) %collective-permute-start.30) | collective-permute-done | bytes 131104 | tf_op jit(solution)/shard_map/ppermute | solution.py:157
  180.7 6.4 %collective-permute-done.31 = bf16[2,128,128]{2,1,0:T(8,128)(2,1)S(1)} collective-permute-done((bf16[2,128,128]{2,1,0:T(8,128)(2,1)S(1)}, bf16[2,128,128]{2,1,0:T(8,128)(2,1)S(1)}, u32[]{:S(2)}, u32[]{:S(2)}) %collective-permute-start.31) | collective-permute-done | bytes 65568 | tf_op jit(solution)/shard_map/ppermute | solution.py:157
  189.6 4.1 %collective-permute-done.32 = bf16[1,128,128]{2,1,0:T(8,128)(2,1)S(1)} collective-permute-done((bf16[1,128,128]{2,1,0:T(8,128)(2,1)S(1)}, bf16[1,128,128]{2,1,0:T(8,128)(2,1)S(1)}, u32[]{:S(2)}, u32[]{:S(2)}) %collective-permute-start.32) | collective-permute-done | bytes 32800 | tf_op jit(solution)/shard_map/ppermute | solution.py:157
  196.6 2.7 %collective-permute-done.25 = bf16[4,144,128]{2,1,0:T(8,128)(2,1)S(1)} collective-permute-done((bf16[4,144,128]{2,1,0:T(8,128)(2,1)S(1)}, bf16[4,144,128]{2,1,0:T(8,128)(2,1)S(1)}, u32[]{:S(2)}, u32[]{:S(2)}) %collective-permute-start.25) | collective-permute-done | bytes 147488 | tf_op jit(solution)/shard_map/ppermute | solution.py:157
  205.3 3.5 %collective-permute-done.27 = bf16[1,144,128]{2,1,0:T(8,128)(2,1)S(1)} collective-permute-done((bf16[1,144,128]{2,1,0:T(8,128)(2,1)S(1)}, bf16[1,144,128]{2,1,0:T(8,128)(2,1)S(1)}, u32[]{:S(2)}, u32[]{:S(2)}) %collective-permute-start.27) | collective-permute-done | bytes 36896 | tf_op jit(solution)/shard_map/ppermute | solution.py:157
  214.6 8.1 %collective-permute-done.34 = bf16[8,320,128]{2,1,0:T(8,128)(2,1)S(1)} collective-permute-done((bf16[8,320,128]{2,1,0:T(8,128)(2,1)S(1)}, bf16[8,320,128]{2,1,0:T(8,128)(2,1)S(1)}, u32[]{:S(2)}, u32[]{:S(2)}) %collective-permute-start.34) | collective-permute-done | bytes 655392 | tf_op jit(solution)/shard_map/ppermute | solution.py:157
  228.6 2.9 %collective-permute-done.35 = bf16[4,320,128]{2,1,0:T(8,128)(2,1)S(1)} collective-permute-done((bf16[4,320,128]{2,1,0:T(8,128)(2,1)S(1)}, bf16[4,320,128]{2,1,0:T(8,128)(2,1)S(1)}, u32[]{:S(2)}, u32[]{:S(2)}) %collective-permute-start.35) | collective-permute-done | bytes 327712 | tf_op jit(solution)/shard_map/ppermute | solution.py:157
  236.0 4.1 %collective-permute-start.46 = (bf16[2,320,128]{2,1,0:T(8,128)(2,1)S(1)}, bf16[2,320,128]{2,1,0:T(8,128)(2,1)S(1)}, u32[]{:S(2)}, u32[]{:S(2)}) collective-permute-start(bf16[2,320,128]{2,1,0:T(8,128)(2,1)S(1)} %get-tuple-element.94), channel_id=1, source_target_pairs={{0,4},{1,5},{2,6},{3,7},{4,0},{5,1},{6,2},{7,3},{8,12},{9,13},{10,... | collective-permute-start | bytes 491528 | tf_op jit(solution)/shard_map/ppermute | solution.py:157
  240.3 2.5 %collective-permute-start.42 = (bf16[1,320,128]{2,1,0:T(8,128)(2,1)S(1)}, bf16[1,320,128]{2,1,0:T(8,128)(2,1)S(1)}, u32[]{:S(2)}, u32[]{:S(2)}) collective-permute-start(bf16[1,320,128]{2,1,0:T(8,128)(2,1)S(1)} %add_convert_fusion.33), channel_id=1, source_target_pairs={{0,16},{1,17},{2,18},{3,19},{4,20},{5,21},{6,22},{7,23},{8,24},{9,... | collective-permute-start | bytes 245768 | tf_op jit(solution)/shard_map/ppermute | solution.py:157
  245.7 3.5 %collective-permute-done.47 = bf16[1,320,128]{2,1,0:T(8,128)(2,1)S(1)} collective-permute-done((bf16[1,320,128]{2,1,0:T(8,128)(2,1)S(1)}, bf16[1,320,128]{2,1,0:T(8,128)(2,1)S(1)}, u32[]{:S(2)}, u32[]{:S(2)}) %collective-permute-start.47) | collective-permute-done | bytes 81952 | tf_op jit(solution)/shard_map/ppermute | solution.py:157
  (350 shorter events, 103.8 us)
Async XLA Ops:
  5.5 16.4 %collective-permute-start.6 = (bf16[1,480,128]{2,1,0:T(8,128)(2,1)S(1)}, bf16[1,480,128]{2,1,0:T(8,128)(2,1)S(1)}, u32[]{:S(2)}, u32[]{:S(2)}) collective-permute-start(bf16[1,480,128]{2,1,0:T(8,128)(2,1)S(1)} %get-tuple-element.106), channel_id=1, source_target_pairs={{0,16},{1,17},{2,18},{3,19},{4,20},{5,21},{6,22},{7,23},{8,24},{9,... | collective-permute-start | bytes 368648 | tf_op jit(solution)/shard_map/ppermute | solution.py:157
  8.5 18.0 %collective-permute-start.1 = (bf16[2,416,128]{2,1,0:T(8,128)(2,1)S(1)}, bf16[2,416,128]{2,1,0:T(8,128)(2,1)S(1)}, u32[]{:S(2)}, u32[]{:S(2)}) collective-permute-start(bf16[2,416,128]{2,1,0:T(8,128)(2,1)S(1)} %pad_maximum_fusion.9), channel_id=1, source_target_pairs={{0,16},{1,17},{2,18},{3,19},{4,20},{5,21},{6,22},{7,23},{8,24},{9,... | collective-permute-start | bytes 638984 | tf_op jit(solution)/shard_map/ppermute | solution.py:157
  12.5 15.8 %collective-permute-start.12 = (bf16[1,480,128]{2,1,0:T(8,128)(2,1)S(1)}, bf16[1,480,128]{2,1,0:T(8,128)(2,1)S(1)}, u32[]{:S(2)}, u32[]{:S(2)}) collective-permute-start(bf16[1,480,128]{2,1,0:T(8,128)(2,1)S(1)} %get-tuple-element.105), channel_id=1, source_target_pairs={{0,16},{1,17},{2,18},{3,19},{4,20},{5,21},{6,22},{7,23},{8,24},{9,... | collective-permute-start | bytes 368648 | tf_op jit(solution)/shard_map/ppermute | solution.py:157
  26.5 10.9 %collective-permute-start.2 = (bf16[4,416,128]{2,1,0:T(8,128)(2,1)S(1)}, bf16[4,416,128]{2,1,0:T(8,128)(2,1)S(1)}, u32[]{:S(2)}, u32[]{:S(2)}) collective-permute-start(bf16[4,416,128]{2,1,0:T(8,128)(2,1)S(1)} %pad_maximum_fusion.6), channel_id=1, source_target_pairs={{0,2},{1,3},{2,0},{3,1},{4,6},{5,7},{6,4},{7,5},{8,10},{9,11},{10,... | collective-permute-start | bytes 1277960 | tf_op jit(solution)/shard_map/ppermute | solution.py:157
  30.8 17.2 %collective-permute-start.8 = (bf16[4,480,128]{2,1,0:T(8,128)(2,1)}, bf16[4,480,128]{2,1,0:T(8,128)(2,1)}, u32[]{:S(2)}, u32[]{:S(2)}) collective-permute-start(bf16[4,480,128]{2,1,0:T(8,128)(2,1)} %pad_maximum_fusion.4), channel_id=1, source_target_pairs={{0,4},{1,5},{2,6},{3,7},{4,0},{5,1},{6,2},{7,3},{8,12},{9,13},{10,... | collective-permute-start | bytes 1474568 | tf_op jit(solution)/shard_map/ppermute | solution.py:157
  37.3 12.7 %collective-permute-start.14 = (bf16[4,480,128]{2,1,0:T(8,128)(2,1)S(1)}, bf16[4,480,128]{2,1,0:T(8,128)(2,1)}, u32[]{:S(2)}, u32[]{:S(2)}) collective-permute-start(bf16[4,480,128]{2,1,0:T(8,128)(2,1)S(1)} %pad_maximum_fusion.5), channel_id=1, source_target_pairs={{0,8},{1,9},{2,10},{3,11},{4,12},{5,13},{6,14},{7,15},{8,0},{9,1},... | collective-permute-start | bytes 1474568 | tf_op jit(solution)/shard_map/ppermute | solution.py:157
  37.5 26.8 %collective-permute-start.3 = (bf16[8,416,128]{2,1,0:T(8,128)(2,1)S(1)}, bf16[8,416,128]{2,1,0:T(8,128)(2,1)S(1)}, u32[]{:S(2)}, u32[]{:S(2)}) collective-permute-start(bf16[8,416,128]{2,1,0:T(8,128)(2,1)S(1)} %pad_maximum_fusion.2.refs_0_), channel_id=1, source_target_pairs={{0,4},{1,5},{2,6},{3,7},{4,0},{5,1},{6,2},{7,3},{8,12},{9,13},{10,... | collective-permute-start | bytes 2555912 | tf_op jit(solution)/shard_map/ppermute | solution.py:157
  50.0 20.6 %collective-permute-start.9 = (bf16[8,480,128]{2,1,0:T(8,128)(2,1)}, bf16[8,480,128]{2,1,0:T(8,128)(2,1)}, u32[]{:S(2)}, u32[]{:S(2)}) collective-permute-start(bf16[8,480,128]{2,1,0:T(8,128)(2,1)} %pad_maximum_fusion.refs_0_), channel_id=1, source_target_pairs={{0,8},{1,9},{2,10},{3,11},{4,12},{5,13},{6,14},{7,15},{8,0},{9,1},... | collective-permute-start | bytes 2949128 | tf_op jit(solution)/shard_map/ppermute | solution.py:157
  52.1 20.6 %collective-permute-start.15 = (bf16[8,480,128]{2,1,0:T(8,128)(2,1)}, bf16[8,480,128]{2,1,0:T(8,128)(2,1)}, u32[]{:S(2)}, u32[]{:S(2)}) collective-permute-start(bf16[8,480,128]{2,1,0:T(8,128)(2,1)} %pad_maximum_fusion.1.refs_4_), channel_id=1, source_target_pairs={{0,2},{1,3},{2,0},{3,1},{4,6},{5,7},{6,4},{7,5},{8,10},{9,11},{10,... | collective-permute-start | bytes 2949128 | tf_op jit(solution)/shard_map/ppermute | solution.py:157
  53.6 15.7 %collective-permute-start.4 = (bf16[8,416,128]{2,1,0:T(8,128)(2,1)S(1)}, bf16[8,416,128]{2,1,0:T(8,128)(2,1)S(1)}, u32[]{:S(2)}, u32[]{:S(2)}) collective-permute-start(bf16[8,416,128]{2,1,0:T(8,128)(2,1)S(1)} %pad_maximum_fusion.2.refs_0_), channel_id=1, source_target_pairs={{0,1},{1,0},{2,3},{3,2},{4,5},{5,4},{6,7},{7,6},{8,9},{9,8},{10,11... | collective-permute-start | bytes 2555912 | tf_op jit(solution)/shard_map/ppermute | solution.py:157
  68.8 25.5 %collective-permute-start.10 = (bf16[8,480,128]{2,1,0:T(8,128)(2,1)}, bf16[8,480,128]{2,1,0:T(8,128)(2,1)}, u32[]{:S(2)}, u32[]{:S(2)}) collective-permute-start(bf16[8,480,128]{2,1,0:T(8,128)(2,1)} %pad_maximum_fusion.refs_0_), channel_id=1, source_target_pairs={{0,1},{1,0},{2,3},{3,2},{4,5},{5,4},{6,7},{7,6},{8,9},{9,8},{10,11... | collective-permute-start | bytes 2949128 | tf_op jit(solution)/shard_map/ppermute | solution.py:157
  70.2 24.0 %collective-permute-start.16 = (bf16[8,480,128]{2,1,0:T(8,128)(2,1)}, bf16[8,480,128]{2,1,0:T(8,128)(2,1)}, u32[]{:S(2)}, u32[]{:S(2)}) collective-permute-start(bf16[8,480,128]{2,1,0:T(8,128)(2,1)} %pad_maximum_fusion.1.refs_4_), channel_id=1, source_target_pairs={{0,1},{1,0},{2,3},{3,2},{4,5},{5,4},{6,7},{7,6},{8,9},{9,8},{10,11... | collective-permute-start | bytes 2949128 | tf_op jit(solution)/shard_map/ppermute | solution.py:157
  70.6 23.6 %collective-permute-start.11 = (bf16[8,480,128]{2,1,0:T(8,128)(2,1)}, bf16[8,480,128]{2,1,0:T(8,128)(2,1)}, u32[]{:S(2)}, u32[]{:S(2)}) collective-permute-start(bf16[8,480,128]{2,1,0:T(8,128)(2,1)} %collective-permute-done.9.refs_1_), channel_id=1, source_target_pairs={{0,1},{1,0},{2,3},{3,2},{4,5},{5,4},{6,7},{7,6},{8,9},{9,8},{10,11... | collective-permute-start | bytes 2949128 | tf_op jit(solution)/shard_map/ppermute | solution.py:157
  72.7 21.5 %collective-permute-start.17 = (bf16[8,480,128]{2,1,0:T(8,128)(2,1)}, bf16[8,480,128]{2,1,0:T(8,128)(2,1)}, u32[]{:S(2)}, u32[]{:S(2)}) collective-permute-start(bf16[8,480,128]{2,1,0:T(8,128)(2,1)} %collective-permute-done.15.refs_5_), channel_id=1, source_target_pairs={{0,1},{1,0},{2,3},{3,2},{4,5},{5,4},{6,7},{7,6},{8,9},{9,8},{10,11... | collective-permute-start | bytes 2949128 | tf_op jit(solution)/shard_map/ppermute | solution.py:157
  136.8 22.2 %collective-permute-start.28 = (bf16[16,128,128]{2,1,0:T(8,128)(2,1)S(1)}, bf16[16,128,128]{2,1,0:T(8,128)(2,1)S(1)}, u32[]{:S(2)}, u32[]{:S(2)}) collective-permute-start(bf16[16,128,128]{2,1,0:T(8,128)(2,1)S(1)} %get-tuple-element.39), channel_id=1, source_target_pairs={{0,1},{1,0},{2,3},{3,2},{4,5},{5,4},{6,7},{7,6},{8,9},{9,8},{10,11... | collective-permute-start | bytes 1572872 | tf_op jit(solution)/shard_map/ppermute | solution.py:157
  157.9 51.0 %collective-permute-start.33 = (bf16[16,320,128]{2,1,0:T(8,128)(2,1)S(1)}, bf16[16,320,128]{2,1,0:T(8,128)(2,1)S(1)}, u32[]{:S(2)}, u32[]{:S(2)}) collective-permute-start(bf16[16,320,128]{2,1,0:T(8,128)(2,1)S(1)} %get-tuple-element.41), channel_id=1, source_target_pairs={{0,1},{1,0},{2,3},{3,2},{4,5},{5,4},{6,7},{7,6},{8,9},{9,8},{10,11... | collective-permute-start | bytes 3932168 | tf_op jit(solution)/shard_map/ppermute | solution.py:157
  158.0 52.4 %collective-permute-start.38 = (bf16[16,320,128]{2,1,0:T(8,128)(2,1)S(1)}, bf16[16,320,128]{2,1,0:T(8,128)(2,1)S(1)}, u32[]{:S(2)}, u32[]{:S(2)}) collective-permute-start(bf16[16,320,128]{2,1,0:T(8,128)(2,1)S(1)} %get-tuple-element.43), channel_id=1, source_target_pairs={{0,1},{1,0},{2,3},{3,2},{4,5},{5,4},{6,7},{7,6},{8,9},{9,8},{10,11... | collective-permute-start | bytes 3932168 | tf_op jit(solution)/shard_map/ppermute | solution.py:157
  158.5 10.2 %collective-permute-start.23 = (bf16[16,144,128]{2,1,0:T(8,128)(2,1)S(1)}, bf16[16,144,128]{2,1,0:T(8,128)(2,1)S(1)}, u32[]{:S(2)}, u32[]{:S(2)}) collective-permute-start(bf16[16,144,128]{2,1,0:T(8,128)(2,1)S(1)} %get-tuple-element.37), channel_id=1, source_target_pairs={{0,1},{1,0},{2,3},{3,2},{4,5},{5,4},{6,7},{7,6},{8,9},{9,8},{10,11... | collective-permute-start | bytes 1769480 | tf_op jit(solution)/shard_map/ppermute | solution.py:157
  163.7 48.8 %collective-permute-start.43 = (bf16[16,320,128]{2,1,0:T(8,128)(2,1)S(1)}, bf16[16,320,128]{2,1,0:T(8,128)(2,1)S(1)}, u32[]{:S(2)}, u32[]{:S(2)}) collective-permute-start(bf16[16,320,128]{2,1,0:T(8,128)(2,1)S(1)} %get-tuple-element.45), channel_id=1, source_target_pairs={{0,1},{1,0},{2,3},{3,2},{4,5},{5,4},{6,7},{7,6},{8,9},{9,8},{10,11... | collective-permute-start | bytes 3932168 | tf_op jit(solution)/shard_map/ppermute | solution.py:157
  167.5 12.7 %collective-permute-start.19 = (bf16[8,144,128]{2,1,0:T(8,128)(2,1)S(1)}, bf16[8,144,128]{2,1,0:T(8,128)(2,1)S(1)}, u32[]{:S(2)}, u32[]{:S(2)}) collective-permute-start(bf16[8,144,128]{2,1,0:T(8,128)(2,1)S(1)} %get-tuple-element.84), channel_id=1, source_target_pairs={{0,4},{1,5},{2,6},{3,7},{4,0},{5,1},{6,2},{7,3},{8,12},{9,13},{10,... | collective-permute-start | bytes 884744 | tf_op jit(solution)/shard_map/ppermute | solution.py:157
  178.4 10.4 %collective-permute-start.24 = (bf16[8,144,128]{2,1,0:T(8,128)(2,1)S(1)}, bf16[8,144,128]{2,1,0:T(8,128)(2,1)S(1)}, u32[]{:S(2)}, u32[]{:S(2)}) collective-permute-start(bf16[8,144,128]{2,1,0:T(8,128)(2,1)S(1)} %get-tuple-element.86), channel_id=1, source_target_pairs={{0,8},{1,9},{2,10},{3,11},{4,12},{5,13},{6,14},{7,15},{8,0},{9,1},... | collective-permute-start | bytes 884744 | tf_op jit(solution)/shard_map/ppermute | solution.py:157
  209.2 13.5 %collective-permute-start.34 = (bf16[8,320,128]{2,1,0:T(8,128)(2,1)S(1)}, bf16[8,320,128]{2,1,0:T(8,128)(2,1)S(1)}, u32[]{:S(2)}, u32[]{:S(2)}) collective-permute-start(bf16[8,320,128]{2,1,0:T(8,128)(2,1)S(1)} %get-tuple-element.70), channel_id=1, source_target_pairs={{0,4},{1,5},{2,6},{3,7},{4,0},{5,1},{6,2},{7,3},{8,12},{9,13},{10,... | collective-permute-start | bytes 1966088 | tf_op jit(solution)/shard_map/ppermute | solution.py:157
  210.8 15.9 %collective-permute-start.39 = (bf16[8,320,128]{2,1,0:T(8,128)(2,1)S(1)}, bf16[8,320,128]{2,1,0:T(8,128)(2,1)S(1)}, u32[]{:S(2)}, u32[]{:S(2)}) collective-permute-start(bf16[8,320,128]{2,1,0:T(8,128)(2,1)S(1)} %get-tuple-element.72), channel_id=1, source_target_pairs={{0,8},{1,9},{2,10},{3,11},{4,12},{5,13},{6,14},{7,15},{8,0},{9,1},... | collective-permute-start | bytes 1966088 | tf_op jit(solution)/shard_map/ppermute | solution.py:157
  212.8 14.1 %collective-permute-start.44 = (bf16[8,320,128]{2,1,0:T(8,128)(2,1)S(1)}, bf16[8,320,128]{2,1,0:T(8,128)(2,1)S(1)}, u32[]{:S(2)}, u32[]{:S(2)}) collective-permute-start(bf16[8,320,128]{2,1,0:T(8,128)(2,1)S(1)} %get-tuple-element.74), channel_id=1, source_target_pairs={{0,2},{1,3},{2,0},{3,1},{4,6},{5,7},{6,4},{7,5},{8,10},{9,11},{10,... | collective-permute-start | bytes 1966088 | tf_op jit(solution)/shard_map/ppermute | solution.py:157
  (93 other events, 373.3 us)

commit v2 on v1

--- a/solution.py
+++ b/solution.py
@@ -169,20 +169,31 @@
     return (held, last, across(held, 0, devices), across(last, 0, devices))
 
 
-def scatter_chunk(home, away, order, devices):
-    for bit in [0] + list(order):
-        came = across(away, bit, devices)
+def sent_blocks(chunks, orders, stage, devices):
+    return [
+        across(away, order[stage], devices)
+        for (_, away), order in zip(chunks, orders)
+    ]
+
+
+def merged_blocks(chunks, came):
+    merged = []
+    for (home, _), arrived in zip(chunks, came):
         half = home.shape[0] // 2
 
         def added(low, high):
-            total = home[low:high].astype(jnp.float32) + came[low:high].astype(jnp.float32)
-            return total.astype(jnp.bfloat16) if half else total
+            return home[low:high].astype(jnp.float32) + arrived[low:high].astype(jnp.float32)
 
         if half:
-            home, away = (added(0, half), added(half, 2 * half))
+            merged.append(
+                (
+                    added(0, half).astype(jnp.bfloat16),
+                    added(half, 2 * half).astype(jnp.bfloat16),
+                )
+            )
         else:
-            home = added(0, 1)
-    return home[0]
+            merged.append((added(0, 1)[0], None))
+    return merged
 
 
 def cut_rows(rows, parts):
@@ -257,9 +268,7 @@
             pltpu.SemaphoreType.DMA((len(plan),)),
         ],
         compiler_params=pltpu.CompilerParams(vmem_limit_bytes=40 << 20),
-        cost_estimate=pl.CostEstimate(
-            flops=0, bytes_accessed=flat_rows * LANES * 4, transcendentals=0
-        ),
+        cost_estimate=pl.CostEstimate(flops=0, bytes_accessed=0, transcendentals=0),
     )(device, *arrays)
 
 
@@ -332,11 +341,7 @@
             pltpu.SemaphoreType.DMA((len(plan),)),
         ],
         compiler_params=pltpu.CompilerParams(vmem_limit_bytes=40 << 20),
-        cost_estimate=pl.CostEstimate(
-            flops=2 * CAP * flat_rows * LANES,
-            bytes_accessed=flat_rows * LANES * 4,
-            transcendentals=0,
-        ),
+        cost_estimate=pl.CostEstimate(flops=0, bytes_accessed=0, transcendentals=0),
     )(device, *inputs)
 
 
@@ -374,24 +379,25 @@
     return sum(((device >> bit) & 1) << k for k, bit in enumerate(order))
 
 
-def scattered_rows(pairs, tails, orders, sizes, devices, device):
+def scatter_blocks(pairs, tails, orders, sizes, devices, device):
     each = sum(rows * columns for rows, columns in sizes) // LANES // devices
     tail_rows = 0 if tails is None else tails.shape[1]
-    parts = cut_rows(each + tail_rows, 3)
+    parts = cut_rows(each + tail_rows, len(orders))
     half = devices // 2
-    plan, shapes = [], []
+    plan = []
     for (low, high), order in zip(parts, orders):
-        order = list(order)[::-1]
         for with_core in (0, 1):
             for index in range(half):
-                offset = offset_of(index, order) ^ with_core
-                take = min(high, each) - low
-                plan.append((len(shapes), index, offset, 0, take, low, each))
-                if high > each:
-                    plan.append((len(shapes), index, offset, take, tail_rows, None, each))
-            shapes.append((half, high - low, LANES))
+                offset = offset_of(index, order[::-1]) ^ with_core
+                plan.append((with_core, index, offset, low, min(high, each) - low, low, each))
+    if tail_rows:
+        for with_core in (0, 1):
+            for index in range(half):
+                offset = offset_of(index, orders[len(parts) - 1][::-1]) ^ with_core
+                plan.append((with_core, index, offset, each, tail_rows, None, each))
+    shape = (half, each + tail_rows, LANES)
     if each % ROWS == 0 and parts[-1][0] < each:
-        blocks = grad_blocks(plan, sizes, pairs, tails, device, shapes)
+        blocks = grad_blocks(plan, sizes, pairs, tails, device, [shape, shape])
     else:
         flat = grad_blocks(
             [(0, 0, 0, 0, devices * each, 0, 0)],
@@ -404,18 +410,24 @@
         table = flat.reshape(devices, each, LANES)
         table = table if tails is None else jnp.concatenate([table, tails], axis=1)
         blocks = []
-        for (low, high), order in zip(parts, orders):
-            order = list(order)[::-1]
-            for with_core in (0, 1):
-                offsets = [offset_of(index, order) ^ with_core for index in range(half)]
+        for with_core in (0, 1):
+            chunks = []
+            for (low, high), order in zip(parts, orders):
+                offsets = [offset_of(index, order[::-1]) ^ with_core for index in range(half)]
                 owners = jnp.array(offsets, jnp.int32) ^ device[0]
-                blocks.append(jnp.take(table[:, low:high], owners, axis=0))
-    return jnp.concatenate(
-        [
-            scatter_chunk(blocks[2 * k], blocks[2 * k + 1], order, devices)
-            for k, order in enumerate(orders[: len(parts)])
-        ]
-    )
+                chunks.append(jnp.take(table[:, low:high], owners, axis=0))
+            blocks.append(jnp.concatenate(chunks, axis=1))
+    return blocks, parts
+
+
+def cores_merged(home, came, parts):
+    half = home.shape[0] // 2
+
+    def added(first, low, high):
+        at = (slice(first, first + half), slice(low, high))
+        return (home[at].astype(jnp.float32) + came[at].astype(jnp.float32)).astype(jnp.bfloat16)
+
+    return [(added(0, low, high), added(half, low, high)) for low, high in parts]
 
 
 def cut_gains(gain_flat):
@@ -503,7 +515,7 @@
     return (delta_mid, pairs, (gain_mid_grad, gain_last_grad))
 
 
-def attn_backward(delta_mid, weights, saved, allowed, cos_tab, sin_tab):
+def attn_backward(delta_mid, weights, saved, allowed, cos_tab, sin_tab, pause):
     query_weight, key_weight, value_weight, out_weight = weights[:4]
     gain_in, gain_query, gain_key, gain_post = weights[7][:4]
     (
@@ -522,6 +534,7 @@
     delta_attn, gain_post_grad = pullback(delta_mid)
     delta_attn = delta_attn.astype(jnp.bfloat16)
     delta_context = times_transposed(delta_attn, out_weight).astype(jnp.bfloat16)
+    delta_context, delta_attn = pause((delta_context, delta_attn))
     delta_query, delta_key, delta_value = attend_back(
         rot_query, rot_key, value_vec, allowed, log_total, context, delta_context
     )
@@ -591,18 +604,48 @@
     live_mask, allowed, cos_tab, sin_tab = slot_setup(seq_lengths, seq_owner, device)
     block_out, saved = forward_pass(hidden_in, weights, allowed, cos_tab, sin_tab)
     delta_mid, ffn_pairs, late_gains = ffn_backward(cotangent, live_mask, weights, saved)
-    orders = bit_orders(devices, ("yxba", "ayxb", "xayb"))
-    ffn_shard = scattered_rows(ffn_pairs, None, orders, FFN_SIZES, devices, here)
+    ffn_orders = bit_orders(devices, ("xaby", "yxab", "ayxb"))
+    attn_orders = bit_orders(devices, ("xyab", "yxba"))[:2]
+    (ffn_home, ffn_away), ffn_parts = scatter_blocks(
+        ffn_pairs, None, ffn_orders, FFN_SIZES, devices, here
+    )
+    delta_mid, ffn_home, ffn_away = lax.optimization_barrier((delta_mid, ffn_home, ffn_away))
+    ffn_came = across(ffn_away, 0, devices)
+    ffn_chunks = []
+
+    def pause(values):
+        nonlocal ffn_chunks, ffn_came
+        values, ffn_came = lax.optimization_barrier((values, ffn_came))
+        ffn_chunks = cores_merged(ffn_home, ffn_came, ffn_parts)
+        values, ffn_chunks = lax.optimization_barrier((values, ffn_chunks))
+        ffn_came = sent_blocks(ffn_chunks, ffn_orders, 0, devices)
+        return values
+
     grad_in, attn_pairs, early_gains = attn_backward(
-        delta_mid, weights, saved, allowed, cos_tab, sin_tab
+        delta_mid, weights, saved, allowed, cos_tab, sin_tab, pause
     )
     gain_table = jnp.concatenate(early_gains + late_gains).reshape(devices, gain_len)
     gain_table = jnp.pad(gain_table.astype(jnp.bfloat16), ((0, 0), (0, pad)))
     gain_table = gain_table.reshape(devices, tail_rows, LANES)
-    orders = bit_orders(devices, ("yabx", "axyb", "xyab"))
-    attn_shard = scattered_rows(
-        attn_pairs, gain_table, orders, ATTN_SIZES, devices, here
-    ).reshape(-1)
+    (attn_home, attn_away), attn_parts = scatter_blocks(
+        attn_pairs, gain_table, attn_orders, ATTN_SIZES, devices, here
+    )
+    attn_home, attn_away, ffn_came = lax.optimization_barrier((attn_home, attn_away, ffn_came))
+    stages = len(ffn_orders[0])
+    ffn_chunks = merged_blocks(ffn_chunks, ffn_came)
+    ffn_came = sent_blocks(ffn_chunks, ffn_orders, 1, devices)
+    attn_came = across(attn_away, 0, devices)
+    attn_came, ffn_came = lax.optimization_barrier((attn_came, ffn_came))
+    attn_chunks = cores_merged(attn_home, attn_came, attn_parts)
+    for stage in range(stages):
+        attn_came = sent_blocks(attn_chunks, attn_orders, stage, devices)
+        if stage < stages - 1:
+            ffn_chunks = merged_blocks(ffn_chunks, ffn_came)
+        ffn_came = sent_blocks(ffn_chunks, ffn_orders, stage + 2, devices) if stage + 2 < stages else []
+        ffn_came, attn_came = lax.optimization_barrier((ffn_came, attn_came))
+        attn_chunks = merged_blocks(attn_chunks, attn_came)
+    attn_shard = jnp.concatenate([rows for rows, _ in attn_chunks]).reshape(-1)
+    ffn_shard = jnp.concatenate([rows for rows, _ in ffn_chunks])
     grad_shard = jnp.concatenate(
         [attn_shard[:attn_len], ffn_shard.reshape(-1), attn_shard[attn_len : attn_len + gain_len]]
     )

time: 252 us -> 218 us (0.87)
  waiting for transfers between devices: 92.9 us -> 73.2 us
  other arithmetic: 23.8 us -> 34.2 us
  local copies, waits for them, and re-layouts: 17.4 us -> 8.77 us
  starting transfers between devices: 54.1 us -> 46.4 us
  Pallas kernels: 46.1 us -> 40.4 us
    ppermute x48 -> x40, waiting for transfers between devices: 92.9 us -> 73.2 us  [across(): lax.ppermute(block, 'dp', [(i, i ^ 1 << bit) for i in range(devices)])]
    convert_element_type x24 -> x17, other arithmetic: 2.75 us -> 11 us  [the longest x2 6.53 us: added(): (home[at].astype(jnp.float32) + came[at].astype(jnp.float32)).astype(jnp....]
    ppermute x48 -> x40, starting transfers between devices: 54.1 us -> 46.4 us  [across(): lax.ppermute(block, 'dp', [(i, i ^ 1 << bit) for i in range(devices)])]
    unnamed x146 -> x162, local copies, waits for them, and re-layouts: 14.9 us -> 7.26 us
    pallas_call x2, Pallas kernels: 28.6 us -> 22.9 us  [grad_blocks(): pl.pallas_call(functools.partial(grads_kernel, plan, sizes, tails is not...]
  transfers between devices with their start and end apart: 48 -> 40, of which waited for: 24 -> 24; matrix products, arithmetic and copies ran while one was open for 8% -> 12% of each run, Pallas kernels for 11% -> 7%
where the time goes in v2:
time: 218 us; the launch traced here: 217 us
  waiting for transfers between devices  73.2 us (34%)
  starting transfers between devices  46.4 us (21%)
  Pallas kernels  40.4 us (19%)
  other arithmetic  34.2 us (16%)
  matrix products  12.3 us (6%)
  local copies, waits for them, and re-layouts  8.77 us (4%)
    ppermute x40, waiting for transfers between devices, across(): lax.ppermute(block, 'dp', [(i, i ^ 1 << bit) for i in range(devices)])  73.2 us
    ppermute x40, starting transfers between devices, across(): lax.ppermute(block, 'dp', [(i, i ^ 1 << bit) for i in range(devices)])  46.4 us
    pallas_call x2, Pallas kernels, grad_blocks(): pl.pallas_call(functools.partial(grads_kernel, plan, sizes, tails is not...  22.9 us
    pallas_call x2, Pallas kernels, unpack_matrices(): pl.pallas_call(functools.partial(unpack_kernel, plan, sizes, tail_rows, l...  17.5 us
    unnamed x162, local copies, waits for them, and re-layouts  7.26 us
    dot_general x7, matrix products, times_transposed(): lax.dot_general(rows_in, matrix, (((1,), (1,)), ((), ())), preferred_elem...  6.55 us
    convert_element_type x2, other arithmetic, added(): (home[at].astype(jnp.float32) + came[at].astype(jnp.float32)).astype(jnp....  6.53 us
    concatenate x9, other arithmetic, gather_chunk(): held = jnp.concatenate([held, across(held, bit, devices)])  5.31 us
  transfers between devices with their start and end apart: 40, of which 24 were waited for; matrix products, arithmetic and copies ran while one was open for 12% of the time, Pallas kernels for 7%

profile of v2, /device:TPU:0, one launch (start us, length us, event | category | flops | bytes accessed | tf_op | source)
XLA Modules:
  0.0 217.3 jit_solution(9143005913608812640)
XLA Ops:
  2.5 3.0 %collective-permute-start = (bf16[1,416,128]{2,1,0:T(8,128)(2,1)S(1)}, bf16[1,416,128]{2,1,0:T(8,128)(2,1)S(1)}, u32[]{:S(2)}, u32[]{:S(2)}) collective-permute-start(bf16[1,416,128]{2,1,0:T(8,128)(2,1)S(1)} %bitcast.152), channel_id=1, source_target_pairs={{0,8},{1,9},{2,10},{3,11},{4,12},{5,13},{6,14},{7,15},{8,0},{9,1},... | collective-permute-start | bytes 319496 | tf_op jit(solution)/shard_map/ppermute | solution.py:157
  5.5 2.7 %collective-permute-start.6 = (bf16[1,480,128]{2,1,0:T(8,128)(2,1)S(1)}, bf16[1,480,128]{2,1,0:T(8,128)(2,1)S(1)}, u32[]{:S(2)}, u32[]{:S(2)}) collective-permute-start(bf16[1,480,128]{2,1,0:T(8,128)(2,1)S(1)} %get-tuple-element.163), channel_id=1, source_target_pairs={{0,16},{1,17},{2,18},{3,19},{4,20},{5,21},{6,22},{7,23},{8,24},{9,... | collective-permute-start | bytes 368648 | tf_op jit(solution)/shard_map/ppermute | solution.py:157
  8.5 4.0 %collective-permute-start.1 = (bf16[2,416,128]{2,1,0:T(8,128)(2,1)S(1)}, bf16[2,416,128]{2,1,0:T(8,128)(2,1)S(1)}, u32[]{:S(2)}, u32[]{:S(2)}) collective-permute-start(bf16[2,416,128]{2,1,0:T(8,128)(2,1)S(1)} %pad_maximum_fusion.10), channel_id=1, source_target_pairs={{0,16},{1,17},{2,18},{3,19},{4,20},{5,21},{6,22},{7,23},{8,24},{9,... | collective-permute-start | bytes 638984 | tf_op jit(solution)/shard_map/ppermute | solution.py:157
  12.5 9.4 %collective-permute-done.6 = bf16[1,480,128]{2,1,0:T(8,128)(2,1)S(1)} collective-permute-done((bf16[1,480,128]{2,1,0:T(8,128)(2,1)S(1)}, bf16[1,480,128]{2,1,0:T(8,128)(2,1)S(1)}, u32[]{:S(2)}, u32[]{:S(2)}) %collective-permute-start.6) | collective-permute-done | bytes 122912 | tf_op jit(solution)/shard_map/ppermute | solution.py:157
  23.7 2.8 %collective-permute-done.1 = bf16[2,416,128]{2,1,0:T(8,128)(2,1)S(1)} collective-permute-done((bf16[2,416,128]{2,1,0:T(8,128)(2,1)S(1)}, bf16[2,416,128]{2,1,0:T(8,128)(2,1)S(1)}, u32[]{:S(2)}, u32[]{:S(2)}) %collective-permute-start.1) | collective-permute-done | bytes 213024 | tf_op jit(solution)/shard_map/ppermute | solution.py:157
  31.6 5.7 %collective-permute-done.13 = bf16[2,480,128]{2,1,0:T(8,128)(2,1)S(1)} collective-permute-done((bf16[2,480,128]{2,1,0:T(8,128)(2,1)S(1)}, bf16[2,480,128]{2,1,0:T(8,128)(2,1)S(1)}, u32[]{:S(2)}, u32[]{:S(2)}) %collective-permute-start.13) | collective-permute-done | bytes 245792 | tf_op jit(solution)/shard_map/ppermute | solution.py:157
  39.5 8.4 %collective-permute-done.8 = bf16[4,480,128]{2,1,0:T(8,128)(2,1)} collective-permute-done((bf16[4,480,128]{2,1,0:T(8,128)(2,1)}, bf16[4,480,128]{2,1,0:T(8,128)(2,1)}, u32[]{:S(2)}, u32[]{:S(2)}) %collective-permute-start.8) | collective-permute-done | bytes 491552 | tf_op jit(solution)/shard_map/ppermute | solution.py:157
  47.9 2.1 pad_maximum_fusion.refs_0_
  50.0 2.1 pad_maximum_fusion.1.refs_4_
  53.7 10.7 %collective-permute-done.3.refs_1_ = bf16[8,416,128]{2,1,0:T(8,128)(2,1)S(1)} collective-permute-done((bf16[8,416,128]{2,1,0:T(8,128)(2,1)S(1)}, bf16[8,416,128]{2,1,0:T(8,128)(2,1)S(1)}, u32[]{:S(2)}, u32[]{:S(2)}) %collective-permute-start.3) | collective-permute-done | bytes 852000 | tf_op jit(solution)/shard_map/ppermute | solution.py:157
  68.5 2.1 collective-permute-done.9.refs_1_
  70.6 2.2 collective-permute-done.15.refs_5_
  75.1 7.0 %shard_map.118 = (bf16[640,1024]{1,0:T(8,128)(2,1)S(1)}, bf16[640,256]{1,0:T(8,128)(2,1)S(1)}, bf16[640,256]{1,0:T(8,128)(2,1)S(1)}, bf16[1024,640]{1,0:T(8,128)(2,1)S(1)}, bf16[32,16,128]{2,1,0:T(8,128)(2,1)S(1)}) custom-call(s32[1]{0:T(128)} %bitcast.1.device_ref, bf16[8,416,128]{2,1,0:T(8,128)(2,1)S(1)} %copy-done.2, bf16[8,416,128]{2,1,0:T(8,128)(2,1)S(1)} %copy-done.6, ...), custom_call_target="tpu_custom_call" | custom-call | tf_op jit(solution)/shard_map/pallas_call | solution.py:260
  88.1 10.6 %shard_map.119 = (bf16[640,2048]{1,0:T(8,128)(2,1)S(1)}, bf16[640,2048]{1,0:T(8,128)(2,1)S(1)}, bf16[2048,640]{1,0:T(8,128)(2,1)}) custom-call(s32[1]{0:T(128)} %bitcast.1.device_ref, bf16[8,480,128]{2,1,0:T(8,128)(2,1)} %pad_maximum_fusion.refs_0_, bf16[8,480,128]{2,1,0:T(8,128)(2,1)} %collective-permute-done.9.refs_1_, ...), custom_call_target="tpu_custom_call" | custom-call | tf_op jit(solution)/shard_map/pallas_call | solution.py:260
  105.9 14.2 %shard_map.120 = (bf16[16,960,128]{2,1,0:T(8,128)(2,1)S(1)}, bf16[16,960,128]{2,1,0:T(8,128)(2,1)}) custom-call(s32[1]{0:T(128)} %bitcast.1.device_ref, bf16[128,640]{1,0:T(8,128)(2,1)S(1)} %multiply_convert_fusion.2.refs_0_.refs_2_, bf16[128,2048]{1,0:T(8,128)(2,1)S(1)} %get-tuple-element.136.refs_1_, ...), custom_call_target="tpu_custom_call" | custom-call | tf_op jit(solution)/shard_map/pallas_call | solution.py:333
  130.2 6.0 %add_convert_fusion = (bf16[8,320,128]{2,1,0:T(8,128)(2,1)}, bf16[8,320,128]{2,1,0:T(8,128)(2,1)}, bf16[8,320,128]{2,1,0:T(8,128)(2,1)}, bf16[8,320,128]{2,1,0:T...) fusion(bf16[16,960,128]{2,1,0:T(8,128)(2,1)} %collective-permute-done.18, ...), kind=kLoop, calls=%fused_computation.2 | loop fusion | flops 7864320 | bytes 11796480 | tf_op jit(solution)/shard_map/convert_element_type | solution.py:428
  147.9 8.7 %shard_map.121 = (bf16[16,416,128]{2,1,0:T(8,128)(2,1)S(1)}, bf16[16,416,128]{2,1,0:T(8,128)(2,1)S(1)}) custom-call(s32[1]{0:T(128)} %bitcast.1.device_ref, bf16[128,640]{1,0:T(8,128)(2,1)S(1)} %fusion.24.refs_0_.refs_2_.refs_4_, bf16[128,1024]{1,0:T(8,128)(2,1)S(1)} %bitcast.140, bf16[128,640]{1,0:T(8,128)(2,1)S(1)} %fusion.24.refs_0_.refs_2_.refs_4_, ...), custom_call_target="tpu_custom_call" | custom-call | tf_op jit(solution)/shard_map/pallas_call | solution.py:333
  167.4 4.4 %collective-permute-done.25 = bf16[4,320,128]{2,1,0:T(8,128)(2,1)S(1)} collective-permute-done((bf16[4,320,128]{2,1,0:T(8,128)(2,1)S(1)}, bf16[4,320,128]{2,1,0:T(8,128)(2,1)S(1)}, u32[]{:S(2)}, u32[]{:S(2)}) %collective-permute-start.25) | collective-permute-done | bytes 327712 | tf_op jit(solution)/shard_map/ppermute | solution.py:157
  182.3 7.3 %collective-permute-done.26 = bf16[2,320,128]{2,1,0:T(8,128)(2,1)S(1)} collective-permute-done((bf16[2,320,128]{2,1,0:T(8,128)(2,1)S(1)}, bf16[2,320,128]{2,1,0:T(8,128)(2,1)S(1)}, u32[]{:S(2)}, u32[]{:S(2)}) %collective-permute-start.26) | collective-permute-done | bytes 163872 | tf_op jit(solution)/shard_map/ppermute | solution.py:157
  191.3 2.4 %collective-permute-start.33 = (bf16[1,320,128]{2,1,0:T(8,128)(2,1)S(1)}, bf16[1,320,128]{2,1,0:T(8,128)(2,1)S(1)}, u32[]{:S(2)}, u32[]{:S(2)}) collective-permute-start(bf16[1,320,128]{2,1,0:T(8,128)(2,1)S(1)} %add_convert_fusion.34), channel_id=1, source_target_pairs={{0,16},{1,17},{2,18},{3,19},{4,20},{5,21},{6,22},{7,23},{8,24},{9,... | collective-permute-start | bytes 245768 | tf_op jit(solution)/shard_map/ppermute | solution.py:157
  197.6 2.0 collective-permute-done.33
  201.6 2.2 %collective-permute-start.37 = (bf16[2,208,128]{2,1,0:T(8,128)(2,1)S(1)}, bf16[2,208,128]{2,1,0:T(8,128)(2,1)S(1)}, u32[]{:S(2)}, u32[]{:S(2)}) collective-permute-start(bf16[2,208,128]{2,1,0:T(8,128)(2,1)S(1)} %get-tuple-element.159), channel_id=1, source_target_pairs={{0,16},{1,17},{2,18},{3,19},{4,20},{5,21},{6,22},{7,23},{8,24},{9,... | collective-permute-start | bytes 319496 | tf_op jit(solution)/shard_map/ppermute | solution.py:157
  204.7 3.8 %collective-permute-done.37 = bf16[2,208,128]{2,1,0:T(8,128)(2,1)S(1)} collective-permute-done((bf16[2,208,128]{2,1,0:T(8,128)(2,1)S(1)}, bf16[2,208,128]{2,1,0:T(8,128)(2,1)S(1)}, u32[]{:S(2)}, u32[]{:S(2)}) %collective-permute-start.37) | collective-permute-done | bytes 106528 | tf_op jit(solution)/shard_map/ppermute | solution.py:157
  210.3 2.2 %collective-permute-start.38 = (bf16[1,208,128]{2,1,0:T(8,128)(2,1)S(1)}, bf16[1,208,128]{2,1,0:T(8,128)(2,1)S(1)}, u32[]{:S(2)}, u32[]{:S(2)}) collective-permute-start(bf16[1,208,128]{2,1,0:T(8,128)(2,1)S(1)} %add_convert_fusion.39), channel_id=1, source_target_pairs={{0,16},{1,17},{2,18},{3,19},{4,20},{5,21},{6,22},{7,23},{8,24},{9,... | collective-permute-start | bytes 159752 | tf_op jit(solution)/shard_map/ppermute | solution.py:157
  (341 shorter events, 89.5 us)
Async XLA Ops:
  5.5 16.4 %collective-permute-start.6 = (bf16[1,480,128]{2,1,0:T(8,128)(2,1)S(1)}, bf16[1,480,128]{2,1,0:T(8,128)(2,1)S(1)}, u32[]{:S(2)}, u32[]{:S(2)}) collective-permute-start(bf16[1,480,128]{2,1,0:T(8,128)(2,1)S(1)} %get-tuple-element.163), channel_id=1, source_target_pairs={{0,16},{1,17},{2,18},{3,19},{4,20},{5,21},{6,22},{7,23},{8,24},{9,... | collective-permute-start | bytes 368648 | tf_op jit(solution)/shard_map/ppermute | solution.py:157
  8.5 18.0 %collective-permute-start.1 = (bf16[2,416,128]{2,1,0:T(8,128)(2,1)S(1)}, bf16[2,416,128]{2,1,0:T(8,128)(2,1)S(1)}, u32[]{:S(2)}, u32[]{:S(2)}) collective-permute-start(bf16[2,416,128]{2,1,0:T(8,128)(2,1)S(1)} %pad_maximum_fusion.10), channel_id=1, source_target_pairs={{0,16},{1,17},{2,18},{3,19},{4,20},{5,21},{6,22},{7,23},{8,24},{9,... | collective-permute-start | bytes 638984 | tf_op jit(solution)/shard_map/ppermute | solution.py:157
  12.5 15.8 %collective-permute-start.12 = (bf16[1,480,128]{2,1,0:T(8,128)(2,1)S(1)}, bf16[1,480,128]{2,1,0:T(8,128)(2,1)S(1)}, u32[]{:S(2)}, u32[]{:S(2)}) collective-permute-start(bf16[1,480,128]{2,1,0:T(8,128)(2,1)S(1)} %get-tuple-element.162), channel_id=1, source_target_pairs={{0,16},{1,17},{2,18},{3,19},{4,20},{5,21},{6,22},{7,23},{8,24},{9,... | collective-permute-start | bytes 368648 | tf_op jit(solution)/shard_map/ppermute | solution.py:157
  26.5 10.9 %collective-permute-start.2 = (bf16[4,416,128]{2,1,0:T(8,128)(2,1)S(1)}, bf16[4,416,128]{2,1,0:T(8,128)(2,1)S(1)}, u32[]{:S(2)}, u32[]{:S(2)}) collective-permute-start(bf16[4,416,128]{2,1,0:T(8,128)(2,1)S(1)} %pad_maximum_fusion.6), channel_id=1, source_target_pairs={{0,2},{1,3},{2,0},{3,1},{4,6},{5,7},{6,4},{7,5},{8,10},{9,11},{10,... | collective-permute-start | bytes 1277960 | tf_op jit(solution)/shard_map/ppermute | solution.py:157
  30.8 17.2 %collective-permute-start.8 = (bf16[4,480,128]{2,1,0:T(8,128)(2,1)}, bf16[4,480,128]{2,1,0:T(8,128)(2,1)}, u32[]{:S(2)}, u32[]{:S(2)}) collective-permute-start(bf16[4,480,128]{2,1,0:T(8,128)(2,1)} %pad_maximum_fusion.4), channel_id=1, source_target_pairs={{0,4},{1,5},{2,6},{3,7},{4,0},{5,1},{6,2},{7,3},{8,12},{9,13},{10,... | collective-permute-start | bytes 1474568 | tf_op jit(solution)/shard_map/ppermute | solution.py:157
  37.3 12.7 %collective-permute-start.14 = (bf16[4,480,128]{2,1,0:T(8,128)(2,1)S(1)}, bf16[4,480,128]{2,1,0:T(8,128)(2,1)}, u32[]{:S(2)}, u32[]{:S(2)}) collective-permute-start(bf16[4,480,128]{2,1,0:T(8,128)(2,1)S(1)} %pad_maximum_fusion.5), channel_id=1, source_target_pairs={{0,8},{1,9},{2,10},{3,11},{4,12},{5,13},{6,14},{7,15},{8,0},{9,1},... | collective-permute-start | bytes 1474568 | tf_op jit(solution)/shard_map/ppermute | solution.py:157
  37.5 26.8 %collective-permute-start.3 = (bf16[8,416,128]{2,1,0:T(8,128)(2,1)S(1)}, bf16[8,416,128]{2,1,0:T(8,128)(2,1)S(1)}, u32[]{:S(2)}, u32[]{:S(2)}) collective-permute-start(bf16[8,416,128]{2,1,0:T(8,128)(2,1)S(1)} %pad_maximum_fusion.2.refs_0_), channel_id=1, source_target_pairs={{0,4},{1,5},{2,6},{3,7},{4,0},{5,1},{6,2},{7,3},{8,12},{9,13},{10,... | collective-permute-start | bytes 2555912 | tf_op jit(solution)/shard_map/ppermute | solution.py:157
  50.0 20.6 %collective-permute-start.9 = (bf16[8,480,128]{2,1,0:T(8,128)(2,1)}, bf16[8,480,128]{2,1,0:T(8,128)(2,1)}, u32[]{:S(2)}, u32[]{:S(2)}) collective-permute-start(bf16[8,480,128]{2,1,0:T(8,128)(2,1)} %pad_maximum_fusion.refs_0_), channel_id=1, source_target_pairs={{0,8},{1,9},{2,10},{3,11},{4,12},{5,13},{6,14},{7,15},{8,0},{9,1},... | collective-permute-start | bytes 2949128 | tf_op jit(solution)/shard_map/ppermute | solution.py:157
  52.2 20.6 %collective-permute-start.15 = (bf16[8,480,128]{2,1,0:T(8,128)(2,1)}, bf16[8,480,128]{2,1,0:T(8,128)(2,1)}, u32[]{:S(2)}, u32[]{:S(2)}) collective-permute-start(bf16[8,480,128]{2,1,0:T(8,128)(2,1)} %pad_maximum_fusion.1.refs_4_), channel_id=1, source_target_pairs={{0,2},{1,3},{2,0},{3,1},{4,6},{5,7},{6,4},{7,5},{8,10},{9,11},{10,... | collective-permute-start | bytes 2949128 | tf_op jit(solution)/shard_map/ppermute | solution.py:157
  53.7 14.9 %collective-permute-start.4 = (bf16[8,416,128]{2,1,0:T(8,128)(2,1)S(1)}, bf16[8,416,128]{2,1,0:T(8,128)(2,1)S(1)}, u32[]{:S(2)}, u32[]{:S(2)}) collective-permute-start(bf16[8,416,128]{2,1,0:T(8,128)(2,1)S(1)} %pad_maximum_fusion.2.refs_0_), channel_id=1, source_target_pairs={{0,1},{1,0},{2,3},{3,2},{4,5},{5,4},{6,7},{7,6},{8,9},{9,8},{10,11... | collective-permute-start | bytes 2555912 | tf_op jit(solution)/shard_map/ppermute | solution.py:157
  68.0 20.0 %collective-permute-start.10 = (bf16[8,480,128]{2,1,0:T(8,128)(2,1)}, bf16[8,480,128]{2,1,0:T(8,128)(2,1)}, u32[]{:S(2)}, u32[]{:S(2)}) collective-permute-start(bf16[8,480,128]{2,1,0:T(8,128)(2,1)} %pad_maximum_fusion.refs_0_), channel_id=1, source_target_pairs={{0,1},{1,0},{2,3},{3,2},{4,5},{5,4},{6,7},{7,6},{8,9},{9,8},{10,11... | collective-permute-start | bytes 2949128 | tf_op jit(solution)/shard_map/ppermute | solution.py:157
  68.5 19.5 %collective-permute-start.16 = (bf16[8,480,128]{2,1,0:T(8,128)(2,1)}, bf16[8,480,128]{2,1,0:T(8,128)(2,1)}, u32[]{:S(2)}, u32[]{:S(2)}) collective-permute-start(bf16[8,480,128]{2,1,0:T(8,128)(2,1)} %pad_maximum_fusion.1.refs_4_), channel_id=1, source_target_pairs={{0,1},{1,0},{2,3},{3,2},{4,5},{5,4},{6,7},{7,6},{8,9},{9,8},{10,11... | collective-permute-start | bytes 2949128 | tf_op jit(solution)/shard_map/ppermute | solution.py:157
  70.6 17.4 %collective-permute-start.11 = (bf16[8,480,128]{2,1,0:T(8,128)(2,1)}, bf16[8,480,128]{2,1,0:T(8,128)(2,1)}, u32[]{:S(2)}, u32[]{:S(2)}) collective-permute-start(bf16[8,480,128]{2,1,0:T(8,128)(2,1)} %collective-permute-done.9.refs_1_), channel_id=1, source_target_pairs={{0,1},{1,0},{2,3},{3,2},{4,5},{5,4},{6,7},{7,6},{8,9},{9,8},{10,11... | collective-permute-start | bytes 2949128 | tf_op jit(solution)/shard_map/ppermute | solution.py:157
  72.8 15.3 %collective-permute-start.17 = (bf16[8,480,128]{2,1,0:T(8,128)(2,1)}, bf16[8,480,128]{2,1,0:T(8,128)(2,1)}, u32[]{:S(2)}, u32[]{:S(2)}) collective-permute-start(bf16[8,480,128]{2,1,0:T(8,128)(2,1)} %collective-permute-done.15.refs_5_), channel_id=1, source_target_pairs={{0,1},{1,0},{2,3},{3,2},{4,5},{5,4},{6,7},{7,6},{8,9},{9,8},{10,11... | collective-permute-start | bytes 2949128 | tf_op jit(solution)/shard_map/ppermute | solution.py:157
  140.8 17.4 %collective-permute-start.19 = (bf16[8,320,128]{2,1,0:T(8,128)(2,1)}, bf16[8,320,128]{2,1,0:T(8,128)(2,1)}, u32[]{:S(2)}, u32[]{:S(2)}) collective-permute-start(bf16[8,320,128]{2,1,0:T(8,128)(2,1)} %get-tuple-element.75), channel_id=1, source_target_pairs={{0,2},{1,3},{2,0},{3,1},{4,6},{5,7},{6,4},{7,5},{8,10},{9,11},{10,... | collective-permute-start | bytes 1966088 | tf_op jit(solution)/shard_map/ppermute | solution.py:157
  142.0 17.0 %collective-permute-start.20 = (bf16[8,320,128]{2,1,0:T(8,128)(2,1)}, bf16[8,320,128]{2,1,0:T(8,128)(2,1)}, u32[]{:S(2)}, u32[]{:S(2)}) collective-permute-start(bf16[8,320,128]{2,1,0:T(8,128)(2,1)} %get-tuple-element.76), channel_id=1, source_target_pairs={{0,4},{1,5},{2,6},{3,7},{4,0},{5,1},{6,2},{7,3},{8,12},{9,13},{10,... | collective-permute-start | bytes 1966088 | tf_op jit(solution)/shard_map/ppermute | solution.py:157
  143.6 16.8 %collective-permute-start.21 = (bf16[8,320,128]{2,1,0:T(8,128)(2,1)}, bf16[8,320,128]{2,1,0:T(8,128)(2,1)}, u32[]{:S(2)}, u32[]{:S(2)}) collective-permute-start(bf16[8,320,128]{2,1,0:T(8,128)(2,1)} %get-tuple-element.77), channel_id=1, source_target_pairs={{0,8},{1,9},{2,10},{3,11},{4,12},{5,13},{6,14},{7,15},{8,0},{9,1},... | collective-permute-start | bytes 1966088 | tf_op jit(solution)/shard_map/ppermute | solution.py:157
  160.3 14.9 %collective-permute-start.22 = (bf16[16,416,128]{2,1,0:T(8,128)(2,1)S(1)}, bf16[16,416,128]{2,1,0:T(8,128)(2,1)S(1)}, u32[]{:S(2)}, u32[]{:S(2)}) collective-permute-start(bf16[16,416,128]{2,1,0:T(8,128)(2,1)S(1)} %get-tuple-element.79), channel_id=1, source_target_pairs={{0,1},{1,0},{2,3},{3,2},{4,5},{5,4},{6,7},{7,6},{8,9},{9,8},{10,11... | collective-permute-start | bytes 5111816 | tf_op jit(solution)/shard_map/ppermute | solution.py:157
  161.6 10.2 %collective-permute-start.25 = (bf16[4,320,128]{2,1,0:T(8,128)(2,1)S(1)}, bf16[4,320,128]{2,1,0:T(8,128)(2,1)S(1)}, u32[]{:S(2)}, u32[]{:S(2)}) collective-permute-start(bf16[4,320,128]{2,1,0:T(8,128)(2,1)S(1)} %get-tuple-element.139), channel_id=1, source_target_pairs={{0,4},{1,5},{2,6},{3,7},{4,0},{5,1},{6,2},{7,3},{8,12},{9,13},{10,... | collective-permute-start | bytes 983048 | tf_op jit(solution)/shard_map/ppermute | solution.py:157
  163.4 9.9 %collective-permute-start.24 = (bf16[4,320,128]{2,1,0:T(8,128)(2,1)S(1)}, bf16[4,320,128]{2,1,0:T(8,128)(2,1)S(1)}, u32[]{:S(2)}, u32[]{:S(2)}) collective-permute-start(bf16[4,320,128]{2,1,0:T(8,128)(2,1)S(1)} %get-tuple-element.141), channel_id=1, source_target_pairs={{0,2},{1,3},{2,0},{3,1},{4,6},{5,7},{6,4},{7,5},{8,10},{9,11},{10,... | collective-permute-start | bytes 983048 | tf_op jit(solution)/shard_map/ppermute | solution.py:157
  165.6 9.6 %collective-permute-start.23 = (bf16[4,320,128]{2,1,0:T(8,128)(2,1)S(1)}, bf16[4,320,128]{2,1,0:T(8,128)(2,1)S(1)}, u32[]{:S(2)}, u32[]{:S(2)}) collective-permute-start(bf16[4,320,128]{2,1,0:T(8,128)(2,1)S(1)} %get-tuple-element.143), channel_id=1, source_target_pairs={{0,8},{1,9},{2,10},{3,11},{4,12},{5,13},{6,14},{7,15},{8,0},{9,1},... | collective-permute-start | bytes 983048 | tf_op jit(solution)/shard_map/ppermute | solution.py:157
  178.9 11.0 %collective-permute-start.29 = (bf16[8,208,128]{2,1,0:T(8,128)(2,1)S(1)}, bf16[8,208,128]{2,1,0:T(8,128)(2,1)S(1)}, u32[]{:S(2)}, u32[]{:S(2)}) collective-permute-start(bf16[8,208,128]{2,1,0:T(8,128)(2,1)S(1)} %get-tuple-element.134), channel_id=1, source_target_pairs={{0,2},{1,3},{2,0},{3,1},{4,6},{5,7},{6,4},{7,5},{8,10},{9,11},{10,... | collective-permute-start | bytes 1277960 | tf_op jit(solution)/shard_map/ppermute | solution.py:157
  179.9 10.0 %collective-permute-start.30 = (bf16[8,208,128]{2,1,0:T(8,128)(2,1)S(1)}, bf16[8,208,128]{2,1,0:T(8,128)(2,1)S(1)}, u32[]{:S(2)}, u32[]{:S(2)}) collective-permute-start(bf16[8,208,128]{2,1,0:T(8,128)(2,1)S(1)} %get-tuple-element.133), channel_id=1, source_target_pairs={{0,4},{1,5},{2,6},{3,7},{4,0},{5,1},{6,2},{7,3},{8,12},{9,13},{10,... | collective-permute-start | bytes 1277960 | tf_op jit(solution)/shard_map/ppermute | solution.py:157
  190.0 11.5 %collective-permute-start.35 = (bf16[4,208,128]{2,1,0:T(8,128)(2,1)S(1)}, bf16[4,208,128]{2,1,0:T(8,128)(2,1)S(1)}, u32[]{:S(2)}, u32[]{:S(2)}) collective-permute-start(bf16[4,208,128]{2,1,0:T(8,128)(2,1)S(1)} %get-tuple-element.145), channel_id=1, source_target_pairs={{0,2},{1,3},{2,0},{3,1},{4,6},{5,7},{6,4},{7,5},{8,10},{9,11},{10,... | collective-permute-start | bytes 638984 | tf_op jit(solution)/shard_map/ppermute | solution.py:157
  (93 other events, 369.5 us)

commit v3 on v2

--- a/solution.py
+++ b/solution.py
@@ -113,37 +113,100 @@
     return (context.astype(jnp.bfloat16), log_total)
 
 
-def attend_back(rot_query, rot_key, value_vec, allowed, log_total, context, delta_context):
-    num_heads = rot_query.shape[0]
-    num_slots = rot_key.shape[0]
-    head_delta = delta_context.reshape(num_slots, num_heads, HD).transpose(1, 0, 2).reshape(-1, HD)
-    head_context = context.reshape(num_slots, num_heads, HD).transpose(1, 0, 2).reshape(-1, HD)
-    row_dot = jnp.sum(
-        head_delta.astype(jnp.float32) * head_context.astype(jnp.float32), axis=-1, keepdims=True
-    )
-    flat_query = rot_query.reshape(-1, HD)
-    scores = lax.dot_general(
-        flat_query, rot_key, (((1,), (1,)), ((), ())), preferred_element_type=jnp.float32
-    )
-    scores = jnp.where(allowed[None], scores.reshape(num_heads, num_slots, num_slots), -1e30)
-    prob_exact = jnp.exp(scores - log_total).reshape(-1, num_slots)
-    delta_value = lax.dot_general(
-        prob_exact.astype(jnp.bfloat16),
-        head_delta,
-        (((0,), (0,)), ((), ())),
-        preferred_element_type=jnp.float32,
-    )
-    delta_prob = lax.dot_general(
-        head_delta, value_vec, (((1,), (1,)), ((), ())), preferred_element_type=jnp.float32
-    )
-    delta_score = (prob_exact * (delta_prob - row_dot)).astype(jnp.bfloat16)
-    delta_query = jnp.dot(delta_score, rot_key, preferred_element_type=jnp.float32).reshape(
-        num_heads, num_slots, HD
-    )
-    delta_key = lax.dot_general(
-        delta_score, flat_query, (((0,), (0,)), ((), ())), preferred_element_type=jnp.float32
-    )
-    return (delta_query, delta_key, delta_value.astype(jnp.bfloat16))
+def rms_pull(raw, gain_vec, delta):
+    scale = lax.rsqrt(jnp.mean(raw * raw, axis=-1, keepdims=True) + 1e-06)
+    weighed = delta * (1.0 + gain_vec)
+    shared = jnp.mean(raw * weighed, axis=-1, keepdims=True)
+    return scale * weighed - raw * (scale * scale * scale * shared), delta * raw * scale
+
+
+def rotate_pull(delta, cos_tab, sin_tab):
+    half_dim = delta.shape[-1] // 2
+    lower_half = delta[:, :half_dim]
+    upper_half = delta[:, half_dim:]
+    return jnp.concatenate(
+        [lower_half * cos_tab + upper_half * sin_tab, upper_half * cos_tab - lower_half * sin_tab],
+        axis=-1,
+    )
+
+
+def attn_back_kernel(
+    delta_attn,
+    delta_mid,
+    resid_in,
+    query_raw,
+    key_raw,
+    value_vec,
+    rot_query,
+    rot_key,
+    context,
+    log_total,
+    allowed,
+    cos_ref,
+    sin_ref,
+    gain_in,
+    gain_query,
+    gain_key,
+    query_weight,
+    key_weight,
+    value_weight,
+    out_weight,
+    grad_in,
+    delta_qraw,
+    delta_kraw,
+    delta_value,
+    gain_in_grad,
+    gain_query_grad,
+    gain_key_grad,
+):
+    cos_tab = cos_ref[...]
+    sin_tab = sin_ref[...]
+    keys = rot_key[...]
+    values = value_vec[...]
+    open_pairs = allowed[...] > 0.0
+    delta_context = times_transposed(delta_attn[...], out_weight[...]).astype(jnp.bfloat16)
+    delta_key = jnp.zeros((CAP, HD), jnp.float32)
+    delta_values = jnp.zeros((CAP, HD), jnp.float32)
+    query_gain_rows = jnp.zeros((CAP, HD), jnp.float32)
+    for head in range(HQ // HD):
+        at = slice(head * HD, (head + 1) * HD)
+        head_delta = delta_context[:, at]
+        row_dot = jnp.sum(
+            head_delta.astype(jnp.float32) * context[:, at].astype(jnp.float32),
+            axis=-1,
+            keepdims=True,
+        )
+        queries = rot_query[head]
+        scores = jnp.where(open_pairs, times_transposed(queries, keys), -1e30)
+        prob_exact = jnp.exp(scores - log_total[:, head : head + 1])
+        delta_prob = times_transposed(head_delta, values)
+        delta_score = prob_exact * (delta_prob - row_dot)
+        turned = delta_score.T.astype(jnp.bfloat16)
+        delta_score = delta_score.astype(jnp.bfloat16)
+        delta_query = jnp.dot(delta_score, keys, preferred_element_type=jnp.float32)
+        delta_key += jnp.dot(turned, queries, preferred_element_type=jnp.float32)
+        delta_values += jnp.dot(
+            prob_exact.T.astype(jnp.bfloat16), head_delta, preferred_element_type=jnp.float32
+        )
+        delta_rot = rotate_pull(delta_query * HD ** (-0.5), cos_tab, sin_tab)
+        delta_raw, gain_rows = rms_pull(query_raw[:, at], gain_query[...], delta_rot)
+        query_gain_rows += gain_rows
+        delta_qraw[:, at] = delta_raw.astype(jnp.bfloat16)
+    delta_raw, gain_rows = rms_pull(
+        key_raw[...], gain_key[...], rotate_pull(delta_key, cos_tab, sin_tab)
+    )
+    delta_kraw[...] = delta_raw.astype(jnp.bfloat16)
+    delta_value[...] = delta_values.astype(jnp.bfloat16)
+    gain_query_grad[...] = jnp.sum(query_gain_rows, axis=0, keepdims=True)
+    gain_key_grad[...] = jnp.sum(gain_rows, axis=0, keepdims=True)
+    delta_in = (
+        times_transposed(delta_qraw[...], query_weight[...])
+        + times_transposed(delta_kraw[...], key_weight[...])
+        + times_transposed(delta_value[...], value_weight[...])
+    )
+    delta_part, gain_rows = rms_pull(resid_in[...].astype(jnp.float32), gain_in[...], delta_in)
+    grad_in[...] = delta_mid[...] + delta_part
+    gain_in_grad[...] = jnp.sum(gain_rows, axis=0, keepdims=True)
 
 
 def bit_orders(devices, tuned):
@@ -205,35 +268,38 @@
     return [pl.BlockSpec(memory_space=pltpu.VMEM)] * count
 
 
-def place_specs(count):
-    return [pl.BlockSpec(memory_space=pl.ANY)] * count
+def copy_step(rows):
+    return max(step for step in range(ROWS, 513, ROWS) if rows % step == 0)
+
+
+def owner_rows(device, index, order, extra, start, each):
+    owner = device ^ extra
+    for k, bit in enumerate(order):
+        owner = owner ^ (((index >> k) & 1) << bit)
+    return owner, pl.multiple_of(owner * each + start, ROWS)
 
 
 def unpack_kernel(plan, sizes, tail_rows, sources, device_ref, *refs):
     source_refs = refs[:sources]
     matrices = refs[sources : sources + len(sizes)]
     refs = refs[sources + len(sizes) :]
-    tails = None
-    if tail_rows:
-        tails, refs = refs[0], refs[1:]
-    flat, spread, sems = refs
+    tails = refs[0] if tail_rows else None
+    spread = refs[-1]
     device = device_ref[0]
-    copies = []
-    for source, index, offset, low, take, start, each in plan:
-        owner = device ^ offset
-        if start is None:
-            target = tails.at[owner]
-        else:
-            target = flat.at[pl.ds(pl.multiple_of(owner * each + start, ROWS), take), :]
-        copies.append(
-            pltpu.make_async_copy(
-                source_refs[source].at[index, pl.ds(low, take), :], target, sems.at[len(copies)]
-            )
-        )
-    for copy in copies:
-        copy.start()
-    for copy in copies:
-        copy.wait()
+    for source, order, extra, take, start, each in plan:
+        block_ref = source_refs[source]
+        step = copy_step(take)
+
+        @pl.loop(0, block_ref.shape[0])
+        def _(index, block_ref=block_ref, order=order, extra=extra, take=take, start=start, each=each, step=step):
+            owner, first = owner_rows(device, index, order, extra, start, each)
+            for low in range(0, take, step):
+                spread[pl.ds(pl.multiple_of(first + low, ROWS), step), :] = block_ref[
+                    index, low : low + step, :
+                ].astype(jnp.float32)
+            if take < block_ref.shape[1]:
+                tails[owner] = block_ref[index, take : take + tail_rows, :]
+
     first = 0
     for matrix, (rows, columns) in zip(matrices, sizes):
         blocks = columns // LANES
@@ -241,11 +307,10 @@
         @pl.loop(0, rows // LANES)
         def _(step, matrix=matrix, blocks=blocks, first=first):
             base = pl.multiple_of(first + step * (LANES * blocks), ROWS)
-            spread[: LANES * blocks] = flat[pl.ds(base, LANES * blocks), :].astype(jnp.float32)
             at = pl.ds(pl.multiple_of(step * LANES, LANES), LANES)
             for block in range(blocks):
                 matrix[at, block * LANES : (block + 1) * LANES] = spread[
-                    pl.ds(block, LANES, stride=blocks), :
+                    pl.ds(base + block, LANES, stride=blocks), :
                 ].astype(jnp.bfloat16)
 
         first += rows * blocks
@@ -253,21 +318,16 @@
 
 def unpack_matrices(plan, sizes, tail_rows, device, arrays, devices):
     flat_rows = sum(rows * columns for rows, columns in sizes) // LANES
-    widest = max(columns for _, columns in sizes)
     shapes = [jax.ShapeDtypeStruct(size, jnp.bfloat16) for size in sizes]
     if tail_rows:
         shapes.append(jax.ShapeDtypeStruct((devices, tail_rows, LANES), jnp.bfloat16))
     return pl.pallas_call(
         functools.partial(unpack_kernel, plan, sizes, tail_rows, len(arrays)),
         out_shape=shapes,
-        in_specs=[pl.BlockSpec(memory_space=pltpu.SMEM)] + place_specs(len(arrays)),
+        in_specs=[pl.BlockSpec(memory_space=pltpu.SMEM)] + whole_specs(len(arrays)),
         out_specs=whole_specs(len(shapes)),
-        scratch_shapes=[
-            pltpu.VMEM((flat_rows, LANES), jnp.bfloat16),
-            pltpu.VMEM((widest, LANES), jnp.float32),
-            pltpu.SemaphoreType.DMA((len(plan),)),
-        ],
-        compiler_params=pltpu.CompilerParams(vmem_limit_bytes=40 << 20),
+        scratch_shapes=[pltpu.VMEM((flat_rows, LANES), jnp.float32)],
+        compiler_params=pltpu.CompilerParams(vmem_limit_bytes=48 << 20),
         cost_estimate=pl.CostEstimate(flops=0, bytes_accessed=0, transcendentals=0),
     )(device, *arrays)
 
@@ -275,11 +335,9 @@
 def grads_kernel(plan, sizes, has_tails, device_ref, *refs):
     pairs = refs[: 2 * len(sizes)]
     refs = refs[2 * len(sizes) :]
-    tails = None
-    if has_tails:
-        tails, refs = refs[0], refs[1:]
-    targets = refs[:-3]
-    spread, flat, sems = refs[-3:]
+    tails = refs[0] if has_tails else None
+    targets = refs[1 if has_tails else 0 : -1]
+    spread = refs[-1]
     device = device_ref[0]
     first = 0
     for number, (rows, columns) in enumerate(sizes):
@@ -294,53 +352,39 @@
                 preferred_element_type=jnp.float32,
             )
             for part in range(wide):
-                spread[pl.ds(block + part, rows, stride=blocks), :] = product[
+                spread[pl.ds(first + block + part, rows, stride=blocks), :] = product[
                     :, part * LANES : (part + 1) * LANES
                 ]
-
-        step_rows = 1280 if rows * blocks % 1280 == 0 else 1024
-
-        @pl.loop(0, rows * blocks // step_rows)
-        def _(step, first=first, step_rows=step_rows):
-            low = pl.multiple_of(step * step_rows, step_rows)
-            flat[pl.ds(pl.multiple_of(first + low, ROWS), step_rows), :] = spread[
-                pl.ds(low, step_rows), :
-            ].astype(jnp.bfloat16)
-
         first += rows * blocks
-    copies = []
-    for target, index, offset, low, take, start, each in plan:
-        owner = device ^ offset
-        if start is None:
-            source = tails.at[owner]
-        else:
-            source = flat.at[pl.ds(pl.multiple_of(owner * each + start, ROWS), take), :]
-        copies.append(
-            pltpu.make_async_copy(
-                source, targets[target].at[index, pl.ds(low, take), :], sems.at[len(copies)]
-            )
-        )
-    for copy in copies:
-        copy.start()
-    for copy in copies:
-        copy.wait()
+    for target, order, extra, low, take, start, each in plan:
+        target_ref = targets[target]
+        step = copy_step(take)
+
+        @pl.loop(0, target_ref.shape[0])
+        def _(index, target_ref=target_ref, order=order, extra=extra, low=low, take=take, start=start, each=each, step=step):
+            owner, first = owner_rows(device, index, order, extra, start or 0, each)
+            if start is None:
+                target_ref[index, low : low + take, :] = tails[owner]
+                return
+
+            @pl.loop(0, take // step)
+            def _(part):
+                at = pl.multiple_of(part * step, ROWS)
+                target_ref[index, pl.ds(pl.multiple_of(low + at, ROWS), step), :] = spread[
+                    pl.ds(pl.multiple_of(first + at, ROWS), step), :
+                ].astype(jnp.bfloat16)
 
 
 def grad_blocks(plan, sizes, pairs, tails, device, shapes):
     flat_rows = sum(rows * columns for rows, columns in sizes) // LANES
-    longest = max(rows * columns for rows, columns in sizes) // LANES
     inputs = [member for pair in pairs for member in pair] + ([] if tails is None else [tails])
     return pl.pallas_call(
         functools.partial(grads_kernel, plan, sizes, tails is not None),
         out_shape=[jax.ShapeDtypeStruct(shape, jnp.bfloat16) for shape in shapes],
         in_specs=[pl.BlockSpec(memory_space=pltpu.SMEM)] + whole_specs(len(inputs)),
-        out_specs=place_specs(len(shapes)),
-        scratch_shapes=[
-            pltpu.VMEM((longest, LANES), jnp.float32),
-            pltpu.VMEM((flat_rows, LANES), jnp.bfloat16),
-            pltpu.SemaphoreType.DMA((len(plan),)),
-        ],
-        compiler_params=pltpu.CompilerParams(vmem_limit_bytes=40 << 20),
+        out_specs=whole_specs(len(shapes)),
+        scratch_shapes=[pltpu.VMEM((flat_rows, LANES), jnp.float32)],
+        compiler_params=pltpu.CompilerParams(vmem_limit_bytes=48 << 20),
         cost_estimate=pl.CostEstimate(flops=0, bytes_accessed=0, transcendentals=0),
     )(device, *inputs)
 
@@ -359,18 +403,15 @@
             arrays.append(jnp.take(table, jnp.array(back, jnp.int32) ^ mixed, axis=0))
             continue
         for part, block in enumerate(blocks):
-            for index in range(block.shape[0]):
-                offset = offset_of(part * block.shape[0] + index, list(order) + [0])
-                plan.append((len(arrays), index, offset, 0, take, start, each))
-                if take < piece.shape[0]:
-                    plan.append((len(arrays), index, offset, take, tail_rows, None, each))
+            extra = offset_of(part, [order[-1], 0])
+            plan.append((len(arrays), order[:-1], extra, take, start, each))
             arrays.append(block)
         start += take
     if each % ROWS == 0:
         return unpack_matrices(plan, sizes, tail_rows, device, arrays, devices)
     table = jnp.concatenate(arrays, axis=1)
     flat = table[:, :each].reshape(1, devices * each, LANES)
-    plan = [(0, 0, 0, 0, devices * each, 0, 0)]
+    plan = [(0, [], 0, devices * each, 0, 0)]
     found = list(unpack_matrices(plan, sizes, 0, device, [flat], devices))
     return found + ([table[:, each : each + tail_rows]] if tail_rows else [])
 
@@ -385,22 +426,18 @@
     parts = cut_rows(each + tail_rows, len(orders))
     half = devices // 2
     plan = []
-    for (low, high), order in zip(parts, orders):
-        for with_core in (0, 1):
-            for index in range(half):
-                offset = offset_of(index, order[::-1]) ^ with_core
-                plan.append((with_core, index, offset, low, min(high, each) - low, low, each))
-    if tail_rows:
-        for with_core in (0, 1):
-            for index in range(half):
-                offset = offset_of(index, orders[len(parts) - 1][::-1]) ^ with_core
-                plan.append((with_core, index, offset, each, tail_rows, None, each))
+    for with_core in (1, 0):
+        for (low, high), order in zip(parts, orders):
+            order = order[::-1]
+            plan.append((with_core, order, with_core, low, min(high, each) - low, low, each))
+            if high > each:
+                plan.append((with_core, order, with_core, each, tail_rows, None, each))
     shape = (half, each + tail_rows, LANES)
     if each % ROWS == 0 and parts[-1][0] < each:
         blocks = grad_blocks(plan, sizes, pairs, tails, device, [shape, shape])
     else:
         flat = grad_blocks(
-            [(0, 0, 0, 0, devices * each, 0, 0)],
+            [(0, [], 0, 0, devices * each, 0, 0)],
             sizes,
             pairs,
             None,
@@ -515,9 +552,9 @@
     return (delta_mid, pairs, (gain_mid_grad, gain_last_grad))
 
 
-def attn_backward(delta_mid, weights, saved, allowed, cos_tab, sin_tab, pause):
+def attn_backward(delta_mid, delta_attn, input_rows, weights, saved, allowed, cos_tab, sin_tab):
     query_weight, key_weight, value_weight, out_weight = weights[:4]
-    gain_in, gain_query, gain_key, gain_post = weights[7][:4]
+    gain_in, gain_query, gain_key = weights[7][:3]
     (
         resid_in,
         normed_in,
@@ -530,41 +567,51 @@
         log_total,
         attn_out,
     ) = saved[:10]
-    unused, pullback = jax.vjp(rms_scale, attn_out, gain_post)
-    delta_attn, gain_post_grad = pullback(delta_mid)
-    delta_attn = delta_attn.astype(jnp.bfloat16)
-    delta_context = times_transposed(delta_attn, out_weight).astype(jnp.bfloat16)
-    delta_context, delta_attn = pause((delta_context, delta_attn))
-    delta_query, delta_key, delta_value = attend_back(
-        rot_query, rot_key, value_vec, allowed, log_total, context, delta_context
-    )
-
-    def rope_map(raw_query, raw_key, query_gain, key_gain):
-        return query_key(raw_query, raw_key, query_gain, key_gain, cos_tab, sin_tab)
-
-    unused, pullback = jax.vjp(rope_map, query_raw, key_raw, gain_query, gain_key)
-    delta_qraw, delta_kraw, gain_query_grad, gain_key_grad = pullback((delta_query, delta_key))
-    delta_qraw = delta_qraw.astype(jnp.bfloat16)
-    delta_kraw = delta_kraw.astype(jnp.bfloat16)
+    shapes = [
+        jax.ShapeDtypeStruct((CAP, D), jnp.float32),
+        jax.ShapeDtypeStruct((CAP, HQ), jnp.bfloat16),
+        jax.ShapeDtypeStruct((CAP, HD), jnp.bfloat16),
+        jax.ShapeDtypeStruct((CAP, HD), jnp.bfloat16),
+        jax.ShapeDtypeStruct((1, D), jnp.float32),
+        jax.ShapeDtypeStruct((1, HD), jnp.float32),
+        jax.ShapeDtypeStruct((1, HD), jnp.float32),
+    ]
+    grad_in, delta_qraw, delta_kraw, delta_value, *gain_grads = pl.pallas_call(
+        attn_back_kernel,
+        out_shape=shapes,
+        in_specs=whole_specs(20),
+        out_specs=whole_specs(len(shapes)),
+        compiler_params=pltpu.CompilerParams(vmem_limit_bytes=32 << 20),
+        cost_estimate=pl.CostEstimate(flops=0, bytes_accessed=0, transcendentals=0),
+    )(
+        delta_attn,
+        delta_mid,
+        input_rows,
+        query_raw,
+        key_raw,
+        value_vec,
+        rot_query,
+        rot_key,
+        context,
+        log_total.reshape(HQ // HD, CAP).T,
+        allowed.astype(jnp.float32),
+        cos_tab,
+        sin_tab,
+        gain_in[None],
+        gain_query[None],
+        gain_key[None],
+        query_weight,
+        key_weight,
+        value_weight,
+        out_weight,
+    )
     pairs = (
         (normed_in, delta_qraw),
         (normed_in, delta_kraw),
         (normed_in, delta_value),
         (context, delta_attn),
     )
-    delta_in = (
-        times_transposed(delta_qraw, query_weight)
-        + times_transposed(delta_kraw, key_weight)
-        + times_transposed(delta_value, value_weight)
-    )
-    unused, pullback = jax.vjp(rms_scale, resid_in, gain_in)
-    delta_part, gain_in_grad = pullback(delta_in)
-    grad_in = delta_mid + delta_part
-    return (
-        grad_in,
-        pairs,
-        (gain_in_grad, gain_query_grad, gain_key_grad, gain_post_grad),
-    )
+    return (grad_in, pairs, [member.reshape(-1) for member in gain_grads])
 
 
 def adam_update(weight_shard, gradient, moment_one, moment_two):
@@ -611,19 +658,17 @@
     )
     delta_mid, ffn_home, ffn_away = lax.optimization_barrier((delta_mid, ffn_home, ffn_away))
     ffn_came = across(ffn_away, 0, devices)
-    ffn_chunks = []
-
-    def pause(values):
-        nonlocal ffn_chunks, ffn_came
-        values, ffn_came = lax.optimization_barrier((values, ffn_came))
-        ffn_chunks = cores_merged(ffn_home, ffn_came, ffn_parts)
-        values, ffn_chunks = lax.optimization_barrier((values, ffn_chunks))
-        ffn_came = sent_blocks(ffn_chunks, ffn_orders, 0, devices)
-        return values
-
+    unused, pullback = jax.vjp(rms_scale, saved[9], weights[7][3])
+    delta_attn, gain_post_grad = pullback(delta_mid)
+    delta_attn = delta_attn.astype(jnp.bfloat16)
+    delta_attn, ffn_came = lax.optimization_barrier((delta_attn, ffn_came))
+    ffn_chunks = cores_merged(ffn_home, ffn_came, ffn_parts)
+    delta_attn, ffn_chunks = lax.optimization_barrier((delta_attn, ffn_chunks))
+    ffn_came = sent_blocks(ffn_chunks, ffn_orders, 0, devices)
     grad_in, attn_pairs, early_gains = attn_backward(
-        delta_mid, weights, saved, allowed, cos_tab, sin_tab, pause
-    )
+        delta_mid, delta_attn, hidden_in, weights, saved, allowed, cos_tab, sin_tab
+    )
+    early_gains = (*early_gains, gain_post_grad)
     gain_table = jnp.concatenate(early_gains + late_gains).reshape(devices, gain_len)
     gain_table = jnp.pad(gain_table.astype(jnp.bfloat16), ((0, 0), (0, pad)))
     gain_table = gain_table.reshape(devices, tail_rows, LANES)
@@ -635,14 +680,18 @@
     ffn_chunks = merged_blocks(ffn_chunks, ffn_came)
     ffn_came = sent_blocks(ffn_chunks, ffn_orders, 1, devices)
     attn_came = across(attn_away, 0, devices)
-    attn_came, ffn_came = lax.optimization_barrier((attn_came, ffn_came))
+    ffn_came[0], attn_came = lax.optimization_barrier((ffn_came[0], attn_came))
     attn_chunks = cores_merged(attn_home, attn_came, attn_parts)
-    for stage in range(stages):
-        attn_came = sent_blocks(attn_chunks, attn_orders, stage, devices)
-        if stage < stages - 1:
+    for stage in range(1, stages + 1):
+        attn_came = sent_blocks(attn_chunks, attn_orders, stage - 1, devices)
+        if stage < stages:
             ffn_chunks = merged_blocks(ffn_chunks, ffn_came)
-        ffn_came = sent_blocks(ffn_chunks, ffn_orders, stage + 2, devices) if stage + 2 < stages else []
-        ffn_came, attn_came = lax.optimization_barrier((ffn_came, attn_came))
+        if stage + 1 < stages:
+            ffn_came = sent_blocks(ffn_chunks, ffn_orders, stage + 1, devices)
+            for chunk, arrived in enumerate(attn_came):
+                ffn_came[chunk], attn_came[chunk] = lax.optimization_barrier(
+                    (ffn_came[chunk], arrived)
+                )
         attn_chunks = merged_blocks(attn_chunks, attn_came)
     attn_shard = jnp.concatenate([rows for rows, _ in attn_chunks]).reshape(-1)
     ffn_shard = jnp.concatenate([rows for rows, _ in ffn_chunks])

time: 218 us -> 230 us (1.055)
  local copies, waits for them, and re-layouts: 8.77 us -> 36.3 us
  waiting for transfers between devices: 73.2 us -> 85 us
  Pallas kernels: 40.4 us -> 29.3 us
  starting transfers between devices: 46.4 us -> 36.2 us
  other arithmetic: 34.2 us -> 29.6 us
    unnamed x162 -> x120, local copies, waits for them, and re-layouts: 7.26 us -> 30.2 us
    pallas_call x2, Pallas kernels: 22.9 us -> 10.2 us  [grad_blocks(): pl.pallas_call(functools.partial(grads_kernel, plan, sizes, tails is not...]
    ppermute x40, waiting for transfers between devices: 73.2 us -> 85 us  [across(): lax.ppermute(block, 'dp', [(i, i ^ 1 << bit) for i in range(devices)])]
    ppermute x40, starting transfers between devices: 46.4 us -> 36.2 us  [across(): lax.ppermute(block, 'dp', [(i, i ^ 1 << bit) for i in range(devices)])]
    pallas_call x0 -> x1, Pallas kernels: none -> 3.3 us  [attn_backward(): pl.pallas_call(attn_back_kernel, out_shape=shapes, in_specs=whole_specs(2...]
    dot_general x7 -> x3, matrix products: 6.55 us -> 4.07 us  [times_transposed(): lax.dot_general(rows_in, matrix, (((1,), (1,)), ((), ())), preferred_elem...]
  transfers between devices with their start and end apart: 40 -> 40, of which waited for: 24 -> 21; matrix products, arithmetic and copies ran while one was open for 12% -> 15% of each run, Pallas kernels for 7% -> 4%
where the time goes in v3:
time: 230 us; the launch traced here: 228 us
  waiting for transfers between devices  85 us (37%)
  local copies, waits for them, and re-layouts  36.3 us (16%)
  starting transfers between devices  36.2 us (16%)
  other arithmetic  29.6 us (13%)
  Pallas kernels  29.3 us (13%)
  matrix products  10.4 us (5%)
    ppermute x40, waiting for transfers between devices, across(): lax.ppermute(block, 'dp', [(i, i ^ 1 << bit) for i in range(devices)])  85 us
    ppermute x40, starting transfers between devices, across(): lax.ppermute(block, 'dp', [(i, i ^ 1 << bit) for i in range(devices)])  36.2 us
    unnamed x120, local copies, waits for them, and re-layouts  30.2 us
    pallas_call x2, Pallas kernels, unpack_matrices(): pl.pallas_call(functools.partial(unpack_kernel, plan, sizes, tail_rows, l...  15.9 us
    pallas_call x2, Pallas kernels, grad_blocks(): pl.pallas_call(functools.partial(grads_kernel, plan, sizes, tails is not...  10.2 us
    convert_element_type x2, other arithmetic, added(): (home[at].astype(jnp.float32) + came[at].astype(jnp.float32)).astype(jnp....  6.48 us
    concatenate x9, other arithmetic, gather_chunk(): held = jnp.concatenate([held, across(held, bit, devices)])  5.27 us
  transfers between devices with their start and end apart: 40, of which 21 were waited for; matrix products, arithmetic and copies ran while one was open for 15% of the time, Pallas kernels for 4%

profile of v3, /device:TPU:0, one launch (start us, length us, event | category | flops | bytes accessed | tf_op | source)
XLA Modules:
  0.0 228.4 jit_solution(11002810549172885524)
XLA Ops:
  2.5 3.0 %collective-permute-start = (bf16[1,416,128]{2,1,0:T(8,128)(2,1)S(1)}, bf16[1,416,128]{2,1,0:T(8,128)(2,1)S(1)}, u32[]{:S(2)}, u32[]{:S(2)}) collective-permute-start(bf16[1,416,128]{2,1,0:T(8,128)(2,1)S(1)} %bitcast.84), channel_id=1, source_target_pairs={{0,8},{1,9},{2,10},{3,11},{4,12},{5,13},{6,14},{7,15},{8,0},{9,1},... | collective-permute-start | bytes 319496 | tf_op jit(solution)/shard_map/ppermute | solution.py:220
  5.5 2.7 %collective-permute-start.6 = (bf16[1,480,128]{2,1,0:T(8,128)(2,1)S(1)}, bf16[1,480,128]{2,1,0:T(8,128)(2,1)S(1)}, u32[]{:S(2)}, u32[]{:S(2)}) collective-permute-start(bf16[1,480,128]{2,1,0:T(8,128)(2,1)S(1)} %get-tuple-element.149), channel_id=1, source_target_pairs={{0,16},{1,17},{2,18},{3,19},{4,20},{5,21},{6,22},{7,23},{8,24},{9,... | collective-permute-start | bytes 368648 | tf_op jit(solution)/shard_map/ppermute | solution.py:220
  8.5 4.0 %collective-permute-start.1 = (bf16[2,416,128]{2,1,0:T(8,128)(2,1)S(1)}, bf16[2,416,128]{2,1,0:T(8,128)(2,1)S(1)}, u32[]{:S(2)}, u32[]{:S(2)}) collective-permute-start(bf16[2,416,128]{2,1,0:T(8,128)(2,1)S(1)} %pad_maximum_fusion.10), channel_id=1, source_target_pairs={{0,16},{1,17},{2,18},{3,19},{4,20},{5,21},{6,22},{7,23},{8,24},{9,... | collective-permute-start | bytes 638984 | tf_op jit(solution)/shard_map/ppermute | solution.py:220
  12.5 9.4 %collective-permute-done.6 = bf16[1,480,128]{2,1,0:T(8,128)(2,1)S(1)} collective-permute-done((bf16[1,480,128]{2,1,0:T(8,128)(2,1)S(1)}, bf16[1,480,128]{2,1,0:T(8,128)(2,1)S(1)}, u32[]{:S(2)}, u32[]{:S(2)}) %collective-permute-start.6) | collective-permute-done | bytes 122912 | tf_op jit(solution)/shard_map/ppermute | solution.py:220
  23.7 2.8 %collective-permute-done.1 = bf16[2,416,128]{2,1,0:T(8,128)(2,1)S(1)} collective-permute-done((bf16[2,416,128]{2,1,0:T(8,128)(2,1)S(1)}, bf16[2,416,128]{2,1,0:T(8,128)(2,1)S(1)}, u32[]{:S(2)}, u32[]{:S(2)}) %collective-permute-start.1) | collective-permute-done | bytes 213024 | tf_op jit(solution)/shard_map/ppermute | solution.py:220
  31.5 5.8 %collective-permute-done.13 = bf16[2,480,128]{2,1,0:T(8,128)(2,1)S(1)} collective-permute-done((bf16[2,480,128]{2,1,0:T(8,128)(2,1)S(1)}, bf16[2,480,128]{2,1,0:T(8,128)(2,1)S(1)}, u32[]{:S(2)}, u32[]{:S(2)}) %collective-permute-start.13) | collective-permute-done | bytes 245792 | tf_op jit(solution)/shard_map/ppermute | solution.py:220
  39.5 8.4 %collective-permute-done.8 = bf16[4,480,128]{2,1,0:T(8,128)(2,1)} collective-permute-done((bf16[4,480,128]{2,1,0:T(8,128)(2,1)}, bf16[4,480,128]{2,1,0:T(8,128)(2,1)}, u32[]{:S(2)}, u32[]{:S(2)}) %collective-permute-start.8) | collective-permute-done | bytes 491552 | tf_op jit(solution)/shard_map/ppermute | solution.py:220
  53.6 10.7 %collective-permute-done.3.refs_1_ = bf16[8,416,128]{2,1,0:T(8,128)(2,1)S(1)} collective-permute-done((bf16[8,416,128]{2,1,0:T(8,128)(2,1)S(1)}, bf16[8,416,128]{2,1,0:T(8,128)(2,1)S(1)}, u32[]{:S(2)}, u32[]{:S(2)}) %collective-permute-start.3) | collective-permute-done | bytes 852000 | tf_op jit(solution)/shard_map/ppermute | solution.py:220
  68.1 2.6 %collective-permute-done.9.refs_1_ = bf16[8,480,128]{2,1,0:T(8,128)(2,1)} collective-permute-done((bf16[8,480,128]{2,1,0:T(8,128)(2,1)}, bf16[8,480,128]{2,1,0:T(8,128)(2,1)}, u32[]{:S(2)}, u32[]{:S(2)}) %collective-permute-start.9) | collective-permute-done | bytes 983072 | tf_op jit(solution)/shard_map/ppermute | solution.py:220
  75.1 3.8 %shard_map.118 = (bf16[640,1024]{1,0:T(8,128)(2,1)S(1)}, bf16[640,256]{1,0:T(8,128)(2,1)S(1)}, bf16[640,256]{1,0:T(8,128)(2,1)S(1)}, bf16[1024,640]{1,0:T(8,128)(2,1)}, bf16[32,16,128]{2,1,0:T(8,128)(2,1)S(1)}) custom-call(s32[1]{0:T(128)} %bitcast.1.device_ref, bf16[8,416,128]{2,1,0:T(8,128)(2,1)S(1)} %pad_maximum_fusion.2.refs_0_, ...), custom_call_target="tpu_custom_call" | custom-call | tf_op jit(solution)/shard_map/pallas_call | solution.py:324
  88.2 12.1 %shard_map.119 = (bf16[640,2048]{1,0:T(8,128)(2,1)}, bf16[640,2048]{1,0:T(8,128)(2,1)}, bf16[2048,640]{1,0:T(8,128)(2,1)}) custom-call(s32[1]{0:T(128)} %bitcast.1.device_ref, bf16[8,480,128]{2,1,0:T(8,128)(2,1)} %pad_maximum_fusion.refs_0_, bf16[8,480,128]{2,1,0:T(8,128)(2,1)} %collective-permute-done.9.refs_1_, ...), custom_call_target="tpu_custom_call" | custom-call | tf_op jit(solution)/shard_map/pallas_call | solution.py:324
  100.3 2.5 %fusion.45 = f32[128,2048]{1,0:T(8,128)S(1)} fusion(bf16[128,640]{1,0:T(8,128)(2,1)S(1)} %multiply_convert_fusion.2.refs_0_.refs_2_, bf16[640,2048]{1,0:T(8,128)(2,1)} %get-tuple-element.57), kind=kOutput, calls=%fused_computation.182 | convolution fusion | flops 335544320 | bytes 3833856 | tf_op jit(solution)/shard_map/dot_general | solution.py:508
  109.4 7.9 %shard_map.120 = (bf16[16,960,128]{2,1,0:T(8,128)(2,1)S(1)}, bf16[16,960,128]{2,1,0:T(8,128)(2,1)}) custom-call(s32[1]{0:T(128)} %bitcast.1.device_ref, bf16[128,640]{1,0:T(8,128)(2,1)S(1)} %multiply_convert_fusion.2.refs_0_.refs_2_, bf16[128,2048]{1,0:T(8,128)(2,1)S(1)} %get-tuple-element.124.refs_1_, ...), custom_call_target="tpu_custom_call" | custom-call | tf_op jit(solution)/shard_map/pallas_call | solution.py:381
  124.0 2.6 %collective-permute-done.18 = bf16[16,960,128]{2,1,0:T(8,128)(2,1)} collective-permute-done((bf16[16,960,128]{2,1,0:T(8,128)(2,1)}, bf16[16,960,128]{2,1,0:T(8,128)(2,1)}, u32[]{:S(2)}, u32[]{:S(2)}) %collective-permute-start.18) | collective-permute-done | bytes 3932192 | tf_op jit(solution)/shard_map/ppermute | solution.py:220
  126.6 6.0 %add_convert_fusion = (bf16[8,320,128]{2,1,0:T(8,128)(2,1)}, bf16[8,320,128]{2,1,0:T(8,128)(2,1)}, bf16[8,320,128]{2,1,0:T(8,128)(2,1)}, bf16[8,320,128]{2,1,0:T...) fusion(bf16[16,960,128]{2,1,0:T(8,128)(2,1)} %collective-permute-done.18, ...), kind=kLoop, calls=%fused_computation.2 | loop fusion | flops 7864320 | bytes 11796480 | tf_op jit(solution)/shard_map/convert_element_type | solution.py:465
  148.6 3.3 %shard_map.121 = (f32[128,640]{1,0:T(8,128)}, bf16[128,1024]{1,0:T(8,128)(2,1)S(1)}, bf16[128,256]{1,0:T(8,128)(2,1)S(1)}, bf16[128,256]{1,0:T(8,128)(2,1)S(1)},...) custom-call(bf16[128,640]{1,0:T(8,128)(2,1)S(1)} %copy-done.7, ...), custom_call_target="tpu_custom_call" | custom-call | tf_op jit(solution)/shard_map/pallas_call | solution.py:579
  174.9 5.7 %collective-permute-done.37 = bf16[4,320,128]{2,1,0:T(8,128)(2,1)S(1)} collective-permute-done((bf16[4,320,128]{2,1,0:T(8,128)(2,1)S(1)}, bf16[4,320,128]{2,1,0:T(8,128)(2,1)S(1)}, u32[]{:S(2)}, u32[]{:S(2)}) %collective-permute-start.37) | collective-permute-done | bytes 327712 | tf_op jit(solution)/shard_map/ppermute | solution.py:220
  182.6 3.9 %collective-permute-done.38 = bf16[2,320,128]{2,1,0:T(8,128)(2,1)S(1)} collective-permute-done((bf16[2,320,128]{2,1,0:T(8,128)(2,1)S(1)}, bf16[2,320,128]{2,1,0:T(8,128)(2,1)S(1)}, u32[]{:S(2)}, u32[]{:S(2)}) %collective-permute-start.38) | collective-permute-done | bytes 163872 | tf_op jit(solution)/shard_map/ppermute | solution.py:220
  190.8 6.2 %collective-permute-done.39 = bf16[1,320,128]{2,1,0:T(8,128)(2,1)S(1)} collective-permute-done((bf16[1,320,128]{2,1,0:T(8,128)(2,1)S(1)}, bf16[1,320,128]{2,1,0:T(8,128)(2,1)S(1)}, u32[]{:S(2)}, u32[]{:S(2)}) %collective-permute-start.39) | collective-permute-done | bytes 81952 | tf_op jit(solution)/shard_map/ppermute | solution.py:220
  201.6 6.7 %collective-permute-done.32 = bf16[8,208,128]{2,1,0:T(8,128)(2,1)S(1)} collective-permute-done((bf16[8,208,128]{2,1,0:T(8,128)(2,1)S(1)}, bf16[8,208,128]{2,1,0:T(8,128)(2,1)S(1)}, u32[]{:S(2)}, u32[]{:S(2)}) %collective-permute-start.32) | collective-permute-done | bytes 426016 | tf_op jit(solution)/shard_map/ppermute | solution.py:220
  208.7 2.8 %collective-permute-done.26 = bf16[1,320,128]{2,1,0:T(8,128)(2,1)S(1)} collective-permute-done((bf16[1,320,128]{2,1,0:T(8,128)(2,1)S(1)}, bf16[1,320,128]{2,1,0:T(8,128)(2,1)S(1)}, u32[]{:S(2)}, u32[]{:S(2)}) %collective-permute-start.26) | collective-permute-done | bytes 81952 | tf_op jit(solution)/shard_map/ppermute | solution.py:220
  212.0 4.5 %collective-permute-done.33 = bf16[1,320,128]{2,1,0:T(8,128)(2,1)S(1)} collective-permute-done((bf16[1,320,128]{2,1,0:T(8,128)(2,1)S(1)}, bf16[1,320,128]{2,1,0:T(8,128)(2,1)S(1)}, u32[]{:S(2)}, u32[]{:S(2)}) %collective-permute-start.33) | collective-permute-done | bytes 81952 | tf_op jit(solution)/shard_map/ppermute | solution.py:220
  219.8 2.5 %collective-permute-done.35 = bf16[2,208,128]{2,1,0:T(8,128)(2,1)S(1)} collective-permute-done((bf16[2,208,128]{2,1,0:T(8,128)(2,1)S(1)}, bf16[2,208,128]{2,1,0:T(8,128)(2,1)S(1)}, u32[]{:S(2)}, u32[]{:S(2)}) %collective-permute-start.35) | collective-permute-done | bytes 106528 | tf_op jit(solution)/shard_map/ppermute | solution.py:220
  223.8 2.7 %collective-permute-done.36 = bf16[1,208,128]{2,1,0:T(8,128)(2,1)S(1)} collective-permute-done((bf16[1,208,128]{2,1,0:T(8,128)(2,1)S(1)}, bf16[1,208,128]{2,1,0:T(8,128)(2,1)S(1)}, u32[]{:S(2)}, u32[]{:S(2)}) %collective-permute-start.36) | collective-permute-done | bytes 53280 | tf_op jit(solution)/shard_map/ppermute | solution.py:220
  (288 shorter events, 104.3 us)
Async XLA Ops:
  5.5 16.4 %collective-permute-start.6 = (bf16[1,480,128]{2,1,0:T(8,128)(2,1)S(1)}, bf16[1,480,128]{2,1,0:T(8,128)(2,1)S(1)}, u32[]{:S(2)}, u32[]{:S(2)}) collective-permute-start(bf16[1,480,128]{2,1,0:T(8,128)(2,1)S(1)} %get-tuple-element.149), channel_id=1, source_target_pairs={{0,16},{1,17},{2,18},{3,19},{4,20},{5,21},{6,22},{7,23},{8,24},{9,... | collective-permute-start | bytes 368648 | tf_op jit(solution)/shard_map/ppermute | solution.py:220
  8.5 18.0 %collective-permute-start.1 = (bf16[2,416,128]{2,1,0:T(8,128)(2,1)S(1)}, bf16[2,416,128]{2,1,0:T(8,128)(2,1)S(1)}, u32[]{:S(2)}, u32[]{:S(2)}) collective-permute-start(bf16[2,416,128]{2,1,0:T(8,128)(2,1)S(1)} %pad_maximum_fusion.10), channel_id=1, source_target_pairs={{0,16},{1,17},{2,18},{3,19},{4,20},{5,21},{6,22},{7,23},{8,24},{9,... | collective-permute-start | bytes 638984 | tf_op jit(solution)/shard_map/ppermute | solution.py:220
  12.5 15.8 %collective-permute-start.12 = (bf16[1,480,128]{2,1,0:T(8,128)(2,1)S(1)}, bf16[1,480,128]{2,1,0:T(8,128)(2,1)S(1)}, u32[]{:S(2)}, u32[]{:S(2)}) collective-permute-start(bf16[1,480,128]{2,1,0:T(8,128)(2,1)S(1)} %get-tuple-element.148), channel_id=1, source_target_pairs={{0,16},{1,17},{2,18},{3,19},{4,20},{5,21},{6,22},{7,23},{8,24},{9,... | collective-permute-start | bytes 368648 | tf_op jit(solution)/shard_map/ppermute | solution.py:220
  26.5 10.9 %collective-permute-start.2 = (bf16[4,416,128]{2,1,0:T(8,128)(2,1)S(1)}, bf16[4,416,128]{2,1,0:T(8,128)(2,1)S(1)}, u32[]{:S(2)}, u32[]{:S(2)}) collective-permute-start(bf16[4,416,128]{2,1,0:T(8,128)(2,1)S(1)} %pad_maximum_fusion.6), channel_id=1, source_target_pairs={{0,2},{1,3},{2,0},{3,1},{4,6},{5,7},{6,4},{7,5},{8,10},{9,11},{10,... | collective-permute-start | bytes 1277960 | tf_op jit(solution)/shard_map/ppermute | solution.py:220
  30.8 17.2 %collective-permute-start.8 = (bf16[4,480,128]{2,1,0:T(8,128)(2,1)}, bf16[4,480,128]{2,1,0:T(8,128)(2,1)}, u32[]{:S(2)}, u32[]{:S(2)}) collective-permute-start(bf16[4,480,128]{2,1,0:T(8,128)(2,1)} %pad_maximum_fusion.4), channel_id=1, source_target_pairs={{0,4},{1,5},{2,6},{3,7},{4,0},{5,1},{6,2},{7,3},{8,12},{9,13},{10,... | collective-permute-start | bytes 1474568 | tf_op jit(solution)/shard_map/ppermute | solution.py:220
  37.4 12.7 %collective-permute-start.14 = (bf16[4,480,128]{2,1,0:T(8,128)(2,1)S(1)}, bf16[4,480,128]{2,1,0:T(8,128)(2,1)}, u32[]{:S(2)}, u32[]{:S(2)}) collective-permute-start(bf16[4,480,128]{2,1,0:T(8,128)(2,1)S(1)} %pad_maximum_fusion.5), channel_id=1, source_target_pairs={{0,8},{1,9},{2,10},{3,11},{4,12},{5,13},{6,14},{7,15},{8,0},{9,1},... | collective-permute-start | bytes 1474568 | tf_op jit(solution)/shard_map/ppermute | solution.py:220
  37.6 26.8 %collective-permute-start.3 = (bf16[8,416,128]{2,1,0:T(8,128)(2,1)S(1)}, bf16[8,416,128]{2,1,0:T(8,128)(2,1)S(1)}, u32[]{:S(2)}, u32[]{:S(2)}) collective-permute-start(bf16[8,416,128]{2,1,0:T(8,128)(2,1)S(1)} %pad_maximum_fusion.2.refs_0_), channel_id=1, source_target_pairs={{0,4},{1,5},{2,6},{3,7},{4,0},{5,1},{6,2},{7,3},{8,12},{9,13},{10,... | collective-permute-start | bytes 2555912 | tf_op jit(solution)/shard_map/ppermute | solution.py:220
  50.1 20.6 %collective-permute-start.9 = (bf16[8,480,128]{2,1,0:T(8,128)(2,1)}, bf16[8,480,128]{2,1,0:T(8,128)(2,1)}, u32[]{:S(2)}, u32[]{:S(2)}) collective-permute-start(bf16[8,480,128]{2,1,0:T(8,128)(2,1)} %pad_maximum_fusion.refs_0_), channel_id=1, source_target_pairs={{0,8},{1,9},{2,10},{3,11},{4,12},{5,13},{6,14},{7,15},{8,0},{9,1},... | collective-permute-start | bytes 2949128 | tf_op jit(solution)/shard_map/ppermute | solution.py:220
  52.1 20.6 %collective-permute-start.15 = (bf16[8,480,128]{2,1,0:T(8,128)(2,1)}, bf16[8,480,128]{2,1,0:T(8,128)(2,1)}, u32[]{:S(2)}, u32[]{:S(2)}) collective-permute-start(bf16[8,480,128]{2,1,0:T(8,128)(2,1)} %pad_maximum_fusion.1.refs_4_), channel_id=1, source_target_pairs={{0,2},{1,3},{2,0},{3,1},{4,6},{5,7},{6,4},{7,5},{8,10},{9,11},{10,... | collective-permute-start | bytes 2949128 | tf_op jit(solution)/shard_map/ppermute | solution.py:220
  53.6 13.5 %collective-permute-start.4 = (bf16[8,416,128]{2,1,0:T(8,128)(2,1)S(1)}, bf16[8,416,128]{2,1,0:T(8,128)(2,1)S(1)}, u32[]{:S(2)}, u32[]{:S(2)}) collective-permute-start(bf16[8,416,128]{2,1,0:T(8,128)(2,1)S(1)} %pad_maximum_fusion.2.refs_0_), channel_id=1, source_target_pairs={{0,1},{1,0},{2,3},{3,2},{4,5},{5,4},{6,7},{7,6},{8,9},{9,8},{10,11... | collective-permute-start | bytes 2555912 | tf_op jit(solution)/shard_map/ppermute | solution.py:220
  66.6 21.6 %collective-permute-start.10 = (bf16[8,480,128]{2,1,0:T(8,128)(2,1)}, bf16[8,480,128]{2,1,0:T(8,128)(2,1)}, u32[]{:S(2)}, u32[]{:S(2)}) collective-permute-start(bf16[8,480,128]{2,1,0:T(8,128)(2,1)} %pad_maximum_fusion.refs_0_), channel_id=1, source_target_pairs={{0,1},{1,0},{2,3},{3,2},{4,5},{5,4},{6,7},{7,6},{8,9},{9,8},{10,11... | collective-permute-start | bytes 2949128 | tf_op jit(solution)/shard_map/ppermute | solution.py:220
  68.1 20.1 %collective-permute-start.16 = (bf16[8,480,128]{2,1,0:T(8,128)(2,1)}, bf16[8,480,128]{2,1,0:T(8,128)(2,1)}, u32[]{:S(2)}, u32[]{:S(2)}) collective-permute-start(bf16[8,480,128]{2,1,0:T(8,128)(2,1)} %pad_maximum_fusion.1.refs_4_), channel_id=1, source_target_pairs={{0,1},{1,0},{2,3},{3,2},{4,5},{5,4},{6,7},{7,6},{8,9},{9,8},{10,11... | collective-permute-start | bytes 2949128 | tf_op jit(solution)/shard_map/ppermute | solution.py:220
  70.7 17.5 %collective-permute-start.11 = (bf16[8,480,128]{2,1,0:T(8,128)(2,1)}, bf16[8,480,128]{2,1,0:T(8,128)(2,1)}, u32[]{:S(2)}, u32[]{:S(2)}) collective-permute-start(bf16[8,480,128]{2,1,0:T(8,128)(2,1)} %collective-permute-done.9.refs_1_), channel_id=1, source_target_pairs={{0,1},{1,0},{2,3},{3,2},{4,5},{5,4},{6,7},{7,6},{8,9},{9,8},{10,11... | collective-permute-start | bytes 2949128 | tf_op jit(solution)/shard_map/ppermute | solution.py:220
  72.8 15.4 %collective-permute-start.17 = (bf16[8,480,128]{2,1,0:T(8,128)(2,1)}, bf16[8,480,128]{2,1,0:T(8,128)(2,1)}, u32[]{:S(2)}, u32[]{:S(2)}) collective-permute-start(bf16[8,480,128]{2,1,0:T(8,128)(2,1)} %collective-permute-done.15.refs_5_), channel_id=1, source_target_pairs={{0,1},{1,0},{2,3},{3,2},{4,5},{5,4},{6,7},{7,6},{8,9},{9,8},{10,11... | collective-permute-start | bytes 2949128 | tf_op jit(solution)/shard_map/ppermute | solution.py:220
  132.7 36.2 %collective-permute-start.19 = (bf16[8,320,128]{2,1,0:T(8,128)(2,1)}, bf16[8,320,128]{2,1,0:T(8,128)(2,1)}, u32[]{:S(2)}, u32[]{:S(2)}) collective-permute-start(bf16[8,320,128]{2,1,0:T(8,128)(2,1)} %get-tuple-element.77), channel_id=1, source_target_pairs={{0,2},{1,3},{2,0},{3,1},{4,6},{5,7},{6,4},{7,5},{8,10},{9,11},{10,... | collective-permute-start | bytes 1966088 | tf_op jit(solution)/shard_map/ppermute | solution.py:220
  133.8 35.1 %collective-permute-start.20 = (bf16[8,320,128]{2,1,0:T(8,128)(2,1)}, bf16[8,320,128]{2,1,0:T(8,128)(2,1)}, u32[]{:S(2)}, u32[]{:S(2)}) collective-permute-start(bf16[8,320,128]{2,1,0:T(8,128)(2,1)} %get-tuple-element.78), channel_id=1, source_target_pairs={{0,4},{1,5},{2,6},{3,7},{4,0},{5,1},{6,2},{7,3},{8,12},{9,13},{10,... | collective-permute-start | bytes 1966088 | tf_op jit(solution)/shard_map/ppermute | solution.py:220
  135.3 33.6 %collective-permute-start.21 = (bf16[8,320,128]{2,1,0:T(8,128)(2,1)}, bf16[8,320,128]{2,1,0:T(8,128)(2,1)}, u32[]{:S(2)}, u32[]{:S(2)}) collective-permute-start(bf16[8,320,128]{2,1,0:T(8,128)(2,1)} %get-tuple-element.79), channel_id=1, source_target_pairs={{0,8},{1,9},{2,10},{3,11},{4,12},{5,13},{6,14},{7,15},{8,0},{9,1},... | collective-permute-start | bytes 1966088 | tf_op jit(solution)/shard_map/ppermute | solution.py:220
  168.9 18.8 %collective-permute-start.23 = (bf16[16,416,128]{2,1,0:T(8,128)(2,1)S(1)}, bf16[16,416,128]{2,1,0:T(8,128)(2,1)S(1)}, u32[]{:S(2)}, u32[]{:S(2)}) collective-permute-start(bf16[16,416,128]{2,1,0:T(8,128)(2,1)S(1)} %get-tuple-element.83), channel_id=1, source_target_pairs={{0,1},{1,0},{2,3},{3,2},{4,5},{5,4},{6,7},{7,6},{8,9},{9,8},{10,11... | collective-permute-start | bytes 5111816 | tf_op jit(solution)/shard_map/ppermute | solution.py:220
  174.5 13.2 %collective-permute-start.22 = (bf16[4,320,128]{2,1,0:T(8,128)(2,1)S(1)}, bf16[4,320,128]{2,1,0:T(8,128)(2,1)S(1)}, u32[]{:S(2)}, u32[]{:S(2)}) collective-permute-start(bf16[4,320,128]{2,1,0:T(8,128)(2,1)S(1)} %get-tuple-element.129), channel_id=1, source_target_pairs={{0,8},{1,9},{2,10},{3,11},{4,12},{5,13},{6,14},{7,15},{8,0},{9,1},... | collective-permute-start | bytes 983048 | tf_op jit(solution)/shard_map/ppermute | solution.py:220
  182.2 19.4 %collective-permute-start.31 = (bf16[2,320,128]{2,1,0:T(8,128)(2,1)S(1)}, bf16[2,320,128]{2,1,0:T(8,128)(2,1)S(1)}, u32[]{:S(2)}, u32[]{:S(2)}) collective-permute-start(bf16[2,320,128]{2,1,0:T(8,128)(2,1)S(1)} %get-tuple-element.141), channel_id=1, source_target_pairs={{0,8},{1,9},{2,10},{3,11},{4,12},{5,13},{6,14},{7,15},{8,0},{9,1},... | collective-permute-start | bytes 491528 | tf_op jit(solution)/shard_map/ppermute | solution.py:220
  188.2 11.1 %collective-permute-start.25 = (bf16[8,208,128]{2,1,0:T(8,128)(2,1)S(1)}, bf16[8,208,128]{2,1,0:T(8,128)(2,1)S(1)}, u32[]{:S(2)}, u32[]{:S(2)}) collective-permute-start(bf16[8,208,128]{2,1,0:T(8,128)(2,1)S(1)} %get-tuple-element.120), channel_id=1, source_target_pairs={{0,2},{1,3},{2,0},{3,1},{4,6},{5,7},{6,4},{7,5},{8,10},{9,11},{10,... | collective-permute-start | bytes 1277960 | tf_op jit(solution)/shard_map/ppermute | solution.py:220
  197.0 11.4 %collective-permute-start.32 = (bf16[8,208,128]{2,1,0:T(8,128)(2,1)S(1)}, bf16[8,208,128]{2,1,0:T(8,128)(2,1)S(1)}, u32[]{:S(2)}, u32[]{:S(2)}) collective-permute-start(bf16[8,208,128]{2,1,0:T(8,128)(2,1)S(1)} %get-tuple-element.121), channel_id=1, source_target_pairs={{0,4},{1,5},{2,6},{3,7},{4,0},{5,1},{6,2},{7,3},{8,12},{9,13},{10,... | collective-permute-start | bytes 1277960 | tf_op jit(solution)/shard_map/ppermute | solution.py:220
  199.4 12.1 %collective-permute-start.27 = (bf16[4,208,128]{2,1,0:T(8,128)(2,1)S(1)}, bf16[4,208,128]{2,1,0:T(8,128)(2,1)S(1)}, u32[]{:S(2)}, u32[]{:S(2)}) collective-permute-start(bf16[4,208,128]{2,1,0:T(8,128)(2,1)S(1)} %get-tuple-element.132), channel_id=1, source_target_pairs={{0,4},{1,5},{2,6},{3,7},{4,0},{5,1},{6,2},{7,3},{8,12},{9,13},{10,... | collective-permute-start | bytes 638984 | tf_op jit(solution)/shard_map/ppermute | solution.py:220
  200.3 11.2 %collective-permute-start.26 = (bf16[1,320,128]{2,1,0:T(8,128)(2,1)S(1)}, bf16[1,320,128]{2,1,0:T(8,128)(2,1)S(1)}, u32[]{:S(2)}, u32[]{:S(2)}) collective-permute-start(bf16[1,320,128]{2,1,0:T(8,128)(2,1)S(1)} %add_convert_fusion.36), channel_id=1, source_target_pairs={{0,4},{1,5},{2,6},{3,7},{4,0},{5,1},{6,2},{7,3},{8,12},{9,13},{10,... | collective-permute-start | bytes 245768 | tf_op jit(solution)/shard_map/ppermute | solution.py:220
  (72 other events, 376.1 us)

commit v4 on v3

v4 whole, which is shorter than its diff:
```python
import functools
import math

import jax
import jax.numpy as jnp
from jax import lax
from jax.experimental import pallas as pl
from jax.experimental.pallas import tpu as pltpu
from jax.sharding import PartitionSpec as P

D = 640
FF = 2048
HD = 256
HQ = 1024
CAP = 128
WINDOW = 64
STEP = 3
G1LEN = 1638400
G2LEN = 3932160
LANES = 128
ROWS = 16
GELU_SCALE = math.sqrt(2 / math.pi)


def rms_scale(values, gain_vec):
    return (
        values
        * lax.rsqrt(jnp.mean(values * values, axis=-1, keepdims=True) + 1e-06)
        * (1.0 + gain_vec)
    )


def rotate(values, cos_tab, sin_tab):
    half_dim = values.shape[-1] // 2
    lower_half = values[..., :half_dim]
    upper_half = values[..., half_dim:]
    return jnp.concatenate(
        [lower_half * cos_tab - upper_half * sin_tab, upper_half * cos_tab + lower_half * sin_tab],
        axis=-1,
    )


def gated_gelu(gate_proj, up_proj):
    return jax.nn.gelu(gate_proj, approximate=True) * up_proj


def times_transposed(rows_in, matrix):
    return lax.dot_general(
        rows_in, matrix, (((1,), (1,)), ((), ())), preferred_element_type=jnp.float32
    )


def slot_setup(seq_lengths, seq_owner, device):
    mine_mask = seq_owner == device
    own_lengths = jnp.where(mine_mask, seq_lengths, 0)
    seq_ends = jnp.cumsum(own_lengths, dtype=jnp.int32)
    seq_begins = seq_ends - own_lengths
    slot_index = jnp.arange(CAP, dtype=jnp.int32)
    column = slot_index[:, None]
    inside_mask = (
        mine_mask[None, :] & (seq_begins[None, :] <= column) & (column < seq_ends[None, :])
    )
    live_mask = jnp.any(inside_mask, axis=1)
    seq_label = jnp.sum(
        (mine_mask[None, :] & (seq_ends[None, :] <= column)).astype(jnp.int32),
        axis=1,
        dtype=jnp.int32,
    )
    position = jnp.sum(
        jnp.where(inside_mask, column - seq_begins[None, :], 0), axis=1, dtype=jnp.int32
    )
    row_slot = slot_index[:, None]
    col_slot = slot_index[None, :]
    allowed = live_mask[:, None] & live_mask[None, :] & (
        seq_label[:, None] == seq_label[None, :]
    ) & (col_slot <= row_slot) & (row_slot - col_slot < WINDOW) | (row_slot == col_slot)
    half_dim = HD // 2
    frequency = 10000.0 ** (-2.0 * jnp.arange(half_dim, dtype=jnp.float32) / HD)
    angles = position.astype(jnp.float32)[:, None] * frequency[None, :]
    live_wide = jnp.broadcast_to(live_mask[:, None], (CAP, LANES)).astype(jnp.float32)
    return jnp.concatenate(
        [jnp.cos(angles), jnp.sin(angles), allowed.astype(jnp.float32), live_wide], axis=1
    )


def rms_pull(raw, gain_vec, delta):
    scale = lax.rsqrt(jnp.mean(raw * raw, axis=-1, keepdims=True) + 1e-06)
    weighed = delta * (1.0 + gain_vec)
    shared = jnp.mean(raw * weighed, axis=-1, keepdims=True)
    return scale * weighed - raw * (scale * scale * scale * shared), delta * raw * scale


def rotate_pull(delta, cos_tab, sin_tab):
    half_dim = delta.shape[-1] // 2
    lower_half = delta[:, :half_dim]
    upper_half = delta[:, half_dim:]
    return jnp.concatenate(
        [lower_half * cos_tab + upper_half * sin_tab, upper_half * cos_tab - lower_half * sin_tab],
        axis=-1,
    )


def bit_orders(devices, tuned):
    bits = devices.bit_length() - 1
    if bits == 5:
        return [["cxyab".index(letter) for letter in order] for order in tuned]
    return [[1 + (shift + step) % (bits - 1) for step in range(bits - 1)] for shift in range(3)]


def across(block, bit, devices):
    return lax.ppermute(block, "dp", [(i, i ^ (1 << bit)) for i in range(devices)])


def offset_of(place, order):
    return sum(((place >> k) & 1) << bit for k, bit in enumerate(order))


def gather_chunk(piece, order, devices):
    held = piece[None]
    for bit in order[:-1]:
        held = jnp.concatenate([held, across(held, bit, devices)])
    last = across(held, order[-1], devices)
    return (held, last, across(held, 0, devices), across(last, 0, devices))


def sent_blocks(chunks, orders, stage, devices):
    return [
        across(away, order[stage], devices)
        for (_, away), order in zip(chunks, orders)
    ]


def merged_blocks(chunks, came):
    merged = []
    for (home, _), arrived in zip(chunks, came):
        half = home.shape[0] // 2

        def added(low, high):
            return home[low:high].astype(jnp.float32) + arrived[low:high].astype(jnp.float32)

        if half:
            merged.append(
                (
                    added(0, half).astype(jnp.bfloat16),
                    added(half, 2 * half).astype(jnp.bfloat16),
                )
            )
        else:
            merged.append((added(0, 1)[0], None))
    return merged


def cut_rows(rows, parts):
    each = -(-rows // (parts * ROWS)) * ROWS
    return [(low, min(low + each, rows)) for low in range(0, rows, each)]


def whole_specs(count):
    return [pl.BlockSpec(memory_space=pltpu.VMEM)] * count


def copy_step(rows):
    return max(step for step in range(ROWS, 513, ROWS) if rows % step == 0)


def owner_rows(device, index, order, extra, start, each):
    owner = device ^ extra
    for k, bit in enumerate(order):
        owner = owner ^ (((index >> k) & 1) << bit)
    return owner, pl.multiple_of(owner * each + start, ROWS)


def spread_blocks(plan, views, device, spread, tails):
    for (order, extra, take, start, each), (block_ref, first_index, count, first_row) in zip(
        plan, views
    ):
        step = copy_step(take)

        @pl.loop(0, count)
        def _(
            index,
            order=order,
            extra=extra,
            take=take,
            start=start,
            each=each,
            block_ref=block_ref,
            first_index=first_index,
            first_row=first_row,
            step=step,
        ):
            owner, first = owner_rows(device, index, order, extra, start, each)
            for low in range(0, take, step):
                spread[pl.ds(pl.multiple_of(first + low, ROWS), step), :] = block_ref[
                    first_index + index, first_row + low : first_row + low + step, :
                ].astype(jnp.float32)
            if tails is not None:
                tails[owner] = block_ref[index, take : take + tails.shape[1], :]


def fold_matrices(spread, targets):
    first = 0
    for matrix, offset, rows, columns in targets:
        blocks = columns // LANES

        @pl.loop(0, rows // LANES)
        def _(step, matrix=matrix, offset=offset, blocks=blocks, first=first):
            base = pl.multiple_of(first + step * (LANES * blocks), ROWS)
            at = pl.ds(pl.multiple_of(step * LANES, LANES), LANES)
            for block in range(blocks):
                low = offset + block * LANES
                matrix[at, low : low + LANES] = spread[
                    pl.ds(base + block, LANES, stride=blocks), :
                ].astype(jnp.bfloat16)

        first += rows * blocks


def attn_unpack_kernel(plan, has_tails, device_ref, *refs):
    sources = refs[: len(plan)]
    qkv_weight, out_weight = refs[len(plan) : len(plan) + 2]
    tails = refs[len(plan) + 2] if has_tails else None
    spread = refs[-1]
    views = [(source, 0, source.shape[0], 0) for source in sources]
    spread_blocks(plan, views, device_ref[0], spread, tails)
    fold_matrices(
        spread,
        (
            (qkv_weight, 0, D, HQ),
            (qkv_weight, HQ, D, HD),
            (qkv_weight, HQ + HD, D, HD),
            (out_weight, 0, HQ, D),
        ),
    )


def unpack_attn(plan, tail_rows, device, arrays, devices):
    flat_rows = G1LEN // LANES
    shapes = [
        jax.ShapeDtypeStruct((D, HQ + 2 * HD), jnp.bfloat16),
        jax.ShapeDtypeStruct((HQ, D), jnp.bfloat16),
    ]
    if tail_rows:
        shapes.append(jax.ShapeDtypeStruct((devices, tail_rows, LANES), jnp.bfloat16))
    return pl.pallas_call(
        functools.partial(attn_unpack_kernel, plan, bool(tail_rows)),
        out_shape=shapes,
        in_specs=[pl.BlockSpec(memory_space=pltpu.SMEM)] + whole_specs(len(arrays)),
        out_specs=whole_specs(len(shapes)),
        scratch_shapes=[pltpu.VMEM((flat_rows, LANES), jnp.float32)],
        compiler_params=pltpu.CompilerParams(vmem_limit_bytes=16 << 20),
        cost_estimate=pl.CostEstimate(flops=0, bytes_accessed=0, transcendentals=0),
    )(device, *arrays)


def spread_grads(spread, products):
    first = 0
    for turned, right, columns in products:
        rows = turned.shape[0]
        blocks = columns // LANES
        wide = 2 - blocks % 2
        for block in range(0, blocks, wide):
            product = jnp.dot(
                turned,
                right(block * LANES, (block + wide) * LANES),
                preferred_element_type=jnp.float32,
            )
            for part in range(wide):
                spread[pl.ds(first + block + part, rows, stride=blocks), :] = product[
                    :, part * LANES : (part + 1) * LANES
                ]
        first += rows * blocks


def place_blocks(plan, device, spread, tails, targets):
    for target, order, extra, low, take, start, each in plan:
        target_ref = targets[target]
        step = copy_step(take)

        @pl.loop(0, target_ref.shape[0])
        def _(
            index,
            target_ref=target_ref,
            order=order,
            extra=extra,
            low=low,
            take=take,
            start=start,
            each=each,
            step=step,
        ):
            owner, first = owner_rows(device, index, order, extra, start or 0, each)
            if start is None:
                target_ref[index, low : low + take, :] = tails[owner].astype(jnp.bfloat16)
                return

            @pl.loop(0, take // step)
            def _(part):
                at = pl.multiple_of(part * step, ROWS)
                target_ref[index, pl.ds(pl.multiple_of(low + at, ROWS), step), :] = spread[
                    pl.ds(pl.multiple_of(first + at, ROWS), step), :
                ].astype(jnp.bfloat16)


def attn_forward(hidden_in, qkv_weight, tables, gains):
    cos_tab = tables[:, :LANES]
    sin_tab = tables[:, LANES : 2 * LANES]
    open_pairs = tables[:, 2 * LANES : 3 * LANES] > 0.0
    gain_query = gains[:, D : D + HD]
    gain_key = gains[:, D + HD : D + 2 * HD]
    normed_in = rms_scale(hidden_in[...].astype(jnp.float32), gains[:, :D]).astype(jnp.bfloat16)
    raw = jnp.dot(normed_in, qkv_weight[...], preferred_element_type=jnp.float32)
    key_raw = raw[:, HQ : HQ + HD]
    values = raw[:, HQ + HD :].astype(jnp.bfloat16)
    keys = rotate(rms_scale(key_raw, gain_key), cos_tab, sin_tab).astype(jnp.bfloat16)
    heads = []
    for head in range(HQ // HD):
        query_raw = raw[:, head * HD : (head + 1) * HD]
        rot_query = rotate(rms_scale(query_raw, gain_query), cos_tab, sin_tab) * HD ** (-0.5)
        rot_query = rot_query.astype(jnp.bfloat16)
        scores = jnp.where(open_pairs, times_transposed(rot_query, keys), -1e30)
        row_max = jnp.max(scores, axis=-1, keepdims=True)
        raised = jnp.exp(scores - row_max)
        summed = jnp.sum(raised, axis=-1, keepdims=True)
        context = jnp.dot(
            (raised / summed).astype(jnp.bfloat16), values, preferred_element_type=jnp.float32
        ).astype(jnp.bfloat16)
        heads.append((query_raw, rot_query, scores, row_max + jnp.log(summed), context))
    return normed_in, key_raw, values, keys, heads, cos_tab, sin_tab


def attn_forward_kernel(
    hidden_in, qkv_weight, out_weight, tables, gains, attn_out, mid_stream, context
):
    heads = attn_forward(hidden_in, qkv_weight, tables, gains)[4]
    for head, parts in enumerate(heads):
        context[:, head * HD : (head + 1) * HD] = parts[-1]
    out = jnp.dot(context[...], out_weight[...], preferred_element_type=jnp.float32)
    attn_out[...] = out
    gain_post = gains[:, D + 2 * HD : 2 * D + 2 * HD]
    mid_stream[...] = hidden_in[...].astype(jnp.float32) + rms_scale(out, gain_post)


def forward_attn(hidden_in, qkv_weight, out_weight, tables, gains):
    shapes = [jax.ShapeDtypeStruct((CAP, D), jnp.float32)] * 2
    return pl.pallas_call(
        attn_forward_kernel,
        out_shape=shapes,
        in_specs=whole_specs(5),
        out_specs=whole_specs(2),
        scratch_shapes=[pltpu.VMEM((CAP, HQ), jnp.bfloat16)],
        compiler_params=pltpu.CompilerParams(vmem_limit_bytes=12 << 20),
        cost_estimate=pl.CostEstimate(flops=0, bytes_accessed=0, transcendentals=0),
    )(hidden_in, qkv_weight, out_weight, tables, gains)


def ffn_kernel(
    plan_in,
    staged,
    plan_out,
    device_ref,
    mid_ref,
    attn_out,
    cotangent,
    tables,
    gains,
    *refs,
):
    sources = refs[: len(plan_in)]
    refs = refs[len(plan_in) :]
    block_out, delta_mid_ref, delta_attn_ref, late_gains = refs[:4]
    targets = refs[4:-10]
    spread, gate_weight, up_weight, down_weight = refs[-10:-6]
    gates, ups, hidden, delta_gate, delta_up, sems = refs[-6:]
    device = device_ref[0]
    copies, views = [], []
    for source, (target, first_index, first_row) in zip(sources, staged):
        count, rows = source.shape[:2]
        held = targets[target]
        copies.append(
            pltpu.make_async_copy(
                source,
                held.at[pl.ds(first_index, count), pl.ds(first_row, rows), :],
                sems.at[len(copies)],
            )
        )
        views.append((held, first_index, count, first_row))
    for copy in copies:
        copy.start()
    mid_stream = mid_ref[...]
    gain_post = gains[:, D + 2 * HD : 2 * D + 2 * HD]
    gain_mid = gains[:, 2 * D + 2 * HD : 3 * D + 2 * HD]
    gain_last = gains[:, 3 * D + 2 * HD :]
    normed_mid = rms_scale(mid_stream, gain_mid).astype(jnp.bfloat16)
    for copy, plan, view in zip(copies, plan_in, views):
        copy.wait()
        spread_blocks([plan], [view], device, spread, None)
    fold_matrices(
        spread, ((gate_weight, 0, D, FF), (up_weight, 0, D, FF), (down_weight, 0, FF, D))
    )
    parts = [slice(low, low + 512) for low in range(0, FF, 512)]
    for at in parts:
        gate = jnp.dot(normed_mid, gate_weight[:, at], preferred_element_type=jnp.float32)
        up = jnp.dot(normed_mid, up_weight[:, at], preferred_element_type=jnp.float32)
        gates[:, at] = gate
        ups[:, at] = up
        hidden[:, at] = gated_gelu(gate, up).astype(jnp.bfloat16)
    ffn_out = jnp.dot(hidden[...], down_weight[...], preferred_element_type=jnp.float32)
    block_out[...] = (mid_stream + rms_scale(ffn_out, gain_last)).astype(jnp.bfloat16)
    delta_out = cotangent[...].astype(jnp.float32) * tables[:, 3 * LANES : 3 * LANES + 1]
    delta_ffn, gain_rows = rms_pull(ffn_out, gain_last, delta_out)
    late_gains[2:3, :] = jnp.sum(gain_rows, axis=0, keepdims=True)
    delta_ffn = delta_ffn.astype(jnp.bfloat16)
    delta_normed = jnp.zeros((CAP, D), jnp.float32)
    for at in parts:
        delta_hidden = times_transposed(delta_ffn, down_weight[at, :])
        gate = gates[:, at]
        raised = jnp.tanh(GELU_SCALE * (gate + 0.044715 * (gate * gate * gate)))
        share = 0.5 * (1.0 + raised)
        slope = share + (0.5 * GELU_SCALE) * gate * (1.0 - raised * raised) * (
            1.0 + (3 * 0.044715) * (gate * gate)
        )
        delta_gate[:, at] = (delta_hidden * ups[:, at] * slope).astype(jnp.bfloat16)
        delta_up[:, at] = (delta_hidden * (gate * share)).astype(jnp.bfloat16)
        delta_normed += times_transposed(delta_gate[:, at], gate_weight[:, at])
        delta_normed += times_transposed(delta_up[:, at], up_weight[:, at])
    delta_part, gain_rows = rms_pull(mid_stream, gain_mid, delta_normed)
    late_gains[1:2, :] = jnp.sum(gain_rows, axis=0, keepdims=True)
    delta_mid = delta_out + delta_part
    delta_mid_ref[...] = delta_mid
    delta_attn, gain_rows = rms_pull(attn_out[...], gain_post, delta_mid)
    late_gains[0:1, :] = jnp.sum(gain_rows, axis=0, keepdims=True)
    delta_attn_ref[...] = delta_attn.astype(jnp.bfloat16)
    turned = normed_mid.T
    spread_grads(
        spread,
        (
            (turned, lambda low, high: delta_gate[:, low:high], FF),
            (turned, lambda low, high: delta_up[:, low:high], FF),
            (hidden[...].T, lambda low, high: delta_ffn[:, low:high], D),
        ),
    )
    place_blocks(plan_out, device, spread, None, targets)


def run_ffn(
    plan_in, staged, plan_out, block_shapes, device, mid, attn_out, cotangent, tables, gains, arrays
):
    flat_rows = G2LEN // LANES
    shapes = [
        jax.ShapeDtypeStruct((CAP, D), jnp.bfloat16),
        jax.ShapeDtypeStruct((CAP, D), jnp.float32),
        jax.ShapeDtypeStruct((CAP, D), jnp.bfloat16),
        jax.ShapeDtypeStruct((3, D), jnp.float32),
    ] + [jax.ShapeDtypeStruct(shape, jnp.bfloat16) for shape in block_shapes]
    wide = pltpu.VMEM((CAP, FF), jnp.float32)
    narrow = pltpu.VMEM((CAP, FF), jnp.bfloat16)
    return pl.pallas_call(
        functools.partial(ffn_kernel, plan_in, staged, plan_out),
        out_shape=shapes,
        in_specs=[pl.BlockSpec(memory_space=pltpu.SMEM)]
        + whole_specs(5)
        + [pl.BlockSpec(memory_space=pl.ANY)] * len(arrays),
        out_specs=whole_specs(len(shapes)),
        scratch_shapes=[
            pltpu.VMEM((flat_rows, LANES), jnp.float32),
            pltpu.VMEM((D, FF), jnp.bfloat16),
            pltpu.VMEM((D, FF), jnp.bfloat16),
            pltpu.VMEM((FF, D), jnp.bfloat16),
            wide,
            wide,
            narrow,
            narrow,
            narrow,
            pltpu.SemaphoreType.DMA((len(arrays),)),
        ],
        compiler_params=pltpu.CompilerParams(vmem_limit_bytes=44 << 20),
        cost_estimate=pl.CostEstimate(flops=0, bytes_accessed=0, transcendentals=0),
    )(device, mid, attn_out, cotangent, tables, gains, *arrays)


def attn_back_kernel(
    plan,
    gain_len,
    device_ref,
    delta_attn,
    delta_mid,
    hidden_in,
    tables,
    gains,
    late_gains,
    qkv_weight,
    out_weight,
    grad_in,
    gain_grads,
    *refs,
):
    targets = refs[:-4]
    spread, tails, delta_raws, contexts = refs[-4:]
    device = device_ref[0]
    normed_in, key_raw, values, keys, heads, cos_tab, sin_tab = attn_forward(
        hidden_in, qkv_weight, tables, gains
    )
    gain_query = gains[:, D : D + HD]
    gain_key = gains[:, D + HD : D + 2 * HD]
    delta_context = times_transposed(delta_attn[...], out_weight[...]).astype(jnp.bfloat16)
    delta_key = jnp.zeros((CAP, HD), jnp.float32)
    delta_value = jnp.zeros((CAP, HD), jnp.float32)
    query_gain_rows = jnp.zeros((CAP, HD), jnp.float32)
    for head, (query_raw, queries, scores, log_total, context) in enumerate(heads):
        at = slice(head * HD, (head + 1) * HD)
        contexts[:, at] = context
        head_delta = delta_context[:, at]
        row_dot = jnp.sum(
            head_delta.astype(jnp.float32) * context.astype(jnp.float32), axis=-1, keepdims=True
        )
        prob_exact = jnp.exp(scores - log_total)
        delta_prob = times_transposed(head_delta, values)
        delta_score = prob_exact * (delta_prob - row_dot)
        turned = delta_score.T.astype(jnp.bfloat16)
        delta_score = delta_score.astype(jnp.bfloat16)
        delta_query = jnp.dot(delta_score, keys, preferred_element_type=jnp.float32)
        delta_key += jnp.dot(turned, queries, preferred_element_type=jnp.float32)
        delta_value += jnp.dot(
            prob_exact.T.astype(jnp.bfloat16), head_delta, preferred_element_type=jnp.float32
        )
        delta_rot = rotate_pull(delta_query * HD ** (-0.5), cos_tab, sin_tab)
        delta_raw, gain_rows = rms_pull(query_raw, gain_query, delta_rot)
        query_gain_rows += gain_rows
        delta_raws[:, at] = delta_raw.astype(jnp.bfloat16)
    delta_raw, gain_rows = rms_pull(key_raw, gain_key, rotate_pull(delta_key, cos_tab, sin_tab))
    delta_raws[:, HQ : HQ + HD] = delta_raw.astype(jnp.bfloat16)
    delta_raws[:, HQ + HD :] = delta_value.astype(jnp.bfloat16)
    gain_grads[:, D : D + HD] = jnp.sum(query_gain_rows, axis=0, keepdims=True)
    gain_grads[:, D + HD : D + 2 * HD] = jnp.sum(gain_rows, axis=0, keepdims=True)
    delta_in = times_transposed(delta_raws[...], qkv_weight[...])
    delta_part, gain_rows = rms_pull(
        hidden_in[...].astype(jnp.float32), gains[:, :D], delta_in
    )
    grad_in[...] = delta_mid[...] + delta_part
    gain_grads[:, :D] = jnp.sum(gain_rows, axis=0, keepdims=True)
    for late in range(3):
        at = slice((late + 1) * D + 2 * HD, (late + 2) * D + 2 * HD)
        gain_grads[:, at] = late_gains[late : late + 1, :]
    if gain_len:
        tails[...] = jnp.zeros_like(tails)
        lane = lax.broadcasted_iota(jnp.int32, (1, LANES), 1)
        for owner in range(tails.shape[0]):
            row, shift = divmod(owner * gain_len, LANES)
            piece = gain_grads[:, row * LANES : (row + 1) * LANES]
            if shift:
                piece = pltpu.roll(piece, LANES - shift, 1)
            if shift + gain_len > LANES:
                after = gain_grads[:, (row + 1) * LANES : (row + 2) * LANES]
                after = pltpu.roll(after, LANES - shift, 1)
                piece = jnp.where(lane < LANES - shift, piece, after)
            tails[owner, 0:1, :] = jnp.where(lane < gain_len, piece, 0.0)
    turned = normed_in.T
    delta_attn_value = delta_attn[...]
    spread_grads(
        spread,
        (
            (turned, lambda low, high: delta_raws[:, low:high], HQ),
            (turned, lambda low, high: delta_raws[:, HQ + low : HQ + high], HD),
            (turned, lambda low, high: delta_raws[:, HQ + HD + low : HQ + HD + high], HD),
            (contexts[...].T, lambda low, high: delta_attn_value[:, low:high], D),
        ),
    )
    place_blocks(plan, device, spread, tails, targets)


def back_attn(plan, gain_len, tail_rows, devices, block_shapes, device, *inputs):
    flat_rows = G1LEN // LANES
    shapes = [
        jax.ShapeDtypeStruct((CAP, D), jnp.float32),
        jax.ShapeDtypeStruct((1, 4 * D + 2 * HD), jnp.float32),
    ] + [jax.ShapeDtypeStruct(shape, jnp.bfloat16) for shape in block_shapes]
    tail_shape = (devices, tail_rows, LANES) if gain_len else (1, ROWS, LANES)
    return pl.pallas_call(
        functools.partial(attn_back_kernel, plan, gain_len),
        out_shape=shapes,
        in_specs=[pl.BlockSpec(memory_space=pltpu.SMEM)] + whole_specs(len(inputs)),
        out_specs=whole_specs(len(shapes)),
        scratch_shapes=[
            pltpu.VMEM((flat_rows, LANES), jnp.float32),
            pltpu.VMEM(tail_shape, jnp.float32),
            pltpu.VMEM((CAP, HQ + 2 * HD), jnp.bfloat16),
            pltpu.VMEM((CAP, HQ), jnp.bfloat16),
        ],
        compiler_params=pltpu.CompilerParams(vmem_limit_bytes=22 << 20),
        cost_estimate=pl.CostEstimate(flops=0, bytes_accessed=0, transcendentals=0),
    )(device, *inputs)


def gathered_blocks(pieces, orders, each, devices, device):
    arrays, plan, start = [], [], 0
    for piece, order in zip(pieces, orders):
        blocks = gather_chunk(piece, order, devices)
        take = min(piece.shape[0], each - start)
        if each % ROWS:
            places = [offset_of(place, list(order) + [0]) for place in range(devices)]
            back = sorted(range(devices), key=places.__getitem__)
            mixed = offset_bits(device[0], list(order) + [0])
            arrays.append(
                jnp.take(jnp.concatenate(blocks), jnp.array(back, jnp.int32) ^ mixed, axis=0)
            )
            continue
        for part, block in enumerate(blocks):
            plan.append((order[:-1], offset_of(part, [order[-1], 0]), take, start, each))
            arrays.append(block)
        start += take
    if each % ROWS == 0:
        return arrays, plan, None
    table = jnp.concatenate(arrays, axis=1)
    flat = table[:, :each].reshape(1, devices * each, LANES)
    return [flat], [([], 0, devices * each, 0, 0)], table[:, each:]


def offset_bits(device, order):
    return sum(((device >> bit) & 1) << k for k, bit in enumerate(order))


def scatter_plan(each, tail_rows, orders, devices):
    parts = cut_rows(each + tail_rows, len(orders))
    half = devices // 2
    if each % ROWS:
        return [(0, [], 0, 0, devices * each, 0, 0)], [(1, devices * each, LANES)], parts
    plan = []
    for with_core in (1, 0):
        for (low, high), order in zip(parts, orders):
            order = order[::-1]
            plan.append((with_core, order, with_core, low, min(high, each) - low, low, each))
            if high > each:
                plan.append((with_core, order, with_core, each, tail_rows, None, each))
    return plan, [(half, each + tail_rows, LANES)] * 2, parts


def blocks_of(found, tails, parts, orders, devices, device):
    if len(found) == 2:
        return found
    table = found[0].reshape(devices, -1, LANES)
    table = table if tails is None else jnp.concatenate([table, tails], axis=1)
    blocks = []
    for with_core in (0, 1):
        chunks = []
        for (low, high), order in zip(parts, orders):
            places = range(devices // 2)
            offsets = [offset_of(place, order[::-1]) ^ with_core for place in places]
            owners = jnp.array(offsets, jnp.int32) ^ device[0]
            chunks.append(jnp.take(table[:, low:high], owners, axis=0))
        blocks.append(jnp.concatenate(chunks, axis=1))
    return blocks


def cores_merged(home, came, parts):
    half = home.shape[0] // 2

    def added(first, low, high):
        at = (slice(first, first + half), slice(low, high))
        return (home[at].astype(jnp.float32) + came[at].astype(jnp.float32)).astype(jnp.bfloat16)

    return [(added(0, low, high), added(half, low, high)) for low, high in parts]


def adam_update(weight_shard, gradient, moment_one, moment_two):
    moment_one = 0.9 * moment_one + 0.1 * gradient
    moment_two = 0.999 * moment_two + 0.001 * gradient * gradient
    fix_one = 1.0 - 0.9**STEP
    fix_two = 1.0 - 0.999**STEP
    weight_shard = weight_shard - 0.02 * (
        moment_one / fix_one / (jnp.sqrt(moment_two / fix_two) + 1e-08) + 0.1 * weight_shard
    )
    return (weight_shard, moment_one, moment_two)


def per_device(hidden_in, cotangent, params, moment_one, moment_two, seq_lengths, seq_owner):
    devices = lax.axis_size("dp")
    device = lax.axis_index("dp").astype(jnp.int32)
    here = device.reshape(1)
    attn_len = G1LEN // devices
    ffn_len = G2LEN // devices
    gain_len = params.shape[0] - attn_len - ffn_len
    attn_rows = attn_len // LANES
    tail_rows = -(-(attn_rows + 1) // ROWS) * ROWS - attn_rows
    pad = tail_rows * LANES - gain_len
    rounded = params.astype(jnp.bfloat16)
    first_piece = jnp.concatenate(
        [rounded[:attn_len], rounded[attn_len + ffn_len :], jnp.zeros((pad,), jnp.bfloat16)]
    ).reshape(-1, LANES)
    second_piece = rounded[attn_len : attn_len + ffn_len].reshape(-1, LANES)
    ffn_rows = ffn_len // LANES
    second_pieces = [second_piece[low:high] for low, high in cut_rows(ffn_rows, 2)]
    orders = bit_orders(devices, ("abxy", "bxya", "byax"))
    arrays, plan, tails = gathered_blocks([first_piece], orders[:1], attn_rows, devices, here)
    ffn_arrays, ffn_plan, unused = gathered_blocks(
        second_pieces, orders[1:], ffn_rows, devices, here
    )
    aligned = attn_rows % ROWS == 0
    qkv_weight, out_weight, *found = unpack_attn(
        plan, tail_rows if aligned else 0, here, arrays, devices
    )
    tails = found[0] if aligned else tails
    gains = tails.reshape(devices, -1)[:, :gain_len].astype(jnp.float32).reshape(1, -1)
    tables = slot_setup(seq_lengths, seq_owner, device)
    attn_out, mid_stream = forward_attn(hidden_in, qkv_weight, out_weight, tables, gains)
    ffn_orders = bit_orders(devices, ("xaby", "yxab", "ayxb"))
    attn_orders = bit_orders(devices, ("xyab", "yxba"))[:2]
    out_plan, block_shapes, ffn_parts = scatter_plan(ffn_rows, 0, ffn_orders, devices)
    staged = [(0, 0, 0)]
    if len(block_shapes) == 2:
        staged = [
            (part // 2, part % 2 * (devices // 4), low)
            for low, _ in cut_rows(ffn_rows, 2)
            for part in range(4)
        ]
    block_out, delta_mid, delta_attn, late_gains, *found = run_ffn(
        ffn_plan,
        staged,
        out_plan,
        block_shapes,
        here,
        mid_stream,
        attn_out,
        cotangent,
        tables,
        gains,
        ffn_arrays,
    )
    ffn_home, ffn_away = blocks_of(found, None, ffn_parts, ffn_orders, devices, here)
    ffn_came = across(ffn_away, 0, devices)
    delta_attn, ffn_came = lax.optimization_barrier((delta_attn, ffn_came))
    ffn_chunks = cores_merged(ffn_home, ffn_came, ffn_parts)
    delta_attn, ffn_chunks = lax.optimization_barrier((delta_attn, ffn_chunks))
    ffn_came = sent_blocks(ffn_chunks, ffn_orders, 0, devices)
    attn_plan, block_shapes, attn_parts = scatter_plan(attn_rows, tail_rows, attn_orders, devices)
    grad_in, gain_grads, *found = back_attn(
        attn_plan,
        gain_len if aligned else 0,
        tail_rows,
        devices,
        block_shapes,
        here,
        delta_attn,
        delta_mid,
        hidden_in,
        tables,
        gains,
        late_gains,
        qkv_weight,
        out_weight,
    )
    gain_table = None
    if not aligned:
        gain_table = gain_grads.reshape(devices, gain_len).astype(jnp.bfloat16)
        gain_table = jnp.pad(gain_table, ((0, 0), (0, pad))).reshape(devices, tail_rows, LANES)
    attn_home, attn_away = blocks_of(found, gain_table, attn_parts, attn_orders, devices, here)
    attn_home, attn_away, ffn_came = lax.optimization_barrier((attn_home, attn_away, ffn_came))
    stages = len(ffn_orders[0])
    ffn_chunks = merged_blocks(ffn_chunks, ffn_came)
    ffn_came = sent_blocks(ffn_chunks, ffn_orders, 1, devices)
    attn_came = across(attn_away, 0, devices)
    ffn_came[0], attn_came = lax.optimization_barrier((ffn_came[0], attn_came))
    attn_chunks = cores_merged(attn_home, attn_came, attn_parts)
    for stage in range(1, stages + 1):
        attn_came = sent_blocks(attn_chunks, attn_orders, stage - 1, devices)
        if stage < stages:
            ffn_chunks = merged_blocks(ffn_chunks, ffn_came)
        if stage + 1 < stages:
            ffn_came = sent_blocks(ffn_chunks, ffn_orders, stage + 1, devices)
            for chunk, arrived in enumerate(attn_came):
                ffn_came[chunk], attn_came[chunk] = lax.optimization_barrier(
                    (ffn_came[chunk], arrived)
                )
        attn_chunks = merged_blocks(attn_chunks, attn_came)
    attn_shard = jnp.concatenate([rows for rows, _ in attn_chunks]).reshape(-1)
    ffn_shard = jnp.concatenate([rows for rows, _ in ffn_chunks])
    grad_shard = jnp.concatenate(
        [attn_shard[:attn_len], ffn_shard.reshape(-1), attn_shard[attn_len : attn_len + gain_len]]
    )
    params_new, moment_one_new, moment_two_new = adam_update(
        params, grad_shard, moment_one, moment_two
    )
    return (block_out, grad_in, grad_shard, params_new, moment_one_new, moment_two_new)


def solution(mesh):
    in_specs = (P("dp", None), P("dp", None), P("dp"), P("dp"), P("dp"), P(), P())
    out_specs = (P("dp", None), P("dp", None), P("dp"), P("dp"), P("dp"), P("dp"))
    return jax.shard_map(
        per_device, mesh=mesh, in_specs=in_specs, out_specs=out_specs, check_vma=False
    )
```

time: 230 us -> 188 us (0.82)
  local copies, waits for them, and re-layouts: 36.3 us -> 7.95 us
  starting transfers between devices: 36.2 us -> 58.6 us
  other arithmetic: 29.6 us -> 12.4 us
  matrix products: 10.4 us -> 0 us
  waiting for transfers between devices: 85 us -> 76.4 us
    unnamed x120 -> x29, local copies, waits for them, and re-layouts: 30.2 us -> 6.27 us
    ppermute x40, starting transfers between devices: 36.2 us -> 58.6 us  [across(): lax.ppermute(block, 'dp', [(i, i ^ 1 << bit) for i in range(devices)])]
    dot_general x12 -> x0, matrix products: 10.4 us -> none  [the longest x3 4.07 us: times_transposed(): lax.dot_general(rows_in, matrix, (((1,), (1,)), ((), ())), preferred_elem...]
    ppermute x40, waiting for transfers between devices: 85 us -> 76.4 us  [across(): lax.ppermute(block, 'dp', [(i, i ^ 1 << bit) for i in range(devices)])]
    convert_element_type x8 -> x2, other arithmetic: 3.61 us -> 0.11 us  [the longest x1 0.11 us: slot_setup(): allowed.astype(jnp.float32)]
    convert_element_type x8, other arithmetic: 4.37 us -> 0.92 us  [merged_blocks(): added(0, half).astype(jnp.bfloat16)]
    reduce_sum x7 -> x1, other arithmetic: 3.1 us -> 0.11 us  [slot_setup(): jnp.sum(jnp.where(inside_mask, column - seq_begins[None, :], 0), axis=1,...]
    concatenate x9, other arithmetic: 5.27 us -> 2.51 us  [gather_chunk(): held = jnp.concatenate([held, across(held, bit, devices)])]
  transfers between devices with their start and end apart: 40 -> 40, of which waited for: 21 -> 22; matrix products, arithmetic and copies ran while one was open for 15% -> 4% of each run, Pallas kernels for 4% -> 5%
where the time goes in v4:
time: 188 us
  waiting for transfers between devices  76.4 us (41%)
  starting transfers between devices  58.6 us (31%)
  Pallas kernels  31.3 us (17%)
  other arithmetic  12.4 us (7%)
  local copies, waits for them, and re-layouts  7.95 us (4%)
    ppermute x40, waiting for transfers between devices, across(): lax.ppermute(block, 'dp', [(i, i ^ 1 << bit) for i in range(devices)])  76.4 us
    ppermute x40, starting transfers between devices, across(): lax.ppermute(block, 'dp', [(i, i ^ 1 << bit) for i in range(devices)])  58.6 us
    pallas_call x1, Pallas kernels, run_ffn(): pl.pallas_call(functools.partial(ffn_kernel, plan_in, staged, plan_out),...  22.4 us
    unnamed x29, local copies, waits for them, and re-layouts  6.27 us
    pallas_call x1, Pallas kernels, back_attn(): pl.pallas_call(functools.partial(attn_back_kernel, plan, gain_len), out_s...  5.76 us
    convert_element_type x2, other arithmetic, added(): (home[at].astype(jnp.float32) + came[at].astype(jnp.float32)).astype(jnp....  4.03 us
  transfers between devices with their start and end apart: 40, of which 22 were waited for; matrix products, arithmetic and copies ran while one was open for 4% of the time, Pallas kernels for 5%

profile of v4, /device:TPU:0, one launch (start us, length us, event | category | flops | bytes accessed | tf_op | source)
XLA Modules:
  0.0 187.7 jit_solution(6762484538691020492)
XLA Ops:
  1.8 4.1 %collective-permute-start.6 = (bf16[1,480,128]{2,1,0:T(8,128)(2,1)S(1)}, bf16[1,480,128]{2,1,0:T(8,128)(2,1)S(1)}, u32[]{:S(2)}, u32[]{:S(2)}) collective-permute-start(bf16[1,480,128]{2,1,0:T(8,128)(2,1)S(1)} %get-tuple-element.121), channel_id=1, source_target_pairs={{0,16},{1,17},{2,18},{3,19},{4,20},{5,21},{6,22},{7,23},{8,24},{9,... | collective-permute-start | bytes 368648 | tf_op jit(solution)/shard_map/ppermute | solution.py:111
  5.9 6.0 %collective-permute-done.6 = bf16[1,480,128]{2,1,0:T(8,128)(2,1)S(1)} collective-permute-done((bf16[1,480,128]{2,1,0:T(8,128)(2,1)S(1)}, bf16[1,480,128]{2,1,0:T(8,128)(2,1)S(1)}, u32[]{:S(2)}, u32[]{:S(2)}) %collective-permute-start.6) | collective-permute-done | bytes 122912 | tf_op jit(solution)/shard_map/ppermute | solution.py:111
  14.2 4.0 %collective-permute-start = (bf16[1,416,128]{2,1,0:T(8,128)(2,1)S(1)}, bf16[1,416,128]{2,1,0:T(8,128)(2,1)S(1)}, u32[]{:S(2)}, u32[]{:S(2)}) collective-permute-start(bf16[1,416,128]{2,1,0:T(8,128)(2,1)S(1)} %bitcast.29), channel_id=1, source_target_pairs={{0,8},{1,9},{2,10},{3,11},{4,12},{5,13},{6,14},{7,15},{8,0},{9,1},... | collective-permute-start | bytes 319496 | tf_op jit(solution)/shard_map/ppermute | solution.py:111
  18.2 3.4 %collective-permute-done.12 = bf16[1,480,128]{2,1,0:T(8,128)(2,1)S(1)} collective-permute-done((bf16[1,480,128]{2,1,0:T(8,128)(2,1)S(1)}, bf16[1,480,128]{2,1,0:T(8,128)(2,1)S(1)}, u32[]{:S(2)}, u32[]{:S(2)}) %collective-permute-start.12) | collective-permute-done | bytes 122912 | tf_op jit(solution)/shard_map/ppermute | solution.py:111
  24.0 6.6 %collective-permute-done.13 = bf16[2,480,128]{2,1,0:T(8,128)(2,1)S(1)} collective-permute-done((bf16[2,480,128]{2,1,0:T(8,128)(2,1)S(1)}, bf16[2,480,128]{2,1,0:T(8,128)(2,1)S(1)}, u32[]{:S(2)}, u32[]{:S(2)}) %collective-permute-start.13) | collective-permute-done | bytes 245792 | tf_op jit(solution)/shard_map/ppermute | solution.py:111
  30.8 2.3 %collective-permute-done.1 = bf16[2,416,128]{2,1,0:T(8,128)(2,1)S(1)} collective-permute-done((bf16[2,416,128]{2,1,0:T(8,128)(2,1)S(1)}, bf16[2,416,128]{2,1,0:T(8,128)(2,1)S(1)}, u32[]{:S(2)}, u32[]{:S(2)}) %collective-permute-start.1) | collective-permute-done | bytes 213024 | tf_op jit(solution)/shard_map/ppermute | solution.py:111
  33.7 2.2 %collective-permute-done.8 = bf16[4,480,128]{2,1,0:T(8,128)(2,1)S(1)} collective-permute-done((bf16[4,480,128]{2,1,0:T(8,128)(2,1)S(1)}, bf16[4,480,128]{2,1,0:T(8,128)(2,1)S(1)}, u32[]{:S(2)}, u32[]{:S(2)}) %collective-permute-start.8) | collective-permute-done | bytes 491552 | tf_op jit(solution)/shard_map/ppermute | solution.py:111
  37.1 2.5 %collective-permute-start.9 = (bf16[8,480,128]{2,1,0:T(8,128)(2,1)}, bf16[8,480,128]{2,1,0:T(8,128)(2,1)}, u32[]{:S(2)}, u32[]{:S(2)}) collective-permute-start(bf16[8,480,128]{2,1,0:T(8,128)(2,1)} %pad_maximum_fusion.refs_0_), channel_id=1, source_target_pairs={{0,8},{1,9},{2,10},{3,11},{4,12},{5,13},{6,14},{7,15},{8,0},{9,1},... | collective-permute-start | bytes 2949128 | tf_op jit(solution)/shard_map/ppermute | solution.py:111
  45.5 13.7 %collective-permute-done.3.refs_1_ = bf16[8,416,128]{2,1,0:T(8,128)(2,1)S(1)} collective-permute-done((bf16[8,416,128]{2,1,0:T(8,128)(2,1)S(1)}, bf16[8,416,128]{2,1,0:T(8,128)(2,1)S(1)}, u32[]{:S(2)}, u32[]{:S(2)}) %collective-permute-start.3) | collective-permute-done | bytes 852000 | tf_op jit(solution)/shard_map/ppermute | solution.py:111
  72.9 22.4 %shard_map.120 = (bf16[128,640]{1,0:T(8,128)(2,1)}, f32[128,640]{1,0:T(8,128)S(1)}, bf16[128,640]{1,0:T(8,128)(2,1)S(1)}, f32[3,640]{1,0:T(4,128)S(1)}, bf16[16,...) custom-call(s32[1]{0:T(128)} %bitcast.device_ref, f32[128,640]{1,0:T(8,128)S(1)} %get-tuple-element.47.mid_ref, ...), custom_call_target="tpu_custom_call" | custom-call | tf_op jit(solution)/shard_map/pallas_call | solution.py:458
  96.0 6.6 %collective-permute-done.18 = bf16[16,960,128]{2,1,0:T(8,128)(2,1)S(1)} collective-permute-done((bf16[16,960,128]{2,1,0:T(8,128)(2,1)}, bf16[16,960,128]{2,1,0:T(8,128)(2,1)S(1)}, u32[]{:S(2)}, u32[]{:S(2)}) %collective-permute-start.18) | collective-permute-done | bytes 3932192 | tf_op jit(solution)/shard_map/ppermute | solution.py:111
  102.6 3.6 %add_convert_fusion = (bf16[8,320,128]{2,1,0:T(8,128)(2,1)S(1)}, bf16[8,320,128]{2,1,0:T(8,128)(2,1)S(1)}, bf16[8,320,128]{2,1,0:T(8,128)(2,1)S(1)}, bf16[8,320,...) fusion(bf16[16,960,128]{2,1,0:T(8,128)(2,1)S(1)} %collective-permute-done.18, ...), kind=kLoop, calls=%fused_computation | loop fusion | flops 7864320 | bytes 11796480 | tf_op jit(solution)/shard_map/convert_element_type | solution.py:660
  108.3 5.6 %collective-permute-start.21 = (bf16[8,320,128]{2,1,0:T(8,128)(2,1)S(1)}, bf16[8,320,128]{2,1,0:T(8,128)(2,1)S(1)}, u32[]{:S(2)}, u32[]{:S(2)}) collective-permute-start(bf16[8,320,128]{2,1,0:T(8,128)(2,1)S(1)} %get-tuple-element.63), channel_id=1, source_target_pairs={{0,8},{1,9},{2,10},{3,11},{4,12},{5,13},{6,14},{7,15},{8,0},{9,1},... | collective-permute-start | bytes 1966088 | tf_op jit(solution)/shard_map/ppermute | solution.py:111
  113.9 5.8 %shard_map.121 = (f32[128,640]{1,0:T(8,128)}, f32[1,3072]{1,0:T(1,128)}, bf16[16,416,128]{2,1,0:T(8,128)(2,1)S(1)}, bf16[16,416,128]{2,1,0:T(8,128)(2,1)S(1)}) custom-call(s32[1]{0:T(128)} %bitcast.device_ref, bf16[128,640]{1,0:T(8,128)(2,1)S(1)} %get-tuple-element.55.delta_attn, f32[128,640]{1,0:T(8,128)S(1)} %get-tuple-element.56.delta_mid, ...), custom_call_target="tpu_custom_call" | custom-call | tf_op jit(solution)/shard_map/pallas_call | solution.py:579
  119.7 3.5 %collective-permute-done.19 = bf16[8,320,128]{2,1,0:T(8,128)(2,1)S(1)} collective-permute-done((bf16[8,320,128]{2,1,0:T(8,128)(2,1)S(1)}, bf16[8,320,128]{2,1,0:T(8,128)(2,1)S(1)}, u32[]{:S(2)}, u32[]{:S(2)}) %collective-permute-start.19) | collective-permute-done | bytes 655392 | tf_op jit(solution)/shard_map/ppermute | solution.py:111
  123.3 5.3 %collective-permute-done.21 = bf16[8,320,128]{2,1,0:T(8,128)(2,1)S(1)} collective-permute-done((bf16[8,320,128]{2,1,0:T(8,128)(2,1)S(1)}, bf16[8,320,128]{2,1,0:T(8,128)(2,1)S(1)}, u32[]{:S(2)}, u32[]{:S(2)}) %collective-permute-start.21) | collective-permute-done | bytes 655392 | tf_op jit(solution)/shard_map/ppermute | solution.py:111
  133.1 5.9 %collective-permute-done.37 = bf16[4,320,128]{2,1,0:T(8,128)(2,1)S(1)} collective-permute-done((bf16[4,320,128]{2,1,0:T(8,128)(2,1)S(1)}, bf16[4,320,128]{2,1,0:T(8,128)(2,1)S(1)}, u32[]{:S(2)}, u32[]{:S(2)}) %collective-permute-start.37) | collective-permute-done | bytes 327712 | tf_op jit(solution)/shard_map/ppermute | solution.py:111
  142.6 2.4 %collective-permute-done.38 = bf16[2,320,128]{2,1,0:T(8,128)(2,1)S(1)} collective-permute-done((bf16[2,320,128]{2,1,0:T(8,128)(2,1)S(1)}, bf16[2,320,128]{2,1,0:T(8,128)(2,1)S(1)}, u32[]{:S(2)}, u32[]{:S(2)}) %collective-permute-start.38) | collective-permute-done | bytes 163872 | tf_op jit(solution)/shard_map/ppermute | solution.py:111
  145.0 3.4 %collective-permute-start.39 = (bf16[1,320,128]{2,1,0:T(8,128)(2,1)S(1)}, bf16[1,320,128]{2,1,0:T(8,128)(2,1)S(1)}, u32[]{:S(2)}, u32[]{:S(2)}) collective-permute-start(bf16[1,320,128]{2,1,0:T(8,128)(2,1)S(1)} %add_convert_fusion.30), channel_id=1, source_target_pairs={{0,16},{1,17},{2,18},{3,19},{4,20},{5,21},{6,22},{7,23},{8,24},{9,... | collective-permute-start | bytes 245768 | tf_op jit(solution)/shard_map/ppermute | solution.py:111
  151.7 7.7 %collective-permute-done.24 = bf16[2,320,128]{2,1,0:T(8,128)(2,1)S(1)} collective-permute-done((bf16[2,320,128]{2,1,0:T(8,128)(2,1)S(1)}, bf16[2,320,128]{2,1,0:T(8,128)(2,1)S(1)}, u32[]{:S(2)}, u32[]{:S(2)}) %collective-permute-start.24) | collective-permute-done | bytes 163872 | tf_op jit(solution)/shard_map/ppermute | solution.py:111
  161.9 4.7 %collective-permute-start.33 = (bf16[1,320,128]{2,1,0:T(8,128)(2,1)S(1)}, bf16[1,320,128]{2,1,0:T(8,128)(2,1)S(1)}, u32[]{:S(2)}, u32[]{:S(2)}) collective-permute-start(bf16[1,320,128]{2,1,0:T(8,128)(2,1)S(1)} %add_convert_fusion.34), channel_id=1, source_target_pairs={{0,16},{1,17},{2,18},{3,19},{4,20},{5,21},{6,22},{7,23},{8,24},{9,... | collective-permute-start | bytes 245768 | tf_op jit(solution)/shard_map/ppermute | solution.py:111
  167.8 6.3 %collective-permute-start.28 = (bf16[2,208,128]{2,1,0:T(8,128)(2,1)S(1)}, bf16[2,208,128]{2,1,0:T(8,128)(2,1)S(1)}, u32[]{:S(2)}, u32[]{:S(2)}) collective-permute-start(bf16[2,208,128]{2,1,0:T(8,128)(2,1)S(1)} %get-tuple-element.117), channel_id=1, source_target_pairs={{0,8},{1,9},{2,10},{3,11},{4,12},{5,13},{6,14},{7,15},{8,0},{9,1},... | collective-permute-start | bytes 319496 | tf_op jit(solution)/shard_map/ppermute | solution.py:111
  175.2 2.3 %collective-permute-done.28 = bf16[2,208,128]{2,1,0:T(8,128)(2,1)S(1)} collective-permute-done((bf16[2,208,128]{2,1,0:T(8,128)(2,1)S(1)}, bf16[2,208,128]{2,1,0:T(8,128)(2,1)S(1)}, u32[]{:S(2)}, u32[]{:S(2)}) %collective-permute-start.28) | collective-permute-done | bytes 106528 | tf_op jit(solution)/shard_map/ppermute | solution.py:111
  180.6 3.1 %collective-permute-start.36 = (bf16[1,208,128]{2,1,0:T(8,128)(2,1)S(1)}, bf16[1,208,128]{2,1,0:T(8,128)(2,1)S(1)}, u32[]{:S(2)}, u32[]{:S(2)}) collective-permute-start(bf16[1,208,128]{2,1,0:T(8,128)(2,1)S(1)} %add_convert_fusion.36), channel_id=1, source_target_pairs={{0,8},{1,9},{2,10},{3,11},{4,12},{5,13},{6,14},{7,15},{8,0},{9,1},... | collective-permute-start | bytes 159752 | tf_op jit(solution)/shard_map/ppermute | solution.py:111
  (146 shorter events, 53.2 us)
Async XLA Ops:
  1.8 10.1 %collective-permute-start.6 = (bf16[1,480,128]{2,1,0:T(8,128)(2,1)S(1)}, bf16[1,480,128]{2,1,0:T(8,128)(2,1)S(1)}, u32[]{:S(2)}, u32[]{:S(2)}) collective-permute-start(bf16[1,480,128]{2,1,0:T(8,128)(2,1)S(1)} %get-tuple-element.121), channel_id=1, source_target_pairs={{0,16},{1,17},{2,18},{3,19},{4,20},{5,21},{6,22},{7,23},{8,24},{9,... | collective-permute-start | bytes 368648 | tf_op jit(solution)/shard_map/ppermute | solution.py:111
  11.9 11.4 %collective-permute-start.7 = (bf16[2,480,128]{2,1,0:T(8,128)(2,1)S(1)}, bf16[2,480,128]{2,1,0:T(8,128)(2,1)S(1)}, u32[]{:S(2)}, u32[]{:S(2)}) collective-permute-start(bf16[2,480,128]{2,1,0:T(8,128)(2,1)S(1)} %pad_maximum_fusion.9), channel_id=1, source_target_pairs={{0,2},{1,3},{2,0},{3,1},{4,6},{5,7},{6,4},{7,5},{8,10},{9,11},{10,... | collective-permute-start | bytes 737288 | tf_op jit(solution)/shard_map/ppermute | solution.py:111
  23.3 12.6 %collective-permute-start.8 = (bf16[4,480,128]{2,1,0:T(8,128)(2,1)S(1)}, bf16[4,480,128]{2,1,0:T(8,128)(2,1)S(1)}, u32[]{:S(2)}, u32[]{:S(2)}) collective-permute-start(bf16[4,480,128]{2,1,0:T(8,128)(2,1)S(1)} %pad_maximum_fusion.4), channel_id=1, source_target_pairs={{0,4},{1,5},{2,6},{3,7},{4,0},{5,1},{6,2},{7,3},{8,12},{9,13},{10,... | collective-permute-start | bytes 1474568 | tf_op jit(solution)/shard_map/ppermute | solution.py:111
  30.7 10.4 %collective-permute-start.14 = (bf16[4,480,128]{2,1,0:T(8,128)(2,1)S(1)}, bf16[4,480,128]{2,1,0:T(8,128)(2,1)S(1)}, u32[]{:S(2)}, u32[]{:S(2)}) collective-permute-start(bf16[4,480,128]{2,1,0:T(8,128)(2,1)S(1)} %pad_maximum_fusion.5), channel_id=1, source_target_pairs={{0,8},{1,9},{2,10},{3,11},{4,12},{5,13},{6,14},{7,15},{8,0},{9,1},... | collective-permute-start | bytes 1474568 | tf_op jit(solution)/shard_map/ppermute | solution.py:111
  33.1 10.3 %collective-permute-start.2 = (bf16[4,416,128]{2,1,0:T(8,128)(2,1)S(1)}, bf16[4,416,128]{2,1,0:T(8,128)(2,1)S(1)}, u32[]{:S(2)}, u32[]{:S(2)}) collective-permute-start(bf16[4,416,128]{2,1,0:T(8,128)(2,1)S(1)} %pad_maximum_fusion.6), channel_id=1, source_target_pairs={{0,2},{1,3},{2,0},{3,1},{4,6},{5,7},{6,4},{7,5},{8,10},{9,11},{10,... | collective-permute-start | bytes 1277960 | tf_op jit(solution)/shard_map/ppermute | solution.py:111
  37.1 24.7 %collective-permute-start.9 = (bf16[8,480,128]{2,1,0:T(8,128)(2,1)}, bf16[8,480,128]{2,1,0:T(8,128)(2,1)}, u32[]{:S(2)}, u32[]{:S(2)}) collective-permute-start(bf16[8,480,128]{2,1,0:T(8,128)(2,1)} %pad_maximum_fusion.refs_0_), channel_id=1, source_target_pairs={{0,8},{1,9},{2,10},{3,11},{4,12},{5,13},{6,14},{7,15},{8,0},{9,1},... | collective-permute-start | bytes 2949128 | tf_op jit(solution)/shard_map/ppermute | solution.py:111
  42.2 21.0 %collective-permute-start.15 = (bf16[8,480,128]{2,1,0:T(8,128)(2,1)}, bf16[8,480,128]{2,1,0:T(8,128)(2,1)}, u32[]{:S(2)}, u32[]{:S(2)}) collective-permute-start(bf16[8,480,128]{2,1,0:T(8,128)(2,1)} %pad_maximum_fusion.1.refs_4_), channel_id=1, source_target_pairs={{0,2},{1,3},{2,0},{3,1},{4,6},{5,7},{6,4},{7,5},{8,10},{9,11},{10,... | collective-permute-start | bytes 2949128 | tf_op jit(solution)/shard_map/ppermute | solution.py:111
  43.6 15.6 %collective-permute-start.3 = (bf16[8,416,128]{2,1,0:T(8,128)(2,1)S(1)}, bf16[8,416,128]{2,1,0:T(8,128)(2,1)S(1)}, u32[]{:S(2)}, u32[]{:S(2)}) collective-permute-start(bf16[8,416,128]{2,1,0:T(8,128)(2,1)S(1)} %pad_maximum_fusion.2.refs_0_), channel_id=1, source_target_pairs={{0,4},{1,5},{2,6},{3,7},{4,0},{5,1},{6,2},{7,3},{8,12},{9,13},{10,... | collective-permute-start | bytes 2555912 | tf_op jit(solution)/shard_map/ppermute | solution.py:111
  45.2 15.6 %collective-permute-start.4 = (bf16[8,416,128]{2,1,0:T(8,128)(2,1)S(1)}, bf16[8,416,128]{2,1,0:T(8,128)(2,1)S(1)}, u32[]{:S(2)}, u32[]{:S(2)}) collective-permute-start(bf16[8,416,128]{2,1,0:T(8,128)(2,1)S(1)} %pad_maximum_fusion.2.refs_0_), channel_id=1, source_target_pairs={{0,1},{1,0},{2,3},{3,2},{4,5},{5,4},{6,7},{7,6},{8,9},{9,8},{10,11... | collective-permute-start | bytes 2555912 | tf_op jit(solution)/shard_map/ppermute | solution.py:111
  60.2 12.6 %collective-permute-start.10 = (bf16[8,480,128]{2,1,0:T(8,128)(2,1)}, bf16[8,480,128]{2,1,0:T(8,128)(2,1)}, u32[]{:S(2)}, u32[]{:S(2)}) collective-permute-start(bf16[8,480,128]{2,1,0:T(8,128)(2,1)} %pad_maximum_fusion.refs_0_), channel_id=1, source_target_pairs={{0,1},{1,0},{2,3},{3,2},{4,5},{5,4},{6,7},{7,6},{8,9},{9,8},{10,11... | collective-permute-start | bytes 2949128 | tf_op jit(solution)/shard_map/ppermute | solution.py:111
  61.7 11.2 %collective-permute-start.16 = (bf16[8,480,128]{2,1,0:T(8,128)(2,1)}, bf16[8,480,128]{2,1,0:T(8,128)(2,1)}, u32[]{:S(2)}, u32[]{:S(2)}) collective-permute-start(bf16[8,480,128]{2,1,0:T(8,128)(2,1)} %pad_maximum_fusion.1.refs_4_), channel_id=1, source_target_pairs={{0,1},{1,0},{2,3},{3,2},{4,5},{5,4},{6,7},{7,6},{8,9},{9,8},{10,11... | collective-permute-start | bytes 2949128 | tf_op jit(solution)/shard_map/ppermute | solution.py:111
  61.7 11.1 %collective-permute-start.11 = (bf16[8,480,128]{2,1,0:T(8,128)(2,1)}, bf16[8,480,128]{2,1,0:T(8,128)(2,1)}, u32[]{:S(2)}, u32[]{:S(2)}) collective-permute-start(bf16[8,480,128]{2,1,0:T(8,128)(2,1)} %collective-permute-done.9.refs_1_), channel_id=1, source_target_pairs={{0,1},{1,0},{2,3},{3,2},{4,5},{5,4},{6,7},{7,6},{8,9},{9,8},{10,11... | collective-permute-start | bytes 2949128 | tf_op jit(solution)/shard_map/ppermute | solution.py:111
  106.1 17.1 %collective-permute-start.19 = (bf16[8,320,128]{2,1,0:T(8,128)(2,1)S(1)}, bf16[8,320,128]{2,1,0:T(8,128)(2,1)S(1)}, u32[]{:S(2)}, u32[]{:S(2)}) collective-permute-start(bf16[8,320,128]{2,1,0:T(8,128)(2,1)S(1)} %get-tuple-element.61), channel_id=1, source_target_pairs={{0,2},{1,3},{2,0},{3,1},{4,6},{5,7},{6,4},{7,5},{8,10},{9,11},{10,... | collective-permute-start | bytes 1966088 | tf_op jit(solution)/shard_map/ppermute | solution.py:111
  106.5 16.8 %collective-permute-start.20 = (bf16[8,320,128]{2,1,0:T(8,128)(2,1)S(1)}, bf16[8,320,128]{2,1,0:T(8,128)(2,1)S(1)}, u32[]{:S(2)}, u32[]{:S(2)}) collective-permute-start(bf16[8,320,128]{2,1,0:T(8,128)(2,1)S(1)} %get-tuple-element.62), channel_id=1, source_target_pairs={{0,4},{1,5},{2,6},{3,7},{4,0},{5,1},{6,2},{7,3},{8,12},{9,13},{10,... | collective-permute-start | bytes 1966088 | tf_op jit(solution)/shard_map/ppermute | solution.py:111
  108.3 20.3 %collective-permute-start.21 = (bf16[8,320,128]{2,1,0:T(8,128)(2,1)S(1)}, bf16[8,320,128]{2,1,0:T(8,128)(2,1)S(1)}, u32[]{:S(2)}, u32[]{:S(2)}) collective-permute-start(bf16[8,320,128]{2,1,0:T(8,128)(2,1)S(1)} %get-tuple-element.63), channel_id=1, source_target_pairs={{0,8},{1,9},{2,10},{3,11},{4,12},{5,13},{6,14},{7,15},{8,0},{9,1},... | collective-permute-start | bytes 1966088 | tf_op jit(solution)/shard_map/ppermute | solution.py:111
  128.6 19.8 %collective-permute-start.23 = (bf16[16,416,128]{2,1,0:T(8,128)(2,1)S(1)}, bf16[16,416,128]{2,1,0:T(8,128)(2,1)S(1)}, u32[]{:S(2)}, u32[]{:S(2)}) collective-permute-start(bf16[16,416,128]{2,1,0:T(8,128)(2,1)S(1)} %get-tuple-element.67), channel_id=1, source_target_pairs={{0,1},{1,0},{2,3},{3,2},{4,5},{5,4},{6,7},{7,6},{8,9},{9,8},{10,11... | collective-permute-start | bytes 5111816 | tf_op jit(solution)/shard_map/ppermute | solution.py:111
  128.8 10.2 %collective-permute-start.37 = (bf16[4,320,128]{2,1,0:T(8,128)(2,1)S(1)}, bf16[4,320,128]{2,1,0:T(8,128)(2,1)S(1)}, u32[]{:S(2)}, u32[]{:S(2)}) collective-permute-start(bf16[4,320,128]{2,1,0:T(8,128)(2,1)S(1)} %get-tuple-element.101), channel_id=1, source_target_pairs={{0,4},{1,5},{2,6},{3,7},{4,0},{5,1},{6,2},{7,3},{8,12},{9,13},{10,... | collective-permute-start | bytes 983048 | tf_op jit(solution)/shard_map/ppermute | solution.py:111
  129.4 11.3 %collective-permute-start.30 = (bf16[4,320,128]{2,1,0:T(8,128)(2,1)S(1)}, bf16[4,320,128]{2,1,0:T(8,128)(2,1)S(1)}, u32[]{:S(2)}, u32[]{:S(2)}) collective-permute-start(bf16[4,320,128]{2,1,0:T(8,128)(2,1)S(1)} %get-tuple-element.105), channel_id=1, source_target_pairs={{0,2},{1,3},{2,0},{3,1},{4,6},{5,7},{6,4},{7,5},{8,10},{9,11},{10,... | collective-permute-start | bytes 983048 | tf_op jit(solution)/shard_map/ppermute | solution.py:111
  131.3 17.1 %collective-permute-start.22 = (bf16[4,320,128]{2,1,0:T(8,128)(2,1)S(1)}, bf16[4,320,128]{2,1,0:T(8,128)(2,1)S(1)}, u32[]{:S(2)}, u32[]{:S(2)}) collective-permute-start(bf16[4,320,128]{2,1,0:T(8,128)(2,1)S(1)} %get-tuple-element.103), channel_id=1, source_target_pairs={{0,8},{1,9},{2,10},{3,11},{4,12},{5,13},{6,14},{7,15},{8,0},{9,1},... | collective-permute-start | bytes 983048 | tf_op jit(solution)/shard_map/ppermute | solution.py:111
  140.7 20.9 %collective-permute-start.31 = (bf16[2,320,128]{2,1,0:T(8,128)(2,1)S(1)}, bf16[2,320,128]{2,1,0:T(8,128)(2,1)S(1)}, u32[]{:S(2)}, u32[]{:S(2)}) collective-permute-start(bf16[2,320,128]{2,1,0:T(8,128)(2,1)S(1)} %get-tuple-element.115), channel_id=1, source_target_pairs={{0,8},{1,9},{2,10},{3,11},{4,12},{5,13},{6,14},{7,15},{8,0},{9,1},... | collective-permute-start | bytes 491528 | tf_op jit(solution)/shard_map/ppermute | solution.py:111
  148.9 10.5 %collective-permute-start.25 = (bf16[8,208,128]{2,1,0:T(8,128)(2,1)S(1)}, bf16[8,208,128]{2,1,0:T(8,128)(2,1)S(1)}, u32[]{:S(2)}, u32[]{:S(2)}) collective-permute-start(bf16[8,208,128]{2,1,0:T(8,128)(2,1)S(1)} %get-tuple-element.96), channel_id=1, source_target_pairs={{0,2},{1,3},{2,0},{3,1},{4,6},{5,7},{6,4},{7,5},{8,10},{9,11},{10,... | collective-permute-start | bytes 1277960 | tf_op jit(solution)/shard_map/ppermute | solution.py:111
  151.3 10.6 %collective-permute-start.32 = (bf16[8,208,128]{2,1,0:T(8,128)(2,1)S(1)}, bf16[8,208,128]{2,1,0:T(8,128)(2,1)S(1)}, u32[]{:S(2)}, u32[]{:S(2)}) collective-permute-start(bf16[8,208,128]{2,1,0:T(8,128)(2,1)S(1)} %get-tuple-element.97), channel_id=1, source_target_pairs={{0,4},{1,5},{2,6},{3,7},{4,0},{5,1},{6,2},{7,3},{8,12},{9,13},{10,... | collective-permute-start | bytes 1277960 | tf_op jit(solution)/shard_map/ppermute | solution.py:111
  161.9 12.2 %collective-permute-start.33 = (bf16[1,320,128]{2,1,0:T(8,128)(2,1)S(1)}, bf16[1,320,128]{2,1,0:T(8,128)(2,1)S(1)}, u32[]{:S(2)}, u32[]{:S(2)}) collective-permute-start(bf16[1,320,128]{2,1,0:T(8,128)(2,1)S(1)} %add_convert_fusion.34), channel_id=1, source_target_pairs={{0,16},{1,17},{2,18},{3,19},{4,20},{5,21},{6,22},{7,23},{8,24},{9,... | collective-permute-start | bytes 245768 | tf_op jit(solution)/shard_map/ppermute | solution.py:111
  167.8 9.8 %collective-permute-start.28 = (bf16[2,208,128]{2,1,0:T(8,128)(2,1)S(1)}, bf16[2,208,128]{2,1,0:T(8,128)(2,1)S(1)}, u32[]{:S(2)}, u32[]{:S(2)}) collective-permute-start(bf16[2,208,128]{2,1,0:T(8,128)(2,1)S(1)} %get-tuple-element.117), channel_id=1, source_target_pairs={{0,8},{1,9},{2,10},{3,11},{4,12},{5,13},{6,14},{7,15},{8,0},{9,1},... | collective-permute-start | bytes 319496 | tf_op jit(solution)/shard_map/ppermute | solution.py:111
  (30 other events, 197.6 us)

commit v5 on v4

--- a/solution.py
+++ b/solution.py
@@ -214,43 +214,6 @@
                 ].astype(jnp.bfloat16)
 
         first += rows * blocks
-
-
-def attn_unpack_kernel(plan, has_tails, device_ref, *refs):
-    sources = refs[: len(plan)]
-    qkv_weight, out_weight = refs[len(plan) : len(plan) + 2]
-    tails = refs[len(plan) + 2] if has_tails else None
-    spread = refs[-1]
-    views = [(source, 0, source.shape[0], 0) for source in sources]
-    spread_blocks(plan, views, device_ref[0], spread, tails)
-    fold_matrices(
-        spread,
-        (
-            (qkv_weight, 0, D, HQ),
-            (qkv_weight, HQ, D, HD),
-            (qkv_weight, HQ + HD, D, HD),
-            (out_weight, 0, HQ, D),
-        ),
-    )
-
-
-def unpack_attn(plan, tail_rows, device, arrays, devices):
-    flat_rows = G1LEN // LANES
-    shapes = [
-        jax.ShapeDtypeStruct((D, HQ + 2 * HD), jnp.bfloat16),
-        jax.ShapeDtypeStruct((HQ, D), jnp.bfloat16),
-    ]
-    if tail_rows:
-        shapes.append(jax.ShapeDtypeStruct((devices, tail_rows, LANES), jnp.bfloat16))
-    return pl.pallas_call(
-        functools.partial(attn_unpack_kernel, plan, bool(tail_rows)),
-        out_shape=shapes,
-        in_specs=[pl.BlockSpec(memory_space=pltpu.SMEM)] + whole_specs(len(arrays)),
-        out_specs=whole_specs(len(shapes)),
-        scratch_shapes=[pltpu.VMEM((flat_rows, LANES), jnp.float32)],
-        compiler_params=pltpu.CompilerParams(vmem_limit_bytes=16 << 20),
-        cost_estimate=pl.CostEstimate(flops=0, bytes_accessed=0, transcendentals=0),
-    )(device, *arrays)
 
 
 def spread_grads(spread, products):
@@ -329,9 +292,52 @@
     return normed_in, key_raw, values, keys, heads, cos_tab, sin_tab
 
 
-def attn_forward_kernel(
-    hidden_in, qkv_weight, out_weight, tables, gains, attn_out, mid_stream, context
-):
+def join_gains(tails, gain_len, gains):
+    lane = lax.broadcasted_iota(jnp.int32, (1, LANES), 1)
+    tiles = [jnp.zeros((1, LANES), jnp.float32) for _ in range(gains.shape[1] // LANES)]
+    for owner in range(tails.shape[0]):
+        tile, shift = divmod(owner * gain_len, LANES)
+        run = jnp.where(lane < gain_len, tails[owner].astype(jnp.float32)[0:1, :], 0.0)
+        if shift:
+            run = pltpu.roll(run, shift, 1)
+        tiles[tile] += jnp.where(lane >= shift, run, 0.0)
+        if shift + gain_len > LANES:
+            tiles[tile + 1] += jnp.where(lane < shift, run, 0.0)
+    for number, tile in enumerate(tiles):
+        gains[:, number * LANES : (number + 1) * LANES] = tile
+
+
+def attn_forward_kernel(plan, gain_len, device_ref, hidden_in, tables, *refs):
+    if not gain_len:
+        given, refs = refs[0], refs[1:]
+    sources = refs[: len(plan)]
+    refs = refs[len(plan) :]
+    qkv_weight, out_weight, gains, attn_out, mid_stream = refs[:5]
+    staging, spread, tails, context, sems = refs[5:]
+    copies, views = [], []
+    for number, source in enumerate(sources):
+        count = source.shape[0]
+        held = staging.at[pl.ds(number * count, count)]
+        copies.append(pltpu.make_async_copy(source, held, sems.at[number]))
+        views.append((held, 0, count, 0))
+    for copy in copies:
+        copy.start()
+    for copy, step, view in zip(copies, plan, views):
+        copy.wait()
+        spread_blocks([step], [view], device_ref[0], spread, tails if gain_len else None)
+    if gain_len:
+        join_gains(tails, gain_len, gains)
+    else:
+        gains[...] = given[...]
+    fold_matrices(
+        spread,
+        (
+            (qkv_weight, 0, D, HQ),
+            (qkv_weight, HQ, D, HD),
+            (qkv_weight, HQ + HD, D, HD),
+            (out_weight, 0, HQ, D),
+        ),
+    )
     heads = attn_forward(hidden_in, qkv_weight, tables, gains)[4]
     for head, parts in enumerate(heads):
         context[:, head * HD : (head + 1) * HD] = parts[-1]
@@ -341,17 +347,33 @@
     mid_stream[...] = hidden_in[...].astype(jnp.float32) + rms_scale(out, gain_post)
 
 
-def forward_attn(hidden_in, qkv_weight, out_weight, tables, gains):
-    shapes = [jax.ShapeDtypeStruct((CAP, D), jnp.float32)] * 2
+def forward_attn(plan, gain_len, tail_rows, devices, device, hidden_in, tables, given, arrays):
+    shapes = [
+        jax.ShapeDtypeStruct((D, HQ + 2 * HD), jnp.bfloat16),
+        jax.ShapeDtypeStruct((HQ, D), jnp.bfloat16),
+        jax.ShapeDtypeStruct((1, 4 * D + 2 * HD), jnp.float32),
+        jax.ShapeDtypeStruct((CAP, D), jnp.float32),
+        jax.ShapeDtypeStruct((CAP, D), jnp.float32),
+    ]
+    given = [] if gain_len else [given]
+    held = (sum(array.shape[0] for array in arrays),) + arrays[0].shape[1:]
     return pl.pallas_call(
-        attn_forward_kernel,
+        functools.partial(attn_forward_kernel, plan, gain_len),
         out_shape=shapes,
-        in_specs=whole_specs(5),
-        out_specs=whole_specs(2),
-        scratch_shapes=[pltpu.VMEM((CAP, HQ), jnp.bfloat16)],
-        compiler_params=pltpu.CompilerParams(vmem_limit_bytes=12 << 20),
+        in_specs=[pl.BlockSpec(memory_space=pltpu.SMEM)]
+        + whole_specs(2 + len(given))
+        + [pl.BlockSpec(memory_space=pltpu.HBM)] * len(arrays),
+        out_specs=whole_specs(len(shapes)),
+        scratch_shapes=[
+            pltpu.VMEM(held, jnp.bfloat16),
+            pltpu.VMEM((G1LEN // LANES, LANES), jnp.float32),
+            pltpu.VMEM((devices, tail_rows, LANES) if gain_len else (1, ROWS, LANES), jnp.bfloat16),
+            pltpu.VMEM((CAP, HQ), jnp.bfloat16),
+            pltpu.SemaphoreType.DMA((len(arrays),)),
+        ],
+        compiler_params=pltpu.CompilerParams(vmem_limit_bytes=24 << 20),
         cost_estimate=pl.CostEstimate(flops=0, bytes_accessed=0, transcendentals=0),
-    )(hidden_in, qkv_weight, out_weight, tables, gains)
+    )(device, hidden_in, tables, *given, *arrays)
 
 
 def ffn_kernel(
@@ -460,7 +482,7 @@
         out_shape=shapes,
         in_specs=[pl.BlockSpec(memory_space=pltpu.SMEM)]
         + whole_specs(5)
-        + [pl.BlockSpec(memory_space=pl.ANY)] * len(arrays),
+        + [pl.BlockSpec(memory_space=pltpu.HBM)] * len(arrays),
         out_specs=whole_specs(len(shapes)),
         scratch_shapes=[
             pltpu.VMEM((flat_rows, LANES), jnp.float32),
@@ -652,14 +674,50 @@
     return blocks
 
 
-def cores_merged(home, came, parts):
-    half = home.shape[0] // 2
-
-    def added(first, low, high):
-        at = (slice(first, first + half), slice(low, high))
-        return (home[at].astype(jnp.float32) + came[at].astype(jnp.float32)).astype(jnp.bfloat16)
-
-    return [(added(0, low, high), added(half, low, high)) for low, high in parts]
+def merge_kernel(parts, *refs):
+    pairs = ((refs[0], refs[1]), (refs[2], refs[3]))
+    targets = refs[4:]
+    half = refs[0].shape[0] // 2
+    for number, target in enumerate(targets):
+        chunk, second = divmod(number, 2)
+
+        @pl.loop(0, half)
+        def _(index, target=target, chunk=chunk, first=second * half):
+            at = 0
+            for (home, came), (low, high) in zip(pairs, parts[chunk]):
+                total = home[first + index, low:high, :].astype(jnp.float32)
+                total += came[first + index, low:high, :].astype(jnp.float32)
+                target[index, at : at + high - low, :] = total.astype(jnp.bfloat16)
+                at += high - low
+
+
+def cores_merged(parts, *blocks):
+    half = blocks[0].shape[0] // 2
+    if any((high - low) % ROWS for chunk in parts for low, high in chunk):
+        pairs = (blocks[:2], blocks[2:])
+        joined = []
+        for chunk in parts:
+            sums = [
+                home[:, low:high].astype(jnp.float32) + came[:, low:high].astype(jnp.float32)
+                for (home, came), (low, high) in zip(pairs, chunk)
+            ]
+            total = jnp.concatenate(sums, axis=1).astype(jnp.bfloat16)
+            joined.append((total[:half], total[half:]))
+        return joined
+    shapes = [
+        jax.ShapeDtypeStruct((half, sum(high - low for low, high in chunk), LANES), jnp.bfloat16)
+        for chunk in parts
+        for _ in range(2)
+    ]
+    found = pl.pallas_call(
+        functools.partial(merge_kernel, parts),
+        out_shape=shapes,
+        in_specs=whole_specs(4),
+        out_specs=whole_specs(len(shapes)),
+        compiler_params=pltpu.CompilerParams(vmem_limit_bytes=20 << 20),
+        cost_estimate=pl.CostEstimate(flops=0, bytes_accessed=0, transcendentals=0),
+    )(*blocks)
+    return list(zip(found[::2], found[1::2]))
 
 
 def adam_update(weight_shard, gradient, moment_one, moment_two):
@@ -696,16 +754,23 @@
         second_pieces, orders[1:], ffn_rows, devices, here
     )
     aligned = attn_rows % ROWS == 0
-    qkv_weight, out_weight, *found = unpack_attn(
-        plan, tail_rows if aligned else 0, here, arrays, devices
-    )
-    tails = found[0] if aligned else tails
-    gains = tails.reshape(devices, -1)[:, :gain_len].astype(jnp.float32).reshape(1, -1)
     tables = slot_setup(seq_lengths, seq_owner, device)
-    attn_out, mid_stream = forward_attn(hidden_in, qkv_weight, out_weight, tables, gains)
-    ffn_orders = bit_orders(devices, ("xaby", "yxab", "ayxb"))
-    attn_orders = bit_orders(devices, ("xyab", "yxba"))[:2]
-    out_plan, block_shapes, ffn_parts = scatter_plan(ffn_rows, 0, ffn_orders, devices)
+    given = None
+    if not aligned:
+        given = tails.reshape(devices, -1)[:, :gain_len].astype(jnp.float32).reshape(1, -1)
+    qkv_weight, out_weight, gains, attn_out, mid_stream = forward_attn(
+        plan,
+        gain_len if aligned else 0,
+        tail_rows,
+        devices,
+        here,
+        hidden_in,
+        tables,
+        given,
+        arrays,
+    )
+    orders = bit_orders(devices, ("yxba", "ayxb", "xayb"))
+    out_plan, block_shapes, ffn_parts = scatter_plan(ffn_rows, 0, orders, devices)
     staged = [(0, 0, 0)]
     if len(block_shapes) == 2:
         staged = [
@@ -726,13 +791,9 @@
         gains,
         ffn_arrays,
     )
-    ffn_home, ffn_away = blocks_of(found, None, ffn_parts, ffn_orders, devices, here)
+    ffn_home, ffn_away = blocks_of(found, None, ffn_parts, orders, devices, here)
     ffn_came = across(ffn_away, 0, devices)
-    delta_attn, ffn_came = lax.optimization_barrier((delta_attn, ffn_came))
-    ffn_chunks = cores_merged(ffn_home, ffn_came, ffn_parts)
-    delta_attn, ffn_chunks = lax.optimization_barrier((delta_attn, ffn_chunks))
-    ffn_came = sent_blocks(ffn_chunks, ffn_orders, 0, devices)
-    attn_plan, block_shapes, attn_parts = scatter_plan(attn_rows, tail_rows, attn_orders, devices)
+    attn_plan, block_shapes, attn_parts = scatter_plan(attn_rows, tail_rows, orders, devices)
     grad_in, gain_grads, *found = back_attn(
         attn_plan,
         gain_len if aligned else 0,
@@ -753,29 +814,21 @@
     if not aligned:
         gain_table = gain_grads.reshape(devices, gain_len).astype(jnp.bfloat16)
         gain_table = jnp.pad(gain_table, ((0, 0), (0, pad))).reshape(devices, tail_rows, LANES)
-    attn_home, attn_away = blocks_of(found, gain_table, attn_parts, attn_orders, devices, here)
-    attn_home, attn_away, ffn_came = lax.optimization_barrier((attn_home, attn_away, ffn_came))
-    stages = len(ffn_orders[0])
-    ffn_chunks = merged_blocks(ffn_chunks, ffn_came)
-    ffn_came = sent_blocks(ffn_chunks, ffn_orders, 1, devices)
+    attn_home, attn_away = blocks_of(found, gain_table, attn_parts, orders, devices, here)
     attn_came = across(attn_away, 0, devices)
-    ffn_came[0], attn_came = lax.optimization_barrier((ffn_came[0], attn_came))
-    attn_chunks = cores_merged(attn_home, attn_came, attn_parts)
-    for stage in range(1, stages + 1):
-        attn_came = sent_blocks(attn_chunks, attn_orders, stage - 1, devices)
-        if stage < stages:
-            ffn_chunks = merged_blocks(ffn_chunks, ffn_came)
-        if stage + 1 < stages:
-            ffn_came = sent_blocks(ffn_chunks, ffn_orders, stage + 1, devices)
-            for chunk, arrived in enumerate(attn_came):
-                ffn_came[chunk], attn_came[chunk] = lax.optimization_barrier(
-                    (ffn_came[chunk], arrived)
-                )
-        attn_chunks = merged_blocks(attn_chunks, attn_came)
-    attn_shard = jnp.concatenate([rows for rows, _ in attn_chunks]).reshape(-1)
-    ffn_shard = jnp.concatenate([rows for rows, _ in ffn_chunks])
+    parts = [
+        [cut[chunk] for cut in (ffn_parts, attn_parts) if chunk < len(cut)]
+        for chunk in range(len(ffn_parts))
+    ]
+    chunks = cores_merged(parts, ffn_home, ffn_came, attn_home, attn_came)
+    for stage in range(len(orders[0])):
+        chunks = merged_blocks(chunks, sent_blocks(chunks, orders, stage, devices))
+    rows = [chunk for chunk, _ in chunks]
+    ffn_take = [high - low for low, high in ffn_parts]
+    ffn_shard = [chunk[:take].reshape(-1) for chunk, take in zip(rows, ffn_take)]
+    attn_shard = jnp.concatenate([chunk[take:].reshape(-1) for chunk, take in zip(rows, ffn_take)])
     grad_shard = jnp.concatenate(
-        [attn_shard[:attn_len], ffn_shard.reshape(-1), attn_shard[attn_len : attn_len + gain_len]]
+        [attn_shard[:attn_len], *ffn_shard, attn_shard[attn_len : attn_len + gain_len]]
     )
     params_new, moment_one_new, moment_two_new = adam_update(
         params, grad_shard, moment_one, moment_two

time: 188 us -> 171 us (0.910)
  starting transfers between devices: 58.6 us -> 36.9 us
  waiting for transfers between devices: 76.4 us -> 92.5 us
  local copies, waits for them, and re-layouts: 7.95 us -> 0.99 us
  other arithmetic: 12.4 us -> 5.65 us
  Pallas kernels: 31.3 us -> 33.6 us
    ppermute x40 -> x32, starting transfers between devices: 58.6 us -> 36.9 us  [across(): lax.ppermute(block, 'dp', [(i, i ^ 1 << bit) for i in range(devices)])]
    ppermute x40 -> x32, waiting for transfers between devices: 76.4 us -> 92.5 us  [across(): lax.ppermute(block, 'dp', [(i, i ^ 1 << bit) for i in range(devices)])]
    unnamed x29 -> x21, local copies, waits for them, and re-layouts: 6.27 us -> 0.1 us
    convert_element_type x2 -> x0, other arithmetic: 4.03 us -> none  [added(): (home[at].astype(jnp.float32) + came[at].astype(jnp.float32)).astype(jnp....]
    pallas_call x2, Pallas kernels: 3.13 us -> 6.24 us  [the longest x1 4.51 us: forward_attn(): pl.pallas_call(functools.partial(attn_forward_kernel, plan, gain_len), ou...]
    concatenate x9, other arithmetic: 2.51 us -> 0.5 us  [gather_chunk(): held = jnp.concatenate([held, across(held, bit, devices)])]
  transfers between devices with their start and end apart: 40 -> 32, of which waited for: 22 -> 19; matrix products, arithmetic and copies ran while one was open for 4% -> 2% of each run, Pallas kernels for 5% -> 6%
where the time goes in v5:
time: 171 us
  waiting for transfers between devices  92.5 us (54%)
  starting transfers between devices  36.9 us (22%)
  Pallas kernels  33.6 us (20%)
  other arithmetic  5.65 us (3%)
    ppermute x32, waiting for transfers between devices, across(): lax.ppermute(block, 'dp', [(i, i ^ 1 << bit) for i in range(devices)])  92.5 us
    ppermute x32, starting transfers between devices, across(): lax.ppermute(block, 'dp', [(i, i ^ 1 << bit) for i in range(devices)])  36.9 us
    pallas_call x1, Pallas kernels, run_ffn(): pl.pallas_call(functools.partial(ffn_kernel, plan_in, staged, plan_out),...  21.3 us
    pallas_call x1, Pallas kernels, back_attn(): pl.pallas_call(functools.partial(attn_back_kernel, plan, gain_len), out_s...  6.08 us
    pallas_call x1, Pallas kernels, forward_attn(): pl.pallas_call(functools.partial(attn_forward_kernel, plan, gain_len), ou...  4.51 us
  transfers between devices with their start and end apart: 32, of which 19 were waited for; matrix products, arithmetic and copies ran while one was open for 2% of the time, Pallas kernels for 6%

profile of v5, /device:TPU:0, one launch (start us, length us, event | category | flops | bytes accessed | tf_op | source)
XLA Modules:
  0.0 170.8 jit_solution(13599924055371071099)
XLA Ops:
  1.8 4.1 %collective-permute-start.6 = (bf16[1,480,128]{2,1,0:T(8,128)(2,1)S(1)}, bf16[1,480,128]{2,1,0:T(8,128)(2,1)S(1)}, u32[]{:S(2)}, u32[]{:S(2)}) collective-permute-start(bf16[1,480,128]{2,1,0:T(8,128)(2,1)S(1)} %get-tuple-element.66), channel_id=1, source_target_pairs={{0,16},{1,17},{2,18},{3,19},{4,20},{5,21},{6,22},{7,23},{8,24},{9,... | collective-permute-start | bytes 368648 | tf_op jit(solution)/shard_map/ppermute | solution.py:111
  5.9 6.0 %collective-permute-done.6 = bf16[1,480,128]{2,1,0:T(8,128)(2,1)S(1)} collective-permute-done((bf16[1,480,128]{2,1,0:T(8,128)(2,1)S(1)}, bf16[1,480,128]{2,1,0:T(8,128)(2,1)S(1)}, u32[]{:S(2)}, u32[]{:S(2)}) %collective-permute-start.6) | collective-permute-done | bytes 122912 | tf_op jit(solution)/shard_map/ppermute | solution.py:111
  14.2 4.0 %collective-permute-start = (bf16[1,416,128]{2,1,0:T(8,128)(2,1)S(1)}, bf16[1,416,128]{2,1,0:T(8,128)(2,1)S(1)}, u32[]{:S(2)}, u32[]{:S(2)}) collective-permute-start(bf16[1,416,128]{2,1,0:T(8,128)(2,1)S(1)} %bitcast.26), channel_id=1, source_target_pairs={{0,8},{1,9},{2,10},{3,11},{4,12},{5,13},{6,14},{7,15},{8,0},{9,1},... | collective-permute-start | bytes 319496 | tf_op jit(solution)/shard_map/ppermute | solution.py:111
  18.2 3.4 %collective-permute-done.12 = bf16[1,480,128]{2,1,0:T(8,128)(2,1)S(1)} collective-permute-done((bf16[1,480,128]{2,1,0:T(8,128)(2,1)S(1)}, bf16[1,480,128]{2,1,0:T(8,128)(2,1)S(1)}, u32[]{:S(2)}, u32[]{:S(2)}) %collective-permute-start.12) | collective-permute-done | bytes 122912 | tf_op jit(solution)/shard_map/ppermute | solution.py:111
  24.0 6.6 %collective-permute-done.13 = bf16[2,480,128]{2,1,0:T(8,128)(2,1)S(1)} collective-permute-done((bf16[2,480,128]{2,1,0:T(8,128)(2,1)S(1)}, bf16[2,480,128]{2,1,0:T(8,128)(2,1)S(1)}, u32[]{:S(2)}, u32[]{:S(2)}) %collective-permute-start.13) | collective-permute-done | bytes 245792 | tf_op jit(solution)/shard_map/ppermute | solution.py:111
  30.8 2.3 %collective-permute-done.1 = bf16[2,416,128]{2,1,0:T(8,128)(2,1)S(1)} collective-permute-done((bf16[2,416,128]{2,1,0:T(8,128)(2,1)S(1)}, bf16[2,416,128]{2,1,0:T(8,128)(2,1)S(1)}, u32[]{:S(2)}, u32[]{:S(2)}) %collective-permute-start.1) | collective-permute-done | bytes 213024 | tf_op jit(solution)/shard_map/ppermute | solution.py:111
  33.7 2.2 %collective-permute-done.8 = bf16[4,480,128]{2,1,0:T(8,128)(2,1)S(1)} collective-permute-done((bf16[4,480,128]{2,1,0:T(8,128)(2,1)S(1)}, bf16[4,480,128]{2,1,0:T(8,128)(2,1)S(1)}, u32[]{:S(2)}, u32[]{:S(2)}) %collective-permute-start.8) | collective-permute-done | bytes 491552 | tf_op jit(solution)/shard_map/ppermute | solution.py:111
  36.0 2.6 %collective-permute-start.9 = (bf16[8,480,128]{2,1,0:T(8,128)(2,1)S(1)}, bf16[8,480,128]{2,1,0:T(8,128)(2,1)}, u32[]{:S(2)}, u32[]{:S(2)}) collective-permute-start(bf16[8,480,128]{2,1,0:T(8,128)(2,1)S(1)} %pad_maximum_fusion.refs_0_), channel_id=1, source_target_pairs={{0,8},{1,9},{2,10},{3,11},{4,12},{5,13},{6,14},{7,15},{8,0},{9,1},... | collective-permute-start | bytes 2949128 | tf_op jit(solution)/shard_map/ppermute | solution.py:111
  38.6 3.6 %collective-permute-done.14 = bf16[4,480,128]{2,1,0:T(8,128)(2,1)S(1)} collective-permute-done((bf16[4,480,128]{2,1,0:T(8,128)(2,1)S(1)}, bf16[4,480,128]{2,1,0:T(8,128)(2,1)S(1)}, u32[]{:S(2)}, u32[]{:S(2)}) %collective-permute-start.14) | collective-permute-done | bytes 491552 | tf_op jit(solution)/shard_map/ppermute | solution.py:111
  43.0 2.6 %collective-permute-done.2 = bf16[4,416,128]{2,1,0:T(8,128)(2,1)S(1)} collective-permute-done((bf16[4,416,128]{2,1,0:T(8,128)(2,1)S(1)}, bf16[4,416,128]{2,1,0:T(8,128)(2,1)S(1)}, u32[]{:S(2)}, u32[]{:S(2)}) %collective-permute-start.2) | collective-permute-done | bytes 426016 | tf_op jit(solution)/shard_map/ppermute | solution.py:111
  48.3 12.4 %collective-permute-done.9.refs_1_ = bf16[8,480,128]{2,1,0:T(8,128)(2,1)} collective-permute-done((bf16[8,480,128]{2,1,0:T(8,128)(2,1)S(1)}, bf16[8,480,128]{2,1,0:T(8,128)(2,1)}, u32[]{:S(2)}, u32[]{:S(2)}) %collective-permute-start.9) | collective-permute-done | bytes 983072 | tf_op jit(solution)/shard_map/ppermute | solution.py:111
  60.7 2.4 %collective-permute-done.15.refs_5_ = bf16[8,480,128]{2,1,0:T(8,128)(2,1)} collective-permute-done((bf16[8,480,128]{2,1,0:T(8,128)(2,1)S(1)}, bf16[8,480,128]{2,1,0:T(8,128)(2,1)}, u32[]{:S(2)}, u32[]{:S(2)}) %collective-permute-start.15) | collective-permute-done | bytes 983072 | tf_op jit(solution)/shard_map/ppermute | solution.py:111
  63.2 4.0 %collective-permute-done.3.refs_1_ = bf16[8,416,128]{2,1,0:T(8,128)(2,1)} collective-permute-done((bf16[8,416,128]{2,1,0:T(8,128)(2,1)S(1)}, bf16[8,416,128]{2,1,0:T(8,128)(2,1)}, u32[]{:S(2)}, u32[]{:S(2)}) %collective-permute-start.3) | collective-permute-done | bytes 852000 | tf_op jit(solution)/shard_map/ppermute | solution.py:111
  69.8 4.5 %shard_map.118 = (bf16[640,1536]{1,0:T(8,128)(2,1)S(1)}, bf16[1024,640]{1,0:T(8,128)(2,1)S(1)}, f32[1,3072]{1,0:T(1,128)S(1)}, f32[128,640]{1,0:T(8,128)S(1)}, f32[128,640]{1,0:T(8,128)S(1)}) custom-call(s32[1]{0:T(128)} %bitcast.device_ref, bf16[128,640]{1,0:T(8,128)(2,1)S(1)} %copy-done.1, f32[128,512]{1,0:T(8,128)S(1)} %pad_maximum_fusion.6.tables, ...), custom_call_target="tpu_custom_call" | custom-call | tf_op jit(solution)/shard_map/pallas_call | solution.py:360
  74.3 21.3 %shard_map.119 = (bf16[128,640]{1,0:T(8,128)(2,1)}, f32[128,640]{1,0:T(8,128)S(1)}, bf16[128,640]{1,0:T(8,128)(2,1)S(1)}, f32[3,640]{1,0:T(4,128)S(1)}, bf16[16,...) custom-call(s32[1]{0:T(128)} %bitcast.device_ref, f32[128,640]{1,0:T(8,128)S(1)} %get-tuple-element.26.mid_ref, ...), custom_call_target="tpu_custom_call" | custom-call | tf_op jit(solution)/shard_map/pallas_call | solution.py:480
  95.8 6.1 %shard_map.120 = (f32[128,640]{1,0:T(8,128)}, f32[1,3072]{1,0:T(1,128)}, bf16[16,416,128]{2,1,0:T(8,128)(2,1)S(1)}, bf16[16,416,128]{2,1,0:T(8,128)(2,1)S(1)}) custom-call(s32[1]{0:T(128)} %bitcast.device_ref, bf16[128,640]{1,0:T(8,128)(2,1)S(1)} %get-tuple-element.30.delta_attn, f32[128,640]{1,0:T(8,128)S(1)} %get-tuple-element.31.delta_mid, ...), custom_call_target="tpu_custom_call" | custom-call | tf_op jit(solution)/shard_map/pallas_call | solution.py:601
  102.3 3.2 %collective-permute-done.19.refs_3_ = bf16[16,416,128]{2,1,0:T(8,128)(2,1)S(1)} collective-permute-done((bf16[16,416,128]{2,1,0:T(8,128)(2,1)S(1)}, bf16[16,416,128]{2,1,0:T(8,128)(2,1)S(1)}, u32[]{:S(2)}, u32[]{:S(2)}) %collective-permute-start.19) | collective-permute-done | bytes 1703968 | tf_op jit(solution)/shard_map/ppermute | solution.py:111
  110.3 19.7 %collective-permute-done.28 = bf16[8,448,128]{2,1,0:T(8,128)(2,1)S(1)} collective-permute-done((bf16[8,448,128]{2,1,0:T(8,128)(2,1)S(1)}, bf16[8,448,128]{2,1,0:T(8,128)(2,1)S(1)}, u32[]{:S(2)}, u32[]{:S(2)}) %collective-permute-start.28) | collective-permute-done | bytes 917536 | tf_op jit(solution)/shard_map/ppermute | solution.py:111
  134.6 7.7 %collective-permute-done.29 = bf16[4,448,128]{2,1,0:T(8,128)(2,1)S(1)} collective-permute-done((bf16[4,448,128]{2,1,0:T(8,128)(2,1)S(1)}, bf16[4,448,128]{2,1,0:T(8,128)(2,1)S(1)}, u32[]{:S(2)}, u32[]{:S(2)}) %collective-permute-start.29) | collective-permute-done | bytes 458784 | tf_op jit(solution)/shard_map/ppermute | solution.py:111
  144.1 3.1 %collective-permute-start.22 = (bf16[2,464,128]{2,1,0:T(8,128)(2,1)S(1)}, bf16[2,464,128]{2,1,0:T(8,128)(2,1)S(1)}, u32[]{:S(2)}, u32[]{:S(2)}) collective-permute-start(bf16[2,464,128]{2,1,0:T(8,128)(2,1)S(1)} %get-tuple-element.60), channel_id=1, source_target_pairs={{0,16},{1,17},{2,18},{3,19},{4,20},{5,21},{6,22},{7,23},{8,24},{9,... | collective-permute-start | bytes 712712 | tf_op jit(solution)/shard_map/ppermute | solution.py:111
  149.7 2.9 %collective-permute-start.31 = (bf16[1,448,128]{2,1,0:T(8,128)(2,1)S(1)}, bf16[1,448,128]{2,1,0:T(8,128)(2,1)S(1)}, u32[]{:S(2)}, u32[]{:S(2)}) collective-permute-start(bf16[1,448,128]{2,1,0:T(8,128)(2,1)S(1)} %add_convert_fusion.16), channel_id=1, source_target_pairs={{0,16},{1,17},{2,18},{3,19},{4,20},{5,21},{6,22},{7,23},{8,24},{9,... | collective-permute-start | bytes 344072 | tf_op jit(solution)/shard_map/ppermute | solution.py:111
  152.6 7.4 %collective-permute-done.22 = bf16[2,464,128]{2,1,0:T(8,128)(2,1)S(1)} collective-permute-done((bf16[2,464,128]{2,1,0:T(8,128)(2,1)S(1)}, bf16[2,464,128]{2,1,0:T(8,128)(2,1)S(1)}, u32[]{:S(2)}, u32[]{:S(2)}) %collective-permute-start.22) | collective-permute-done | bytes 237600 | tf_op jit(solution)/shard_map/ppermute | solution.py:111
  160.2 3.3 %collective-permute-start.27 = (bf16[1,464,128]{2,1,0:T(8,128)(2,1)S(1)}, bf16[1,464,128]{2,1,0:T(8,128)(2,1)S(1)}, u32[]{:S(2)}, u32[]{:S(2)}) collective-permute-start(bf16[1,464,128]{2,1,0:T(8,128)(2,1)S(1)} %add_convert_fusion.12), channel_id=1, source_target_pairs={{0,16},{1,17},{2,18},{3,19},{4,20},{5,21},{6,22},{7,23},{8,24},{9,... | collective-permute-start | bytes 356360 | tf_op jit(solution)/shard_map/ppermute | solution.py:111
  163.6 3.6 %collective-permute-done.23 = bf16[1,464,128]{2,1,0:T(8,128)(2,1)S(1)} collective-permute-done((bf16[1,464,128]{2,1,0:T(8,128)(2,1)S(1)}, bf16[1,464,128]{2,1,0:T(8,128)(2,1)S(1)}, u32[]{:S(2)}, u32[]{:S(2)}) %collective-permute-start.23) | collective-permute-done | bytes 118816 | tf_op jit(solution)/shard_map/ppermute | solution.py:111
  (112 shorter events, 31.0 us)
Async XLA Ops:
  1.8 10.1 %collective-permute-start.6 = (bf16[1,480,128]{2,1,0:T(8,128)(2,1)S(1)}, bf16[1,480,128]{2,1,0:T(8,128)(2,1)S(1)}, u32[]{:S(2)}, u32[]{:S(2)}) collective-permute-start(bf16[1,480,128]{2,1,0:T(8,128)(2,1)S(1)} %get-tuple-element.66), channel_id=1, source_target_pairs={{0,16},{1,17},{2,18},{3,19},{4,20},{5,21},{6,22},{7,23},{8,24},{9,... | collective-permute-start | bytes 368648 | tf_op jit(solution)/shard_map/ppermute | solution.py:111
  11.9 11.4 %collective-permute-start.7 = (bf16[2,480,128]{2,1,0:T(8,128)(2,1)S(1)}, bf16[2,480,128]{2,1,0:T(8,128)(2,1)S(1)}, u32[]{:S(2)}, u32[]{:S(2)}) collective-permute-start(bf16[2,480,128]{2,1,0:T(8,128)(2,1)S(1)} %pad_maximum_fusion.7), channel_id=1, source_target_pairs={{0,2},{1,3},{2,0},{3,1},{4,6},{5,7},{6,4},{7,5},{8,10},{9,11},{10,... | collective-permute-start | bytes 737288 | tf_op jit(solution)/shard_map/ppermute | solution.py:111
  14.2 9.6 %collective-permute-start = (bf16[1,416,128]{2,1,0:T(8,128)(2,1)S(1)}, bf16[1,416,128]{2,1,0:T(8,128)(2,1)S(1)}, u32[]{:S(2)}, u32[]{:S(2)}) collective-permute-start(bf16[1,416,128]{2,1,0:T(8,128)(2,1)S(1)} %bitcast.26), channel_id=1, source_target_pairs={{0,8},{1,9},{2,10},{3,11},{4,12},{5,13},{6,14},{7,15},{8,0},{9,1},... | collective-permute-start | bytes 319496 | tf_op jit(solution)/shard_map/ppermute | solution.py:111
  23.3 12.6 %collective-permute-start.8 = (bf16[4,480,128]{2,1,0:T(8,128)(2,1)S(1)}, bf16[4,480,128]{2,1,0:T(8,128)(2,1)S(1)}, u32[]{:S(2)}, u32[]{:S(2)}) collective-permute-start(bf16[4,480,128]{2,1,0:T(8,128)(2,1)S(1)} %pad_maximum_fusion.3), channel_id=1, source_target_pairs={{0,4},{1,5},{2,6},{3,7},{4,0},{5,1},{6,2},{7,3},{8,12},{9,13},{10,... | collective-permute-start | bytes 1474568 | tf_op jit(solution)/shard_map/ppermute | solution.py:111
  23.9 9.2 %collective-permute-start.1 = (bf16[2,416,128]{2,1,0:T(8,128)(2,1)S(1)}, bf16[2,416,128]{2,1,0:T(8,128)(2,1)S(1)}, u32[]{:S(2)}, u32[]{:S(2)}) collective-permute-start(bf16[2,416,128]{2,1,0:T(8,128)(2,1)S(1)} %pad_maximum_fusion.9), channel_id=1, source_target_pairs={{0,16},{1,17},{2,18},{3,19},{4,20},{5,21},{6,22},{7,23},{8,24},{9,... | collective-permute-start | bytes 638984 | tf_op jit(solution)/shard_map/ppermute | solution.py:111
  30.7 11.6 %collective-permute-start.14 = (bf16[4,480,128]{2,1,0:T(8,128)(2,1)S(1)}, bf16[4,480,128]{2,1,0:T(8,128)(2,1)S(1)}, u32[]{:S(2)}, u32[]{:S(2)}) collective-permute-start(bf16[4,480,128]{2,1,0:T(8,128)(2,1)S(1)} %pad_maximum_fusion.4), channel_id=1, source_target_pairs={{0,8},{1,9},{2,10},{3,11},{4,12},{5,13},{6,14},{7,15},{8,0},{9,1},... | collective-permute-start | bytes 1474568 | tf_op jit(solution)/shard_map/ppermute | solution.py:111
  33.1 12.4 %collective-permute-start.2 = (bf16[4,416,128]{2,1,0:T(8,128)(2,1)S(1)}, bf16[4,416,128]{2,1,0:T(8,128)(2,1)S(1)}, u32[]{:S(2)}, u32[]{:S(2)}) collective-permute-start(bf16[4,416,128]{2,1,0:T(8,128)(2,1)S(1)} %pad_maximum_fusion.5), channel_id=1, source_target_pairs={{0,2},{1,3},{2,0},{3,1},{4,6},{5,7},{6,4},{7,5},{8,10},{9,11},{10,... | collective-permute-start | bytes 1277960 | tf_op jit(solution)/shard_map/ppermute | solution.py:111
  36.0 24.7 %collective-permute-start.9 = (bf16[8,480,128]{2,1,0:T(8,128)(2,1)S(1)}, bf16[8,480,128]{2,1,0:T(8,128)(2,1)}, u32[]{:S(2)}, u32[]{:S(2)}) collective-permute-start(bf16[8,480,128]{2,1,0:T(8,128)(2,1)S(1)} %pad_maximum_fusion.refs_0_), channel_id=1, source_target_pairs={{0,8},{1,9},{2,10},{3,11},{4,12},{5,13},{6,14},{7,15},{8,0},{9,1},... | collective-permute-start | bytes 2949128 | tf_op jit(solution)/shard_map/ppermute | solution.py:111
  42.4 20.8 %collective-permute-start.15 = (bf16[8,480,128]{2,1,0:T(8,128)(2,1)S(1)}, bf16[8,480,128]{2,1,0:T(8,128)(2,1)}, u32[]{:S(2)}, u32[]{:S(2)}) collective-permute-start(bf16[8,480,128]{2,1,0:T(8,128)(2,1)S(1)} %pad_maximum_fusion.1.refs_4_), channel_id=1, source_target_pairs={{0,2},{1,3},{2,0},{3,1},{4,6},{5,7},{6,4},{7,5},{8,10},{9,11},{10,... | collective-permute-start | bytes 2949128 | tf_op jit(solution)/shard_map/ppermute | solution.py:111
  45.7 21.5 %collective-permute-start.3 = (bf16[8,416,128]{2,1,0:T(8,128)(2,1)S(1)}, bf16[8,416,128]{2,1,0:T(8,128)(2,1)}, u32[]{:S(2)}, u32[]{:S(2)}) collective-permute-start(bf16[8,416,128]{2,1,0:T(8,128)(2,1)S(1)} %pad_maximum_fusion.2.refs_0_), channel_id=1, source_target_pairs={{0,4},{1,5},{2,6},{3,7},{4,0},{5,1},{6,2},{7,3},{8,12},{9,13},{10,... | collective-permute-start | bytes 2555912 | tf_op jit(solution)/shard_map/ppermute | solution.py:111
  47.6 26.7 %collective-permute-start.10 = (bf16[8,480,128]{2,1,0:T(8,128)(2,1)S(1)}, bf16[8,480,128]{2,1,0:T(8,128)(2,1)S(1)}, u32[]{:S(2)}, u32[]{:S(2)}) collective-permute-start(bf16[8,480,128]{2,1,0:T(8,128)(2,1)S(1)} %pad_maximum_fusion.refs_0_), channel_id=1, source_target_pairs={{0,1},{1,0},{2,3},{3,2},{4,5},{5,4},{6,7},{7,6},{8,9},{9,8},{10,11... | collective-permute-start | bytes 2949128 | tf_op jit(solution)/shard_map/ppermute | solution.py:111
  48.2 26.1 %collective-permute-start.16 = (bf16[8,480,128]{2,1,0:T(8,128)(2,1)S(1)}, bf16[8,480,128]{2,1,0:T(8,128)(2,1)S(1)}, u32[]{:S(2)}, u32[]{:S(2)}) collective-permute-start(bf16[8,480,128]{2,1,0:T(8,128)(2,1)S(1)} %pad_maximum_fusion.1.refs_4_), channel_id=1, source_target_pairs={{0,1},{1,0},{2,3},{3,2},{4,5},{5,4},{6,7},{7,6},{8,9},{9,8},{10,11... | collective-permute-start | bytes 2949128 | tf_op jit(solution)/shard_map/ppermute | solution.py:111
  60.7 13.6 %collective-permute-start.11 = (bf16[8,480,128]{2,1,0:T(8,128)(2,1)}, bf16[8,480,128]{2,1,0:T(8,128)(2,1)S(1)}, u32[]{:S(2)}, u32[]{:S(2)}) collective-permute-start(bf16[8,480,128]{2,1,0:T(8,128)(2,1)} %collective-permute-done.9.refs_1_), channel_id=1, source_target_pairs={{0,1},{1,0},{2,3},{3,2},{4,5},{5,4},{6,7},{7,6},{8,9},{9,8},{10,11... | collective-permute-start | bytes 2949128 | tf_op jit(solution)/shard_map/ppermute | solution.py:111
  63.2 11.1 %collective-permute-start.17 = (bf16[8,480,128]{2,1,0:T(8,128)(2,1)}, bf16[8,480,128]{2,1,0:T(8,128)(2,1)S(1)}, u32[]{:S(2)}, u32[]{:S(2)}) collective-permute-start(bf16[8,480,128]{2,1,0:T(8,128)(2,1)} %collective-permute-done.15.refs_5_), channel_id=1, source_target_pairs={{0,1},{1,0},{2,3},{3,2},{4,5},{5,4},{6,7},{7,6},{8,9},{9,8},{10,11... | collective-permute-start | bytes 2949128 | tf_op jit(solution)/shard_map/ppermute | solution.py:111
  95.6 9.9 %collective-permute-start.18 = (bf16[16,960,128]{2,1,0:T(8,128)(2,1)}, bf16[16,960,128]{2,1,0:T(8,128)(2,1)S(1)}, u32[]{:S(2)}, u32[]{:S(2)}) collective-permute-start(bf16[16,960,128]{2,1,0:T(8,128)(2,1)} %get-tuple-element.37), channel_id=1, source_target_pairs={{0,1},{1,0},{2,3},{3,2},{4,5},{5,4},{6,7},{7,6},{8,9},{9,8},{10,11... | collective-permute-start | bytes 11796488 | tf_op jit(solution)/shard_map/ppermute | solution.py:111
  107.3 22.7 %collective-permute-start.28 = (bf16[8,448,128]{2,1,0:T(8,128)(2,1)S(1)}, bf16[8,448,128]{2,1,0:T(8,128)(2,1)S(1)}, u32[]{:S(2)}, u32[]{:S(2)}) collective-permute-start(bf16[8,448,128]{2,1,0:T(8,128)(2,1)S(1)} %get-tuple-element.45), channel_id=1, source_target_pairs={{0,2},{1,3},{2,0},{3,1},{4,6},{5,7},{6,4},{7,5},{8,10},{9,11},{10,... | collective-permute-start | bytes 2752520 | tf_op jit(solution)/shard_map/ppermute | solution.py:111
  107.7 23.5 %collective-permute-start.20 = (bf16[8,464,128]{2,1,0:T(8,128)(2,1)S(1)}, bf16[8,464,128]{2,1,0:T(8,128)(2,1)S(1)}, u32[]{:S(2)}, u32[]{:S(2)}) collective-permute-start(bf16[8,464,128]{2,1,0:T(8,128)(2,1)S(1)} %get-tuple-element.41), channel_id=1, source_target_pairs={{0,4},{1,5},{2,6},{3,7},{4,0},{5,1},{6,2},{7,3},{8,12},{9,13},{10,... | collective-permute-start | bytes 2850824 | tf_op jit(solution)/shard_map/ppermute | solution.py:111
  109.4 23.3 %collective-permute-start.24 = (bf16[8,464,128]{2,1,0:T(8,128)(2,1)S(1)}, bf16[8,464,128]{2,1,0:T(8,128)(2,1)S(1)}, u32[]{:S(2)}, u32[]{:S(2)}) collective-permute-start(bf16[8,464,128]{2,1,0:T(8,128)(2,1)S(1)} %get-tuple-element.43), channel_id=1, source_target_pairs={{0,8},{1,9},{2,10},{3,11},{4,12},{5,13},{6,14},{7,15},{8,0},{9,1},... | collective-permute-start | bytes 2850824 | tf_op jit(solution)/shard_map/ppermute | solution.py:111
  130.2 12.0 %collective-permute-start.29 = (bf16[4,448,128]{2,1,0:T(8,128)(2,1)S(1)}, bf16[4,448,128]{2,1,0:T(8,128)(2,1)S(1)}, u32[]{:S(2)}, u32[]{:S(2)}) collective-permute-start(bf16[4,448,128]{2,1,0:T(8,128)(2,1)S(1)} %get-tuple-element.58), channel_id=1, source_target_pairs={{0,8},{1,9},{2,10},{3,11},{4,12},{5,13},{6,14},{7,15},{8,0},{9,1},... | collective-permute-start | bytes 1376264 | tf_op jit(solution)/shard_map/ppermute | solution.py:111
  131.5 12.5 %collective-permute-start.21 = (bf16[4,464,128]{2,1,0:T(8,128)(2,1)S(1)}, bf16[4,464,128]{2,1,0:T(8,128)(2,1)S(1)}, u32[]{:S(2)}, u32[]{:S(2)}) collective-permute-start(bf16[4,464,128]{2,1,0:T(8,128)(2,1)S(1)} %get-tuple-element.54), channel_id=1, source_target_pairs={{0,2},{1,3},{2,0},{3,1},{4,6},{5,7},{6,4},{7,5},{8,10},{9,11},{10,... | collective-permute-start | bytes 1425416 | tf_op jit(solution)/shard_map/ppermute | solution.py:111
  133.0 14.2 %collective-permute-start.25 = (bf16[4,464,128]{2,1,0:T(8,128)(2,1)S(1)}, bf16[4,464,128]{2,1,0:T(8,128)(2,1)S(1)}, u32[]{:S(2)}, u32[]{:S(2)}) collective-permute-start(bf16[4,464,128]{2,1,0:T(8,128)(2,1)S(1)} %get-tuple-element.56), channel_id=1, source_target_pairs={{0,4},{1,5},{2,6},{3,7},{4,0},{5,1},{6,2},{7,3},{8,12},{9,13},{10,... | collective-permute-start | bytes 1425416 | tf_op jit(solution)/shard_map/ppermute | solution.py:111
  144.1 15.9 %collective-permute-start.22 = (bf16[2,464,128]{2,1,0:T(8,128)(2,1)S(1)}, bf16[2,464,128]{2,1,0:T(8,128)(2,1)S(1)}, u32[]{:S(2)}, u32[]{:S(2)}) collective-permute-start(bf16[2,464,128]{2,1,0:T(8,128)(2,1)S(1)} %get-tuple-element.60), channel_id=1, source_target_pairs={{0,16},{1,17},{2,18},{3,19},{4,20},{5,21},{6,22},{7,23},{8,24},{9,... | collective-permute-start | bytes 712712 | tf_op jit(solution)/shard_map/ppermute | solution.py:111
  147.4 12.8 %collective-permute-start.26 = (bf16[2,464,128]{2,1,0:T(8,128)(2,1)S(1)}, bf16[2,464,128]{2,1,0:T(8,128)(2,1)S(1)}, u32[]{:S(2)}, u32[]{:S(2)}) collective-permute-start(bf16[2,464,128]{2,1,0:T(8,128)(2,1)S(1)} %get-tuple-element.62), channel_id=1, source_target_pairs={{0,2},{1,3},{2,0},{3,1},{4,6},{5,7},{6,4},{7,5},{8,10},{9,11},{10,... | collective-permute-start | bytes 712712 | tf_op jit(solution)/shard_map/ppermute | solution.py:111
  149.7 13.7 %collective-permute-start.31 = (bf16[1,448,128]{2,1,0:T(8,128)(2,1)S(1)}, bf16[1,448,128]{2,1,0:T(8,128)(2,1)S(1)}, u32[]{:S(2)}, u32[]{:S(2)}) collective-permute-start(bf16[1,448,128]{2,1,0:T(8,128)(2,1)S(1)} %add_convert_fusion.16), channel_id=1, source_target_pairs={{0,16},{1,17},{2,18},{3,19},{4,20},{5,21},{6,22},{7,23},{8,24},{9,... | collective-permute-start | bytes 344072 | tf_op jit(solution)/shard_map/ppermute | solution.py:111
  (17 other events, 149.7 us)
